TPU v7x, 32 devices: a whole 2x2x4 slice. The times are simulated.
32 devices in a mesh: walker: 8 (over z, x), gx: 2 (over y), gy: 2 (over core).
Axes of the slice: x: 2, y: 2, z: 4, core: 2. Of those that a mesh axis runs over, the one named last changes fastest.
Arguments:
- positions: float32 [8, 8, 8, 3, 128], P('walker', 'gx', 'gy')
- velocities: float32 [8, 8, 8, 3, 128], P('walker', 'gx', 'gy'), may hold values from -6 to 6
- lambda_theta: float32 [8, 4, 8], P('walker'), may hold values from -3 to 3
- theta_velocity: float32 [8, 4, 8], P('walker'), may hold values from -4 to 4
- source_slot: int32 [8], replicated, may hold values from 0 to 7
- atom_noise: float32 [8, 4, 8, 8, 3, 128], P('walker', None, 'gx', 'gy'), may hold values from -6 to 6
- theta_noise: float32 [8, 4, 4, 8], P('walker'), may hold values from -6 to 6
- charges: float32 [8, 8, 128], P('gx', 'gy'), may hold values from -3 to 3
- strengths: float32 [8, 8, 128], P('gx', 'gy'), may hold values from 0.3 to 1.2
- inverse_mass: float32 [8, 8, 128], P('gx', 'gy'), may hold values from 0.1 to 1
- atom_site: int32 [8, 8, 128], P('gx', 'gy'), may hold values from 0 to 4
- atom_sub: int32 [8, 8, 128], P('gx', 'gy'), may hold values from 0 to 7
- partners: int32 [8, 8, 9], P('gx', 'gy'), may hold values from -1 to 35, as said below
Outputs:
- displacement: float32 [8, 8, 8, 3, 128], P('walker', 'gx', 'gy')
- new_velocities: float32 [8, 8, 8, 3, 128], P('walker', 'gx', 'gy')
- new_theta: float32 [8, 4, 8], P('walker')
- new_theta_velocity: float32 [8, 4, 8], P('walker')
Inputs may be any that keep to these rules, and one draw needn't show every extreme that they name: `atom_site`: 4 marks an environment atom. `partners`: entry values are indices (i mod 4 + 1 + di) * 6 + (j mod 4) + 1 + dj of tiles of the 3 x 3 neighbourhood of tile (i, j), with -1 <= di, dj <= 1, in increasing order of (di, dj), followed by -1 padding; the tile itself is always listed; tile A lists tile B exactly when B lists A; some tile lists all 9.
All inputs are finite; a program needn't handle non-finite values.
Results may differ from a plain program's by a relative error of at most 0.0003.
Values sent between devices are 32-bit elements; how exact they have to be, the bound alone decides.
No kernel may reach another device: no remote copies, remote signals or barrier semaphores. Data moves between devices by JAX's collectives and lax.ppermute only.
A program may use at most 64 MiB of HBM per device.

v0:
```python
import functools
import math

import jax
import jax.numpy as jnp
from jax import lax
from jax.experimental import pallas as pl
from jax.experimental.pallas import tpu as pltpu
from jax.sharding import PartitionSpec as P

NSITE = 4
NSUB = 8
STEPS = 4

step_size = 0.02
friction_rate = 1.0
theta_friction = 20.0
soft_alpha = 0.5
soft_beta = 0.5
theta_share = 1.0 / 1024.0

MIDDLE_Z = 1.0
REACH = 1.49
FAR = 2.0**126

X, Y, Z, LAM, CHG, STR, GRP, SIT = range(8)


def wrap_image(offset, length):
    shift = jnp.where(offset > 0.5 * length, length, 0.0)
    shift = jnp.where(offset < -0.5 * length, -length, shift)
    return offset - shift


def neighbour_offsets(count_x, count_y):
    found = []
    for di in (-1, 0, 1):
        for dj in (-1, 0, 1):
            key = (di % count_x, dj % count_y)
            if key != (0, 0) and key not in found:
                found.append(key)
    return found


def shifted(value, offset, count_x, count_y):
    pairs = []
    for i in range(count_x):
        for j in range(count_y):
            source = ((i + offset[0]) % count_x) * count_y + (j + offset[1]) % count_y
            pairs.append((source, i * count_y + j))
    return lax.ppermute(value, ("gx", "gy"), pairs)


def pool_sources(rows_x, rows_y, count_x, count_y, offsets):
    sources = []
    for pi in range(rows_x + 2):
        for pj in range(rows_y + 2):
            di = -1 if pi == 0 else (1 if pi == rows_x + 1 else 0)
            dj = -1 if pj == 0 else (1 if pj == rows_y + 1 else 0)
            key = (di % count_x, dj % count_y)
            block = 0 if key == (0, 0) else 1 + offsets.index(key)
            tile = ((pi - 1) % rows_x) * rows_y + (pj - 1) % rows_y
            sources.append((block, tile))
    return sources


def softmax_angles(angles):
    weights = jnp.exp(angles)
    return weights / jnp.sum(weights, axis=1, keepdims=True)


def angle_step(angles, speeds, packed, noise, angle_mass):
    lanes = packed.shape[1]
    share = lanes // NSITE
    lane_site = lax.broadcasted_iota(jnp.int32, packed.shape, 1) // share
    lambdas = softmax_angles(angles)
    totals = jnp.stack(
        [
            jnp.broadcast_to(
                jnp.sum(jnp.where(lane_site == site, packed, 0.0), axis=1, keepdims=True),
                packed.shape,
            )
            for site in range(NSITE)
        ]
    )
    angle_damping = math.exp(-theta_friction * step_size)
    force = -lambdas * (totals - jnp.sum(lambdas * totals, axis=1, keepdims=True))
    speeds = (
        angle_damping * speeds
        + step_size * force / angle_mass
        + math.sqrt((1.0 - angle_damping**2) / angle_mass) * noise
    )
    return angles + step_size * speeds, speeds


def step_kernel(cfg, moment, *refs):
    nb = cfg["blocks"]
    tiles, pool = cfg["tiles"], cfg["pool"]
    lanes = cfg["lanes"]
    count_ref, part_ref, off_ref = refs[:3]
    refs = refs[1:]
    coord_refs = refs[2 : 2 + nb]
    stat_refs = refs[2 + nb : 2 + 2 * nb]
    tot_ref, vel_ref, ang_ref, noise_ref, anoise_ref, inv_ref = refs[2 + 2 * nb : 8 + 2 * nb]
    pay_ref, velo_ref, ango_ref = refs[8 + 2 * nb : 11 + 2 * nb]
    pool_ref, col_ref, fcol_ref, sum_ref, feat_ref, wide_ref, rhs_ref, sel_ref = refs[11 + 2 * nb :]

    angles, aspeeds = ang_ref[0], ang_ref[1]
    if moment > 0:
        if cfg["covered"]:
            packed = coord_refs[0][0:NSUB, 3, :]
            for ref in coord_refs[1:]:
                packed = packed + ref[0:NSUB, 3, :]
        else:
            packed = tot_ref[...]
        angles, aspeeds = angle_step(
            angles, aspeeds, packed, anoise_ref[moment - 1], cfg["angle_mass"]
        )
    ango_ref[0] = angles
    ango_ref[1] = aspeeds
    lambdas = softmax_angles(angles)

    sub_iota = lax.broadcasted_iota(jnp.int32, (NSUB, lanes), 0).astype(jnp.float32)
    worst = jnp.zeros((3, lanes), jnp.float32)
    row3 = lax.broadcasted_iota(jnp.int32, (3, lanes), 0)
    for index, (block, tile) in enumerate(cfg["sources"]):
        stat = stat_refs[block][tile]
        cell = jnp.where(row3 == 0, off_ref[2, index], off_ref[3, index])
        cell = jnp.where(row3 == 2, -MIDDLE_Z, cell)
        worst = jnp.maximum(worst, jnp.abs(coord_refs[block][tile, 0:3, :] + cell))
        pool_ref[index, 0:3, :] = coord_refs[block][tile, 0:3, :]
        pool_ref[index, 4:8, :] = stat
        group = stat[2:3, :]
        lam = jnp.zeros((NSUB, lanes), jnp.float32)
        for site in range(NSITE):
            lam = lam + jnp.where(group == sub_iota + float(site * NSUB), lambdas[site], 0.0)
        lam = jnp.sum(lam, axis=0, keepdims=True)
        pool_ref[index, 3:4, :] = jnp.where(group >= 0.0, lam, 1.0)

    stray = jnp.max(worst * jnp.where(row3 == 2, 0.5, 1.0))
    sum_ref[...] = jnp.zeros_like(sum_ref)
    fcol_ref[...] = jnp.zeros_like(fcol_ref)
    ins = (vel_ref, noise_ref, inv_ref)
    outs = (pay_ref, velo_ref, sum_ref)
    near = cfg["roomy"] & (stray < REACH)

    @pl.when(near)
    def _():
        near_forces(
            cfg, lambdas, count_ref, part_ref, off_ref, pool_ref, feat_ref, wide_ref, rhs_ref,
            sel_ref, ins, outs, sub_iota,
        )

    @pl.when(jnp.logical_not(near))
    def _():
        any_forces(cfg, count_ref, part_ref, pool_ref, col_ref, fcol_ref, ins, outs, sub_iota)

    pay_sums(cfg, pay_ref, sum_ref)


def split3(value):
    high = value.astype(jnp.bfloat16).astype(jnp.float32)
    rest = value - high
    middle = rest.astype(jnp.bfloat16).astype(jnp.float32)
    return high, middle, rest - middle


def by_group(lambdas_of_site, group, sub_iota):
    return [
        jnp.where(group == sub_iota + float(site * NSUB), lambdas_of_site[site], 0.0)
        for site in range(NSITE)
    ]


def near_forces(
    cfg, lambdas, count_ref, part_ref, off_ref, pool_ref, feat_ref, wide_ref, rhs_ref,
    sel_ref, ins, outs, sub_iota,
):
    lanes = cfg["lanes"]
    depth = cfg["depth"]
    rows = lax.broadcasted_iota(jnp.int32, (8, lanes), 0)
    ones = jnp.ones((NSUB, lanes), jnp.float32)
    nothing = jnp.zeros((8, lanes), jnp.float32)
    pad = [nothing] * ((depth - 6 * 8 - 2 * NSITE * NSUB) // 8)

    pick_rows = lax.broadcasted_iota(jnp.int32, (depth, lanes), 0)
    for column, row in enumerate((0, 1, 2, 7)):
        hit = (pick_rows == row) | (pick_rows == 16 + row) | (pick_rows == 40 + row)
        sel_ref[:, column * lanes : (column + 1) * lanes] = jnp.where(hit, 1.0, 0.0).astype(
            jnp.bfloat16
        )

    def centred(index):
        block = pool_ref[index]
        shift = jnp.where(rows == 0, off_ref[0, index], 0.0)
        shift = jnp.where(rows == 1, off_ref[1, index], shift)
        shift = jnp.where(rows == 2, -MIDDLE_Z, shift)
        moved = block + shift
        square = jnp.where(rows < 3, moved * moved, 0.0)
        return block, moved, jnp.sum(square, axis=0, keepdims=True)

    def one_pool(index, carry):
        block, moved, norm = centred(index)
        table = jnp.where(rows == 5, norm, moved)
        table = jnp.where(rows == 6, 1.0, table)
        table = jnp.where(rows == 7, block[STR : STR + 1, :], table)
        high, middle, low = split3(table)
        member = by_group([ones] * NSITE, block[GRP : GRP + 1, :], sub_iota)
        features = jnp.concatenate(
            [high, high, middle, middle, high, low] + member + member + pad, axis=0
        )
        features = features.T.astype(jnp.bfloat16)
        feat_ref[index] = features
        wide_ref[index] = jnp.dot(features, sel_ref[...], preferred_element_type=jnp.float32)
        return carry

    lax.fori_loop(0, cfg["pool"], one_pool, 0)

    spread = [lam - lam * lam for lam in lambdas]
    half = [0.5 - lam for lam in lambdas]

    def one_tile(tile, carry):
        own = (tile // cfg["rows_y"] + 1) * (cfg["rows_y"] + 2) + tile % cfg["rows_y"] + 1
        block, moved, norm = centred(own)
        group, site_row = block[GRP : GRP + 1, :], block[SIT : SIT + 1, :]
        lam, charge, strength = (block[r : r + 1, :] for r in (LAM, CHG, STR))
        ratio = charge / strength

        gap = jnp.where(rows < 3, -2.0 * moved, 0.0)
        gap = jnp.where(rows == 3, -0.5 * lam, gap)
        gap = jnp.where(rows == 5, 1.0, gap)
        gap = jnp.where(rows == 6, norm + 1.5, gap)
        pair = by_group(spread, group, sub_iota)
        far = [
            jnp.where(
                (site_row == float(site)) & (group != sub_iota + float(site * NSUB)), FAR, 0.0
            )
            for site in range(NSITE)
        ]
        columns = (
            (gap, [f - 0.5 * p for f, p in zip(far, pair)]),
            (jnp.where(rows == 3, lam, 0.0), pair),
            (jnp.where(rows == 3, 1.0, 0.0), by_group(half, group, sub_iota)),
            (jnp.where(rows == 4, ratio, 0.0), [nothing] * NSITE),
        )
        for column, (table, member) in enumerate(columns):
            high, middle, low = split3(table)
            tops = [m.astype(jnp.bfloat16).astype(jnp.float32) for m in member]
            rests = [m - t for m, t in zip(member, tops)]
            rhs_ref[:, column * lanes : (column + 1) * lanes] = jnp.concatenate(
                [high, middle, high, middle, low, high] + tops + rests + pad, axis=0
            ).astype(jnp.bfloat16)

        def one_partner(k, sums):
            index = part_ref[tile, k]
            out = jnp.dot(feat_ref[index], rhs_ref[...], preferred_element_type=jnp.float32)
            fx, fy, fz, fo, fd = sums
            for i in range(lanes // 8):
                here = slice(8 * i, 8 * i + 8)
                gap2, s, w, q = (out[here, c * lanes : (c + 1) * lanes] for c in range(4))
                xb, yb, zb, eb = (
                    wide_ref[index, here, c * lanes : (c + 1) * lanes] for c in range(4)
                )
                rs = lax.rsqrt(gap2)
                t = rs * rs * rs
                a = eb * t
                b = (s * t) * (a + 0.25 * q)
                sens = rs * (a + q) + b
                fx = fx + b * xb
                fy = fy + b * yb
                fz = fz + b * zb
                fo = fo + b
                fd = fd + sens * w
            return fx, fy, fz, fo, fd

        sums = lax.fori_loop(0, count_ref[tile], one_partner, (nothing,) * 5)
        fx, fy, fz, fo, fd = (jnp.sum(value, axis=0, keepdims=True) for value in sums)
        forces = jnp.concatenate(
            [moved[r : r + 1, :] * fo - f for r, f in enumerate((fx, fy, fz))], axis=0
        )
        rs = lax.rsqrt(1.5 - 0.5 * lam)
        t = rs * rs * rs
        a, q = strength * t, ratio * charge
        itself = rs * (a + q) + lam * t * (a + 0.25 * q)
        drive = strength * (fd - 0.5 * itself)
        finish_tile(cfg, tile, (4.0 * strength) * forces, drive, block, ins, outs, sub_iota)
        return carry

    lax.fori_loop(0, cfg["tiles"], one_tile, 0)


def any_forces(cfg, count_ref, part_ref, pool_ref, col_ref, fcol_ref, ins, outs, sub_iota):
    tiles, lanes = cfg["tiles"], cfg["lanes"]
    chunk = 32

    def one_tile(tile, carry):
        own = (tile // cfg["rows_y"] + 1) * (cfg["rows_y"] + 2) + tile % cfg["rows_y"] + 1
        block = pool_ref[own]
        col_ref[...] = block.T
        count = count_ref[tile]

        def one_chunk(c, carry):
            start = pl.multiple_of(c * chunk, chunk)
            cols = col_ref[pl.ds(start, chunk), :]
            lanes_iota = lax.broadcasted_iota(jnp.int32, (chunk, lanes), 1)
            diagonal = lanes_iota == lax.broadcasted_iota(jnp.int32, (chunk, lanes), 0) + start

            def one_partner(k, sums):
                fx, fy, fz, fd = sums
                index = part_ref[tile, k]
                other = pool_ref[index]

                def own_col(row):
                    return cols[:, row : row + 1]

                def other_row(row):
                    return other[row : row + 1, :]

                dx = wrap_image(own_col(X) - other_row(X), cfg["box_x"])
                dy = wrap_image(own_col(Y) - other_row(Y), cfg["box_y"])
                dz = own_col(Z) - other_row(Z)
                r2 = dx * dx + dy * dy + dz * dz
                same = (own_col(GRP) == other_row(GRP)) & (own_col(GRP) >= 0.0)
                site = (own_col(SIT) == other_row(SIT)) & (own_col(SIT) >= 0.0)
                drop = (site & jnp.logical_not(same)) | (diagonal & (index == own))
                lam_a, lam_b = own_col(LAM), other_row(LAM)
                s = jnp.where(same, lam_a, lam_a * lam_b)
                w = jnp.where(same, 0.5, lam_b)
                e = own_col(STR) * other_row(STR)
                q = own_col(CHG) * other_row(CHG)
                rs = lax.rsqrt(1.0 + 0.5 * (1.0 - s) + r2)
                t = rs * rs * rs
                a = e * t
                b = s * t * (a + 0.25 * q)
                sens = rs * (a + q) + b
                b = jnp.where(drop, 0.0, b)
                sens = jnp.where(drop, 0.0, sens * w)
                return fx + b * dx, fy + b * dy, fz + b * dz, fd + sens

            zero = jnp.zeros((chunk, lanes), jnp.float32)
            sums = lax.fori_loop(0, count, one_partner, (zero, zero, zero, zero))
            for row, value in enumerate(sums):
                fcol_ref[pl.ds(start, chunk), row : row + 1] = jnp.sum(
                    value, axis=1, keepdims=True
                )
            return carry

        lax.fori_loop(0, lanes // chunk, one_chunk, 0)
        forces = fcol_ref[...].T
        finish_tile(
            cfg, tile, 4.0 * forces[0:3, :], forces[3:4, :], block,
            ins, outs, sub_iota,
        )
        return carry

    lax.fori_loop(0, tiles, one_tile, 0)


def finish_tile(cfg, tile, forces, drive, block, ins, outs, sub_iota):
    vel_ref, noise_ref, inv_ref = ins
    pay_ref, velo_ref, sum_ref = outs
    damping = math.exp(-friction_rate * step_size)
    inverse = inv_ref[tile]
    speeds = (
        damping * vel_ref[tile, 0:3, :]
        + step_size * forces * inverse
        + jnp.sqrt((1.0 - damping**2) * inverse) * noise_ref[0, tile]
    )
    velo_ref[tile] = speeds
    pay_ref[tile, 0:3, :] = block[0:3, :] + step_size * speeds
    group = block[GRP : GRP + 1, :]
    for site in range(NSITE):
        sum_ref[site] += jnp.where(group == sub_iota + float(site * NSUB), drive, 0.0)


def pay_sums(cfg, pay_ref, sum_ref):
    lanes = cfg["lanes"]
    share = lanes // NSITE
    lane_site = lax.broadcasted_iota(jnp.int32, (NSUB, lanes), 1) // share
    packed = jnp.zeros((NSUB, lanes), jnp.float32)
    for site in range(NSITE):
        folded = sum_ref[site]
        width = lanes
        while width > share:
            width //= 2
            folded = folded + pltpu.roll(folded, width, 1)
        packed = packed + jnp.where(lane_site == site, folded, 0.0)
    for sub in range(cfg["tiles"]):
        pay_ref[sub, 3:4, :] = (
            packed[sub : sub + 1, :] if sub < NSUB else jnp.zeros((1, lanes), jnp.float32)
        )


def step_call(cfg, moment, count, parts, places, blocks, stats, totals, vel, ang, noise, anoise, inverse):
    tiles, lanes = cfg["tiles"], cfg["lanes"]
    nb = cfg["blocks"]
    vmem = pl.BlockSpec(memory_space=pltpu.VMEM)
    smem = pl.BlockSpec(memory_space=pltpu.SMEM)
    noise_spec = pl.BlockSpec((1, tiles, 3, lanes), lambda i: (moment, 0, 0, 0))

    return pl.pallas_call(
        functools.partial(step_kernel, cfg, moment),
        grid=(1,),
        out_shape=(
            jax.ShapeDtypeStruct((tiles, 4, lanes), jnp.float32),
            jax.ShapeDtypeStruct((tiles, 3, lanes), jnp.float32),
            jax.ShapeDtypeStruct((2, NSITE, NSUB, lanes), jnp.float32),
        ),
        in_specs=[smem, smem, smem] + [vmem] * (2 * nb + 3) + [noise_spec, vmem, vmem],
        out_specs=(vmem, vmem, vmem),
        scratch_shapes=[
            pltpu.VMEM((cfg["pool"], 8, lanes), jnp.float32),
            pltpu.VMEM((lanes, 8), jnp.float32),
            pltpu.VMEM((lanes, 8), jnp.float32),
            pltpu.VMEM((NSITE, NSUB, lanes), jnp.float32),
            pltpu.VMEM((cfg["pool"], lanes, cfg["depth"]), jnp.bfloat16),
            pltpu.VMEM((cfg["pool"], lanes, 4 * lanes), jnp.float32),
            pltpu.VMEM((cfg["depth"], 4 * lanes), jnp.bfloat16),
            pltpu.VMEM((cfg["depth"], 4 * lanes), jnp.bfloat16),
        ],
        name="langevin_step",
    )(count, parts, places, *blocks, *stats, totals, vel, ang, noise, anoise, inverse)


def per_device(
    positions,
    velocities,
    lambda_theta,
    theta_velocity,
    source_slot,
    atom_noise,
    theta_noise,
    charges,
    strengths,
    inverse_mass,
    atom_site,
    atom_sub,
    partners,
):
    count_x, count_y = lax.axis_size("gx"), lax.axis_size("gy")
    peers = lax.axis_size("walker")
    rows_x, rows_y, lanes = charges.shape
    tiles = rows_x * rows_y
    offsets = neighbour_offsets(count_x, count_y)
    cfg = dict(
        blocks=1 + len(offsets),
        covered=1 + len(offsets) == count_x * count_y,
        tiles=tiles,
        lanes=lanes,
        rows_y=rows_y,
        pool=(rows_x + 2) * (rows_y + 2),
        sources=pool_sources(rows_x, rows_y, count_x, count_y, offsets),
        depth=128,
        roomy=min(rows_x * count_x, rows_y * count_y) >= 8,
        box_x=float(rows_x * count_x),
        box_y=float(rows_y * count_y),
        angle_mass=rows_x * count_x * rows_y * count_y * lanes * theta_share,
    )

    def gather_blocks(value):
        return [value] + [shifted(value, offset, count_x, count_y) for offset in offsets]

    is_group = atom_site < NSITE
    groups = jnp.where(is_group, atom_site * NSUB + atom_sub, -1)
    sites = jnp.where(is_group, atom_site, -1)
    stat = jnp.stack(
        [charges, strengths, groups.astype(jnp.float32), sites.astype(jnp.float32)], axis=2
    ).reshape(tiles, 4, lanes)
    stats = gather_blocks(stat)

    mine = source_slot[lax.axis_index("walker")]
    angles = jnp.stack([lambda_theta[0], theta_velocity[0]]).reshape(1, 2 * NSITE * NSUB)
    angles = jnp.pad(angles, ((0, 0), (0, lanes - 2 * NSITE * NSUB)))
    extra = jnp.broadcast_to(angles[:, None, :], (tiles, 1, lanes))
    first = jnp.concatenate([positions.reshape(tiles, 3, lanes), extra], axis=1)
    second = velocities.reshape(tiles, 3, lanes)

    def picked(value):
        everyone = lax.all_to_all(
            jnp.broadcast_to(value, (peers,) + value.shape), "walker", 0, 0, tiled=True
        )
        return lax.dynamic_index_in_dim(everyone, mine, 0, keepdims=False)

    start = picked(first)
    vel = picked(second)
    ang = start[0, 3, : 2 * NSITE * NSUB].reshape(2, NSITE, NSUB, 1)
    ang = jnp.broadcast_to(ang, (2, NSITE, NSUB, lanes))
    anoise = jnp.broadcast_to(theta_noise[0][..., None], (STEPS, NSITE, NSUB, lanes))
    noise = atom_noise.reshape(STEPS, tiles, 3, lanes)
    inverse = inverse_mass.reshape(tiles, 1, lanes)
    parts = partners.reshape(tiles, -1)
    count = jnp.sum((parts >= 0).astype(jnp.int32), axis=1)

    def line(axis, rows, count):
        at = lax.axis_index(axis)
        ring = jnp.arange(rows + 2)
        turn = jnp.where(ring == 0, jnp.where(at == 0, -1.0, 0.0), 0.0)
        turn = jnp.where(ring == rows + 1, jnp.where(at == count - 1, 1.0, 0.0), turn)
        middle = at.astype(jnp.float32) * rows + 0.5 * rows
        shift = turn * (rows * count) - middle
        return shift, shift - (ring.astype(jnp.float32) - 0.5 - 0.5 * rows)

    shift_x, cell_x = line("gx", rows_x, count_x)
    shift_y, cell_y = line("gy", rows_y, count_y)
    places = jnp.stack(
        [
            jnp.broadcast_to(value, (rows_x + 2, rows_y + 2)).reshape(-1)
            for value in (shift_x[:, None], shift_y, cell_x[:, None], cell_y)
        ]
    )

    pay = start
    for moment in range(STEPS):
        blocks = gather_blocks(pay)
        if moment > 0 and not cfg["covered"]:
            totals = lax.psum(pay[:NSUB, 3, :], ("gx", "gy"))
        else:
            totals = jnp.zeros((NSUB, lanes), jnp.float32)
        pay, vel, ang = step_call(
            cfg, moment, count, parts, places, blocks, stats, totals, vel, ang, noise, anoise, inverse
        )
    packed = pay[:NSUB, 3, :]
    if cfg["covered"]:
        totals = packed
        for offset in offsets:
            totals = totals + shifted(packed, offset, count_x, count_y)
    else:
        totals = lax.psum(packed, ("gx", "gy"))
    angles, aspeeds = angle_step(ang[0], ang[1], totals, anoise[STEPS - 1], cfg["angle_mass"])
    displacement = (pay[:, 0:3, :] - start[:, 0:3, :]).reshape(positions.shape)
    return (
        displacement,
        vel.reshape(velocities.shape),
        angles[None, :, :, 0],
        aspeeds[None, :, :, 0],
    )


def solution(mesh):
    in_specs = (
        P("walker", "gx", "gy", None, None),
        P("walker", "gx", "gy", None, None),
        P("walker", None, None),
        P("walker", None, None),
        P(),
        P("walker", None, "gx", "gy", None, None),
        P("walker", None, None, None),
        P("gx", "gy", None),
        P("gx", "gy", None),
        P("gx", "gy", None),
        P("gx", "gy", None),
        P("gx", "gy", None),
        P("gx", "gy", None),
    )
    out_specs = (
        P("walker", "gx", "gy", None, None),
        P("walker", "gx", "gy", None, None),
        P("walker", None, None),
        P("walker", None, None),
    )
    return jax.shard_map(
        per_device, mesh=mesh, in_specs=in_specs, out_specs=out_specs, check_vma=False
    )
```

profile of v0, /device:TPU:0, one launch (start us, length us, event | category | flops | bytes accessed | tf_op | source)
XLA Modules:
  0.0 213.2 jit_solution(5932426681781914915)
XLA Ops:
  0.6 0.7 copy.31
  1.4 0.7 broadcast_in_dim.96
  2.1 7.4 %all-to-all-start.1 = ((f32[8,16,3,128]{3,1,2,0:T(8,128)}), f32[8,16,3,128]{3,1,2,0:T(8,128)S(1)}, u32[]{:S(2)}, u32[]{:S(2)}) async-start(f32[8,16,3,128]{3,1,2,0:T(8,128)} %broadcast_in_dim.96), calls=%async_computation.1 | async-start | bytes 393216 | tf_op jit(solution)/shard_map/all_to_all | solution.py:479
  9.5 0.1 reshape.75
  9.7 0.7 copy-done.25
  10.4 7.1 %all-to-all-done.1 = f32[8,16,3,128]{3,1,2,0:T(8,128)S(1)} async-done(((f32[8,16,3,128]{3,1,2,0:T(8,128)}), f32[8,16,3,128]{3,1,2,0:T(8,128)S(1)}, u32[]{:S(2)}, u32[]{:S(2)}) %all-to-all-start.1) | async-done | bytes 196640 | tf_op jit(solution)/shard_map/all_to_all | solution.py:479
  17.4 0.7 broadcast_in_dim.94
  18.2 3.5 %all-to-all-start = ((f32[8,16,4,128]{3,2,1,0:T(4,128)}), f32[8,16,4,128]{3,2,1,0:T(4,128)S(1)}, u32[]{:S(2)}, u32[]{:S(2)}) async-start(f32[8,16,4,128]{3,2,1,0:T(4,128)} %broadcast_in_dim.94), calls=%async_computation | async-start | bytes 524288 | tf_op jit(solution)/shard_map/all_to_all | solution.py:479
  21.8 0.2 collective-permute-start.3
  22.0 1.4 collective-permute-start.4
  23.5 0.3 collective-permute-start.5
  23.7 0.7 copy-done.31
  24.4 0.6 dynamic_slice.11
  26.3 0.1 broadcast_in_dim.86
  26.4 0.1 stack_reshape.12
  26.5 0.1 stack_reshape.13
  26.5 0.1 broadcast_in_dim.90
  26.6 0.1 stack_reshape.14
  26.7 0.1 stack_reshape.15
  26.8 0.7 copy.33
  27.5 0.1 convert_reduce_fusion
  27.6 0.6 reduce_sum.66.refs_0_
  28.9 0.6 pad_maximum_fusion.4.refs_2_
  29.5 0.6 copy.38
  30.2 1.2 collective-permute-start
  31.3 0.8 collective-permute-start.1
  32.1 0.1 broadcast_in_dim.97
  32.2 1.3 collective-permute-done.refs_4_
  33.5 1.7 collective-permute-done.1.refs_5_
  35.2 0.7 broadcast_in_dim.98.refs_13_
  36.0 0.7 broadcast_in_dim.100.refs_15_
  36.7 0.6 broadcast_8_refs_11_.2.refs_11_
  37.3 38.3 %langevin_step.4 = (f32[16,4,128]{2,1,0:T(4,128)}, f32[16,3,128]{2,1,0:T(4,128)}, f32[2,4,8,128]{3,2,1,0:T(8,128)}) custom-call(s32[16]{0:T(128)} %reduce_sum.66.refs_0_, s32[16,9]{1,0:T(8,128)} %bitcast.43, f32[4,36]{1,0:T(4,128)} %pad_maximum_fusion.4.refs_2_, f32[16,4,128]{2,1,0:T(4,128)} %copy-done.4, f32[16,4,128]{2,1,0:T(4,128)} %copy-done.9, ...), custom_call_target="tpu_custom_call" | custom-call | tf_op jit(solution)/shard_map/langevin_step/pallas_call | solution.py:401
  75.6 2.2 %collective-permute-start.7 = (f32[16,4,128]{2,1,0:T(4,128)}, f32[16,4,128]{2,1,0:T(4,128)S(1)}, u32[]{:S(2)}, u32[]{:S(2)}) collective-permute-start(f32[16,4,128]{2,1,0:T(4,128)} %get-tuple-element.16.refs_3_), channel_id=1, source_target_pairs={{2,0},{3,1},{0,2},{1,3},{6,4},{7,5},{4,6},{5,7},{10,8},{11,9},{8,1... | collective-permute-start | bytes 98312 | tf_op jit(solution)/shard_map/ppermute | solution.py:51
  77.8 1.4 collective-permute-done.6.refs_4_
  79.2 1.1 collective-permute-done.7.refs_5_
  80.2 0.6 copy-done.18
  80.8 38.3 %langevin_step.5 = (f32[16,4,128]{2,1,0:T(4,128)}, f32[16,3,128]{2,1,0:T(4,128)}, f32[2,4,8,128]{3,2,1,0:T(8,128)}) custom-call(s32[16]{0:T(128)} %reduce_sum.66.refs_0_, s32[16,9]{1,0:T(8,128)} %bitcast.44, f32[4,36]{1,0:T(4,128)} %pad_maximum_fusion.4.refs_2_, f32[16,4,128]{2,1,0:T(4,128)} %get-tuple-element.16.refs_3_, f32[16,4,128]{2,1,0:T(4,128)} %copy-done.16, ...), custom_call_target="tpu_custom_call" | custom-call | tf_op jit(solution)/shard_map/langevin_step/pallas_call | solution.py:401
  119.2 0.7 collective-permute-start.11
  119.9 1.4 collective-permute-start.9
  121.3 2.2 %collective-permute-done.10.refs_5_ = f32[16,4,128]{2,1,0:T(4,128)S(1)} collective-permute-done((f32[16,4,128]{2,1,0:T(4,128)}, f32[16,4,128]{2,1,0:T(4,128)S(1)}, u32[]{:S(2)}, u32[]{:S(2)}) %collective-permute-start.10) | collective-permute-done | bytes 32800 | tf_op jit(solution)/shard_map/ppermute | solution.py:51
  123.6 0.2 collective-permute-done.9.refs_4_
  123.8 0.4 copy-done.15
  124.2 0.2 copy-done.19
  124.4 38.3 %langevin_step.6 = (f32[16,4,128]{2,1,0:T(4,128)}, f32[16,3,128]{2,1,0:T(4,128)}, f32[2,4,8,128]{3,2,1,0:T(8,128)}) custom-call(s32[16]{0:T(128)} %reduce_sum.66.refs_0_, s32[16,9]{1,0:T(8,128)} %bitcast.45, f32[4,36]{1,0:T(4,128)} %pad_maximum_fusion.4.refs_2_, f32[16,4,128]{2,1,0:T(4,128)} %get-tuple-element.19.refs_3_, f32[16,4,128]{2,1,0:T(4,128)} %copy-done.19, ...), custom_call_target="tpu_custom_call" | custom-call | tf_op jit(solution)/shard_map/langevin_step/pallas_call | solution.py:401
  162.7 2.9 %collective-permute-start.13 = (f32[16,4,128]{2,1,0:T(4,128)}, f32[16,4,128]{2,1,0:T(4,128)S(1)}, u32[]{:S(2)}, u32[]{:S(2)}) collective-permute-start(f32[16,4,128]{2,1,0:T(4,128)} %get-tuple-element.22.refs_3_), channel_id=1, source_target_pairs={{2,0},{3,1},{0,2},{1,3},{6,4},{7,5},{4,6},{5,7},{10,8},{11,9},{8,1... | collective-permute-start | bytes 98312 | tf_op jit(solution)/shard_map/ppermute | solution.py:51
  165.6 0.6 collective-permute-done.12.refs_4_
  166.3 1.8 collective-permute-done.13.refs_5_
  168.1 0.6 copy-done.12
  168.7 38.3 %langevin_step.7 = (f32[16,4,128]{2,1,0:T(4,128)}, f32[16,3,128]{2,1,0:T(4,128)}, f32[2,4,8,128]{3,2,1,0:T(8,128)}) custom-call(s32[16]{0:T(128)} %reduce_sum.66.refs_0_, s32[16,9]{1,0:T(8,128)} %bitcast.46, f32[4,36]{1,0:T(4,128)} %pad_maximum_fusion.4.refs_2_, f32[16,4,128]{2,1,0:T(4,128)} %get-tuple-element.22.refs_3_, f32[16,4,128]{2,1,0:T(4,128)} %copy-done.11, ...), custom_call_target="tpu_custom_call" | custom-call | tf_op jit(solution)/shard_map/langevin_step/pallas_call | solution.py:401
  207.0 0.8 copy.34
  207.9 2.3 %collective-permute-start.16 = (f32[8,128]{1,0:T(8,128)S(1)}, f32[8,128]{1,0:T(8,128)S(1)}, u32[]{:S(2)}, u32[]{:S(2)}) collective-permute-start(f32[8,128]{1,0:T(8,128)S(1)} %slice_bitcast_fusion.1), channel_id=1, source_target_pairs={{2,0},{3,1},{0,2},{1,3},{6,4},{7,5},{4,6},{5,7},{10,8},{11,9},{8,1... | collective-permute-start | bytes 12296 | tf_op jit(solution)/shard_map/ppermute | solution.py:51
  210.2 0.1 fusion.2
  210.3 0.6 copy.35
  210.9 0.1 copy-done.21
  211.1 0.6 copy.36
  211.7 0.1 collective-permute-done.16
  211.8 0.1 select_reduce_fusion.3
  211.9 0.1 stack_broadcast_in_dim.10
  212.0 0.1 stack_broadcast_in_dim.11
  212.1 0.1 stack_broadcast_in_dim.8
  212.1 0.1 stack_broadcast_in_dim.9
  212.2 0.3 fusion.8
  212.5 0.7 slice_reduce_fusion
  (95 shorter events, 0.5 us)
Async XLA Ops:
  2.1 7.4 %copy-start.29 = (f32[1,4,8]{2,1,0:T(4,128)S(1)}, f32[1,4,8]{2,1,0:T(4,128)}, u32[]{:S(2)}) copy-start(f32[1,4,8]{2,1,0:T(4,128)} %param.16) | copy-start | bytes 388
  2.1 7.4 %copy-start.30 = (f32[1,4,8]{2,1,0:T(4,128)S(1)}, f32[1,4,8]{2,1,0:T(4,128)}, u32[]{:S(2)}) copy-start(f32[1,4,8]{2,1,0:T(4,128)} %param.15) | copy-start | bytes 388
  2.1 7.5 %copy-start.22 = (f32[1,4,4,3,128]{4,2,3,1,0:T(4,128)S(1)}, f32[1,4,4,3,128]{4,2,3,1,0:T(4,128)}, u32[]{:S(2)}) copy-start(f32[1,4,4,3,128]{4,2,3,1,0:T(4,128)} %param.13) | copy-start | bytes 73732
  2.1 15.4 %all-to-all-start.1 = ((f32[8,16,3,128]{3,1,2,0:T(8,128)}), f32[8,16,3,128]{3,1,2,0:T(8,128)S(1)}, u32[]{:S(2)}, u32[]{:S(2)}) async-start(f32[8,16,3,128]{3,1,2,0:T(8,128)} %broadcast_in_dim.96), calls=%async_computation.1 | async-start | bytes 393216 | tf_op jit(solution)/shard_map/all_to_all | solution.py:479
  9.6 0.7 copy-start.25
  9.7 0.7 copy-start.26
  18.2 3.6 %copy-start.27 = (f32[4,4,128]{2,1,0:T(4,128)S(1)}, f32[4,4,128]{2,1,0:T(4,128)}, u32[]{:S(2)}) copy-start(f32[4,4,128]{2,1,0:T(4,128)} %param.21) | copy-start | bytes 24580
  18.2 3.6 %copy-start.28 = (f32[4,4,128]{2,1,0:T(4,128)S(1)}, f32[4,4,128]{2,1,0:T(4,128)}, u32[]{:S(2)}) copy-start(f32[4,4,128]{2,1,0:T(4,128)} %param.20) | copy-start | bytes 24580
  18.2 12.0 %all-to-all-start = ((f32[8,16,4,128]{3,2,1,0:T(4,128)}), f32[8,16,4,128]{3,2,1,0:T(4,128)S(1)}, u32[]{:S(2)}, u32[]{:S(2)}) async-start(f32[8,16,4,128]{3,2,1,0:T(4,128)} %broadcast_in_dim.94), calls=%async_computation | async-start | bytes 524288 | tf_op jit(solution)/shard_map/all_to_all | solution.py:479
  21.7 5.1 %copy-start.8 = (f32[1,4,4,4,3,128]{5,3,4,2,1,0:T(4,128)S(1)}, f32[1,4,4,4,3,128]{5,3,4,2,1,0:T(4,128)}, u32[]{:S(2)}) copy-start(f32[1,4,4,4,3,128]{5,3,4,2,1,0:T(4,128)} %param.18) | copy-start | bytes 294916
  21.8 4.5 %copy-start = (f32[16,4,128]{2,1,0:T(4,128)}, f32[16,4,128]{2,1,0:T(4,128)S(1)}, u32[]{:S(2)}) copy-start(f32[16,4,128]{2,1,0:T(4,128)S(1)} %pad_maximum_fusion.1.refs_7_) | copy-start | bytes 98308
  21.8 10.3 %collective-permute-start.3 = (f32[16,4,128]{2,1,0:T(4,128)S(1)}, f32[16,4,128]{2,1,0:T(4,128)S(1)}, u32[]{:S(2)}, u32[]{:S(2)}) collective-permute-start(f32[16,4,128]{2,1,0:T(4,128)S(1)} %pad_maximum_fusion.1.refs_7_), channel_id=1, source_target_pairs={{3,0},{2,1},{1,2},{0,3},{7,4},{6,5},{5,6},{4,7},{11,8},{10,9},{9,1... | collective-permute-start | bytes 98312 | tf_op jit(solution)/shard_map/ppermute | solution.py:51
  22.0 10.2 %collective-permute-start.4 = (f32[16,4,128]{2,1,0:T(4,128)S(1)}, f32[16,4,128]{2,1,0:T(4,128)S(1)}, u32[]{:S(2)}, u32[]{:S(2)}) collective-permute-start(f32[16,4,128]{2,1,0:T(4,128)S(1)} %pad_maximum_fusion.1.refs_7_), channel_id=1, source_target_pairs={{2,0},{3,1},{0,2},{1,3},{6,4},{7,5},{4,6},{5,7},{10,8},{11,9},{8,1... | collective-permute-start | bytes 98312 | tf_op jit(solution)/shard_map/ppermute | solution.py:51
  23.5 8.7 %collective-permute-start.5 = (f32[16,4,128]{2,1,0:T(4,128)S(1)}, f32[16,4,128]{2,1,0:T(4,128)S(1)}, u32[]{:S(2)}, u32[]{:S(2)}) collective-permute-start(f32[16,4,128]{2,1,0:T(4,128)S(1)} %pad_maximum_fusion.1.refs_7_), channel_id=1, source_target_pairs={{1,0},{0,1},{3,2},{2,3},{5,4},{4,5},{7,6},{6,7},{9,8},{8,9},{11,10... | collective-permute-start | bytes 98312 | tf_op jit(solution)/shard_map/ppermute | solution.py:51
  23.7 0.7 copy-start.31
  26.8 0.7 copy-start.6
  30.2 7.1 %copy-start.4 = (f32[16,4,128]{2,1,0:T(4,128)}, f32[16,4,128]{2,1,0:T(4,128)S(1)}, u32[]{:S(2)}) copy-start(f32[16,4,128]{2,1,0:T(4,128)S(1)} %dynamic-slice_bitcast_fusion.refs_3_) | copy-start | bytes 98308
  30.2 3.4 %collective-permute-start = (f32[16,4,128]{2,1,0:T(4,128)S(1)}, f32[16,4,128]{2,1,0:T(4,128)S(1)}, u32[]{:S(2)}, u32[]{:S(2)}) collective-permute-start(f32[16,4,128]{2,1,0:T(4,128)S(1)} %dynamic-slice_bitcast_fusion.refs_3_), channel_id=1, source_target_pairs={{3,0},{2,1},{1,2},{0,3},{7,4},{6,5},{5,6},{4,7},{11,8},{10,9},{9,1... | collective-permute-start | bytes 98312 | tf_op jit(solution)/shard_map/ppermute | solution.py:51
  31.3 3.9 %collective-permute-start.1 = (f32[16,4,128]{2,1,0:T(4,128)S(1)}, f32[16,4,128]{2,1,0:T(4,128)S(1)}, u32[]{:S(2)}, u32[]{:S(2)}) collective-permute-start(f32[16,4,128]{2,1,0:T(4,128)S(1)} %dynamic-slice_bitcast_fusion.refs_3_), channel_id=1, source_target_pairs={{2,0},{3,1},{0,2},{1,3},{6,4},{7,5},{4,6},{5,7},{10,8},{11,9},{8,1... | collective-permute-start | bytes 98312 | tf_op jit(solution)/shard_map/ppermute | solution.py:51
  32.1 4.6 %copy-start.1 = (f32[16,4,128]{2,1,0:T(4,128)}, f32[16,4,128]{2,1,0:T(4,128)S(1)}, u32[]{:S(2)}) copy-start(f32[16,4,128]{2,1,0:T(4,128)S(1)} %collective-permute-done.3.refs_8_) | copy-start | bytes 98308
  32.1 3.2 %collective-permute-start.2 = (f32[16,4,128]{2,1,0:T(4,128)S(1)}, f32[16,4,128]{2,1,0:T(4,128)S(1)}, u32[]{:S(2)}, u32[]{:S(2)}) collective-permute-start(f32[16,4,128]{2,1,0:T(4,128)S(1)} %dynamic-slice_bitcast_fusion.refs_3_), channel_id=1, source_target_pairs={{1,0},{0,1},{3,2},{2,3},{5,4},{4,5},{7,6},{6,7},{9,8},{8,9},{11,10... | collective-permute-start | bytes 98312 | tf_op jit(solution)/shard_map/ppermute | solution.py:51
  32.2 4.5 %copy-start.2 = (f32[16,4,128]{2,1,0:T(4,128)}, f32[16,4,128]{2,1,0:T(4,128)S(1)}, u32[]{:S(2)}) copy-start(f32[16,4,128]{2,1,0:T(4,128)S(1)} %collective-permute-done.4.refs_9_) | copy-start | bytes 98308
  32.2 4.5 %copy-start.3 = (f32[16,4,128]{2,1,0:T(4,128)}, f32[16,4,128]{2,1,0:T(4,128)S(1)}, u32[]{:S(2)}) copy-start(f32[16,4,128]{2,1,0:T(4,128)S(1)} %collective-permute-done.5.refs_10_) | copy-start | bytes 98308
  33.5 3.7 %copy-start.9 = (f32[16,4,128]{2,1,0:T(4,128)}, f32[16,4,128]{2,1,0:T(4,128)S(1)}, u32[]{:S(2)}) copy-start(f32[16,4,128]{2,1,0:T(4,128)S(1)} %collective-permute-done.refs_4_) | copy-start | bytes 98308
  35.2 2.0 copy-start.10
  35.2 2.0 copy-start.13
  35.2 0.7 copy-start.23
  75.6 3.6 %collective-permute-start.6 = (f32[16,4,128]{2,1,0:T(4,128)}, f32[16,4,128]{2,1,0:T(4,128)S(1)}, u32[]{:S(2)}, u32[]{:S(2)}) collective-permute-start(f32[16,4,128]{2,1,0:T(4,128)} %get-tuple-element.16.refs_3_), channel_id=1, source_target_pairs={{3,0},{2,1},{1,2},{0,3},{7,4},{6,5},{5,6},{4,7},{11,8},{10,9},{9,1... | collective-permute-start | bytes 98312 | tf_op jit(solution)/shard_map/ppermute | solution.py:51
  75.6 4.6 %collective-permute-start.7 = (f32[16,4,128]{2,1,0:T(4,128)}, f32[16,4,128]{2,1,0:T(4,128)S(1)}, u32[]{:S(2)}, u32[]{:S(2)}) collective-permute-start(f32[16,4,128]{2,1,0:T(4,128)} %get-tuple-element.16.refs_3_), channel_id=1, source_target_pairs={{2,0},{3,1},{0,2},{1,3},{6,4},{7,5},{4,6},{5,7},{10,8},{11,9},{8,1... | collective-permute-start | bytes 98312 | tf_op jit(solution)/shard_map/ppermute | solution.py:51
  77.8 2.5 %collective-permute-start.8 = (f32[16,4,128]{2,1,0:T(4,128)}, f32[16,4,128]{2,1,0:T(4,128)S(1)}, u32[]{:S(2)}, u32[]{:S(2)}) collective-permute-start(f32[16,4,128]{2,1,0:T(4,128)} %get-tuple-element.16.refs_3_), channel_id=1, source_target_pairs={{1,0},{0,1},{3,2},{2,3},{5,4},{4,5},{7,6},{6,7},{9,8},{8,9},{11,10... | collective-permute-start | bytes 98312 | tf_op jit(solution)/shard_map/ppermute | solution.py:51
  79.2 1.1 copy-start.16
  80.2 0.6 copy-start.18
  80.2 0.6 copy-start.20
  119.2 4.4 %collective-permute-start.10 = (f32[16,4,128]{2,1,0:T(4,128)}, f32[16,4,128]{2,1,0:T(4,128)S(1)}, u32[]{:S(2)}, u32[]{:S(2)}) collective-permute-start(f32[16,4,128]{2,1,0:T(4,128)} %get-tuple-element.19.refs_3_), channel_id=1, source_target_pairs={{2,0},{3,1},{0,2},{1,3},{6,4},{7,5},{4,6},{5,7},{10,8},{11,9},{8,1... | collective-permute-start | bytes 98312 | tf_op jit(solution)/shard_map/ppermute | solution.py:51
  119.2 4.4 %collective-permute-start.11 = (f32[16,4,128]{2,1,0:T(4,128)}, f32[16,4,128]{2,1,0:T(4,128)S(1)}, u32[]{:S(2)}, u32[]{:S(2)}) collective-permute-start(f32[16,4,128]{2,1,0:T(4,128)} %get-tuple-element.19.refs_3_), channel_id=1, source_target_pairs={{1,0},{0,1},{3,2},{2,3},{5,4},{4,5},{7,6},{6,7},{9,8},{8,9},{11,10... | collective-permute-start | bytes 98312 | tf_op jit(solution)/shard_map/ppermute | solution.py:51
  119.9 3.9 %collective-permute-start.9 = (f32[16,4,128]{2,1,0:T(4,128)}, f32[16,4,128]{2,1,0:T(4,128)S(1)}, u32[]{:S(2)}, u32[]{:S(2)}) collective-permute-start(f32[16,4,128]{2,1,0:T(4,128)} %get-tuple-element.19.refs_3_), channel_id=1, source_target_pairs={{3,0},{2,1},{1,2},{0,3},{7,4},{6,5},{5,6},{4,7},{11,8},{10,9},{9,1... | collective-permute-start | bytes 98312 | tf_op jit(solution)/shard_map/ppermute | solution.py:51
  123.6 0.6 copy-start.15
  123.6 0.6 copy-start.17
  123.8 0.6 copy-start.19
  162.7 3.6 %collective-permute-start.12 = (f32[16,4,128]{2,1,0:T(4,128)}, f32[16,4,128]{2,1,0:T(4,128)S(1)}, u32[]{:S(2)}, u32[]{:S(2)}) collective-permute-start(f32[16,4,128]{2,1,0:T(4,128)} %get-tuple-element.22.refs_3_), channel_id=1, source_target_pairs={{3,0},{2,1},{1,2},{0,3},{7,4},{6,5},{5,6},{4,7},{11,8},{10,9},{9,1... | collective-permute-start | bytes 98312 | tf_op jit(solution)/shard_map/ppermute | solution.py:51
  162.7 5.4 %collective-permute-start.13 = (f32[16,4,128]{2,1,0:T(4,128)}, f32[16,4,128]{2,1,0:T(4,128)S(1)}, u32[]{:S(2)}, u32[]{:S(2)}) collective-permute-start(f32[16,4,128]{2,1,0:T(4,128)} %get-tuple-element.22.refs_3_), channel_id=1, source_target_pairs={{2,0},{3,1},{0,2},{1,3},{6,4},{7,5},{4,6},{5,7},{10,8},{11,9},{8,1... | collective-permute-start | bytes 98312 | tf_op jit(solution)/shard_map/ppermute | solution.py:51
  165.6 2.5 %collective-permute-start.14 = (f32[16,4,128]{2,1,0:T(4,128)}, f32[16,4,128]{2,1,0:T(4,128)S(1)}, u32[]{:S(2)}, u32[]{:S(2)}) collective-permute-start(f32[16,4,128]{2,1,0:T(4,128)} %get-tuple-element.22.refs_3_), channel_id=1, source_target_pairs={{1,0},{0,1},{3,2},{2,3},{5,4},{4,5},{7,6},{6,7},{9,8},{8,9},{11,10... | collective-permute-start | bytes 98312 | tf_op jit(solution)/shard_map/ppermute | solution.py:51
  166.3 1.8 copy-start.11
  168.1 0.6 copy-start.12
  168.1 0.6 copy-start.14
  207.0 3.1 %copy-start.5 = (f32[16,4,128]{2,1,0:T(4,128)S(1)}, f32[16,4,128]{2,1,0:T(4,128)}, u32[]{:S(2)}) copy-start(f32[16,4,128]{2,1,0:T(4,128)} %copy-done.4) | copy-start | bytes 98308
  207.0 3.1 %copy-start.7 = (f32[16,4,128]{2,1,0:T(4,128)S(1)}, f32[16,4,128]{2,1,0:T(4,128)}, u32[]{:S(2)}) copy-start(f32[16,4,128]{2,1,0:T(4,128)} %get-tuple-element.25) | copy-start | bytes 98308
  207.9 2.3 %copy-start.24 = (f32[2,4,8,128]{3,2,1,0:T(8,128)S(1)}, f32[2,4,8,128]{3,2,1,0:T(8,128)}, u32[]{:S(2)}) copy-start(f32[2,4,8,128]{3,2,1,0:T(8,128)} %get-tuple-element.27) | copy-start | bytes 98308
  207.9 3.8 %collective-permute-start.15 = (f32[8,128]{1,0:T(8,128)S(1)}, f32[8,128]{1,0:T(8,128)S(1)}, u32[]{:S(2)}, u32[]{:S(2)}) collective-permute-start(f32[8,128]{1,0:T(8,128)S(1)} %slice_bitcast_fusion.1), channel_id=1, source_target_pairs={{3,0},{2,1},{1,2},{0,3},{7,4},{6,5},{5,6},{4,7},{11,8},{10,9},{9,1... | collective-permute-start | bytes 12296 | tf_op jit(solution)/shard_map/ppermute | solution.py:51
  207.9 3.9 %collective-permute-start.16 = (f32[8,128]{1,0:T(8,128)S(1)}, f32[8,128]{1,0:T(8,128)S(1)}, u32[]{:S(2)}, u32[]{:S(2)}) collective-permute-start(f32[8,128]{1,0:T(8,128)S(1)} %slice_bitcast_fusion.1), channel_id=1, source_target_pairs={{2,0},{3,1},{0,2},{1,3},{6,4},{7,5},{4,6},{5,7},{10,8},{11,9},{8,1... | collective-permute-start | bytes 12296 | tf_op jit(solution)/shard_map/ppermute | solution.py:51
  210.1 1.6 collective-permute-start.17
  210.3 0.8 copy-start.21
where the time goes:
time: 213 us
  Pallas kernels  153 us (72%)
  starting transfers between devices  24.3 us (11%)
  waiting for transfers between devices  17.6 us (8%)
  local copies, waits for them, and re-layouts  13.1 us (6%)
  between operations  2.92 us (1%)
    pallas_call x4, Pallas kernels, step_call(): pl.pallas_call(functools.partial(step_kernel, cfg, moment), grid=(1,), ou...  153 us
    ppermute x18, starting transfers between devices, shifted(): return lax.ppermute(value, ('gx', 'gy'), pairs)  13.3 us
    all_to_all x2, starting transfers between devices, picked(): lax.all_to_all(jnp.broadcast_to(value, (peers,) + value.shape), 'walker',...  11 us
    ppermute x18, waiting for transfers between devices, shifted(): return lax.ppermute(value, ('gx', 'gy'), pairs)  10.5 us
    all_to_all x2, waiting for transfers between devices, picked(): lax.all_to_all(jnp.broadcast_to(value, (peers,) + value.shape), 'walker',...  7.11 us
    unnamed x69, local copies, waits for them, and re-layouts  6.09 us
  transfers between devices with their start and end apart: 20, of which 10 were waited for; matrix products, arithmetic and copies ran while one was open for 3% of the time, Pallas kernels for 0%

commit v1 on v0

--- a/solution.py
+++ b/solution.py
@@ -22,6 +22,8 @@
 MIDDLE_Z = 1.0
 REACH = 1.49
 FAR = 2.0**126
+GROUP = 9
+ROWS = 16
 
 X, Y, Z, LAM, CHG, STR, GRP, SIT = range(8)
 
@@ -103,7 +105,7 @@
     stat_refs = refs[2 + nb : 2 + 2 * nb]
     tot_ref, vel_ref, ang_ref, noise_ref, anoise_ref, inv_ref = refs[2 + 2 * nb : 8 + 2 * nb]
     pay_ref, velo_ref, ango_ref = refs[8 + 2 * nb : 11 + 2 * nb]
-    pool_ref, col_ref, fcol_ref, sum_ref, feat_ref, wide_ref, rhs_ref, sel_ref = refs[11 + 2 * nb :]
+    pool_ref, col_ref, fcol_ref, sum_ref, feat_ref, wide_ref, rhs_ref, coef_ref = refs[11 + 2 * nb :]
 
     angles, aspeeds = ang_ref[0], ang_ref[1]
     if moment > 0:
@@ -148,7 +150,7 @@
     def _():
         near_forces(
             cfg, lambdas, count_ref, part_ref, off_ref, pool_ref, feat_ref, wide_ref, rhs_ref,
-            sel_ref, ins, outs, sub_iota,
+            coef_ref, ins, outs, sub_iota,
         )
 
     @pl.when(jnp.logical_not(near))
@@ -174,7 +176,7 @@
 
 def near_forces(
     cfg, lambdas, count_ref, part_ref, off_ref, pool_ref, feat_ref, wide_ref, rhs_ref,
-    sel_ref, ins, outs, sub_iota,
+    coef_ref, ins, outs, sub_iota,
 ):
     lanes = cfg["lanes"]
     depth = cfg["depth"]
@@ -184,11 +186,8 @@
     pad = [nothing] * ((depth - 6 * 8 - 2 * NSITE * NSUB) // 8)
 
     pick_rows = lax.broadcasted_iota(jnp.int32, (depth, lanes), 0)
-    for column, row in enumerate((0, 1, 2, 7)):
-        hit = (pick_rows == row) | (pick_rows == 16 + row) | (pick_rows == 40 + row)
-        sel_ref[:, column * lanes : (column + 1) * lanes] = jnp.where(hit, 1.0, 0.0).astype(
-            jnp.bfloat16
-        )
+    hit = (pick_rows == 7) | (pick_rows == 16 + 7) | (pick_rows == 40 + 7)
+    pick = jnp.where(hit, 1.0, 0.0).astype(jnp.bfloat16)
 
     def centred(index):
         block = pool_ref[index]
@@ -199,7 +198,16 @@
         square = jnp.where(rows < 3, moved * moved, 0.0)
         return block, moved, jnp.sum(square, axis=0, keepdims=True)
 
-    def one_pool(index, carry):
+    def table_dot(features, ref):
+        table = jnp.concatenate([ref[c] for c in range(ref.shape[0])], axis=1)
+        return jnp.dot(features, table, preferred_element_type=jnp.float32)
+
+    def some_pool(k, carry):
+        for u in range(cfg["pool_group"]):
+            one_pool(k * cfg["pool_group"] + u)
+        return carry
+
+    def one_pool(index):
         block, moved, norm = centred(index)
         table = jnp.where(rows == 5, norm, moved)
         table = jnp.where(rows == 6, 1.0, table)
@@ -211,10 +219,15 @@
         )
         features = features.T.astype(jnp.bfloat16)
         feat_ref[index] = features
-        wide_ref[index] = jnp.dot(features, sel_ref[...], preferred_element_type=jnp.float32)
-        return carry
-
-    lax.fori_loop(0, cfg["pool"], one_pool, 0)
+        wide_ref[index] = jnp.dot(features, pick, preferred_element_type=jnp.float32)
+        coef = jnp.concatenate([high, middle, low, nothing], axis=0).astype(jnp.bfloat16)
+        coef_ref[index] = jnp.concatenate([coef, coef], axis=1)
+
+    lax.fori_loop(0, cfg["pool"] // cfg["pool_group"], some_pool, 0)
+    none_columns = lax.broadcasted_iota(jnp.int32, (lanes, depth), 1)
+    feat_ref[cfg["pool"]] = jnp.where(none_columns == 6, 1.0, 0.0).astype(jnp.bfloat16)
+    wide_ref[cfg["pool"]] = jnp.zeros((lanes, lanes), jnp.float32)
+    coef_ref[cfg["pool"]] = jnp.zeros((32, 2 * lanes), jnp.bfloat16)
 
     spread = [lam - lam * lam for lam in lambdas]
     half = [0.5 - lam for lam in lambdas]
@@ -247,37 +260,44 @@
             high, middle, low = split3(table)
             tops = [m.astype(jnp.bfloat16).astype(jnp.float32) for m in member]
             rests = [m - t for m, t in zip(member, tops)]
-            rhs_ref[:, column * lanes : (column + 1) * lanes] = jnp.concatenate(
+            rhs_ref[column] = jnp.concatenate(
                 [high, middle, high, middle, low, high] + tops + rests + pad, axis=0
             ).astype(jnp.bfloat16)
 
-        def one_partner(k, sums):
-            index = part_ref[tile, k]
-            out = jnp.dot(feat_ref[index], rhs_ref[...], preferred_element_type=jnp.float32)
-            fx, fy, fz, fo, fd = sums
-            for i in range(lanes // 8):
-                here = slice(8 * i, 8 * i + 8)
-                gap2, s, w, q = (out[here, c * lanes : (c + 1) * lanes] for c in range(4))
-                xb, yb, zb, eb = (
-                    wide_ref[index, here, c * lanes : (c + 1) * lanes] for c in range(4)
+        def some_partners(k, sums):
+            indices = [part_ref[tile, GROUP * k + u] for u in range(GROUP)]
+            outs = [table_dot(feat_ref[index], rhs_ref) for index in indices]
+            moments, fd = sums
+            for index, out in zip(indices, outs):
+                tops, rests = [], []
+                for i in range(lanes // ROWS):
+                    here = slice(ROWS * i, ROWS * i + ROWS)
+                    gap2, s, w, q = (out[here, c * lanes : (c + 1) * lanes] for c in range(4))
+                    eb = wide_ref[index, here, :]
+                    rs = lax.rsqrt(gap2)
+                    t = rs * rs * rs
+                    a = eb * t
+                    b = (s * t) * (a + 0.25 * q)
+                    sens = (rs * (a + q) + b) * w
+                    for j in range(ROWS // 8):
+                        fd = fd + sens[8 * j : 8 * j + 8, :]
+                    top = b.astype(jnp.bfloat16)
+                    tops.append(top)
+                    rests.append((b - top.astype(jnp.float32)).astype(jnp.bfloat16))
+                moments = moments + jnp.dot(
+                    coef_ref[index],
+                    jnp.concatenate(tops + rests, axis=0),
+                    preferred_element_type=jnp.float32,
                 )
-                rs = lax.rsqrt(gap2)
-                t = rs * rs * rs
-                a = eb * t
-                b = (s * t) * (a + 0.25 * q)
-                sens = rs * (a + q) + b
-                fx = fx + b * xb
-                fy = fy + b * yb
-                fz = fz + b * zb
-                fo = fo + b
-                fd = fd + sens * w
-            return fx, fy, fz, fo, fd
-
-        sums = lax.fori_loop(0, count_ref[tile], one_partner, (nothing,) * 5)
-        fx, fy, fz, fo, fd = (jnp.sum(value, axis=0, keepdims=True) for value in sums)
-        forces = jnp.concatenate(
-            [moved[r : r + 1, :] * fo - f for r, f in enumerate((fx, fy, fz))], axis=0
-        )
+            return moments, fd
+
+        groups = (count_ref[tile] + GROUP - 1) // GROUP
+        moments, fd = lax.fori_loop(
+            0, groups, some_partners, (jnp.zeros((32, lanes), jnp.float32), nothing)
+        )
+        moments = moments[0:8] + moments[8:16] + moments[16:24]
+        fd = jnp.sum(fd, axis=0, keepdims=True)
+        forces = moved[0:3, :] * moments[6:7, :] - moments[0:3, :]
         rs = lax.rsqrt(1.5 - 0.5 * lam)
         t = rs * rs * rs
         a, q = strength * t, ratio * charge
@@ -413,13 +433,32 @@
             pltpu.VMEM((lanes, 8), jnp.float32),
             pltpu.VMEM((lanes, 8), jnp.float32),
             pltpu.VMEM((NSITE, NSUB, lanes), jnp.float32),
-            pltpu.VMEM((cfg["pool"], lanes, cfg["depth"]), jnp.bfloat16),
-            pltpu.VMEM((cfg["pool"], lanes, 4 * lanes), jnp.float32),
-            pltpu.VMEM((cfg["depth"], 4 * lanes), jnp.bfloat16),
-            pltpu.VMEM((cfg["depth"], 4 * lanes), jnp.bfloat16),
+            pltpu.VMEM((cfg["pool"] + 1, lanes, cfg["depth"]), jnp.bfloat16),
+            pltpu.VMEM((cfg["pool"] + 1, lanes, lanes), jnp.float32),
+            pltpu.VMEM((4, cfg["depth"], lanes), jnp.bfloat16),
+            pltpu.VMEM((cfg["pool"] + 1, 32, 2 * lanes), jnp.bfloat16),
         ],
         name="langevin_step",
     )(count, parts, places, *blocks, *stats, totals, vel, ang, noise, anoise, inverse)
+
+
+def make_cfg(rows_x, rows_y, lanes, count_x, count_y, offsets):
+    tiles = rows_x * rows_y
+    return dict(
+        blocks=1 + len(offsets),
+        covered=1 + len(offsets) == count_x * count_y,
+        tiles=tiles,
+        lanes=lanes,
+        rows_y=rows_y,
+        pool=(rows_x + 2) * (rows_y + 2),
+        sources=pool_sources(rows_x, rows_y, count_x, count_y, offsets),
+        depth=128,
+        pool_group=next(g for g in (12, 6, 4, 3, 2, 1) if (rows_x + 2) * (rows_y + 2) % g == 0),
+        roomy=min(rows_x * count_x, rows_y * count_y) >= 8,
+        box_x=float(rows_x * count_x),
+        box_y=float(rows_y * count_y),
+        angle_mass=rows_x * count_x * rows_y * count_y * lanes * theta_share,
+    )
 
 
 def per_device(
@@ -442,20 +481,7 @@
     rows_x, rows_y, lanes = charges.shape
     tiles = rows_x * rows_y
     offsets = neighbour_offsets(count_x, count_y)
-    cfg = dict(
-        blocks=1 + len(offsets),
-        covered=1 + len(offsets) == count_x * count_y,
-        tiles=tiles,
-        lanes=lanes,
-        rows_y=rows_y,
-        pool=(rows_x + 2) * (rows_y + 2),
-        sources=pool_sources(rows_x, rows_y, count_x, count_y, offsets),
-        depth=128,
-        roomy=min(rows_x * count_x, rows_y * count_y) >= 8,
-        box_x=float(rows_x * count_x),
-        box_y=float(rows_y * count_y),
-        angle_mass=rows_x * count_x * rows_y * count_y * lanes * theta_share,
-    )
+    cfg = make_cfg(rows_x, rows_y, lanes, count_x, count_y, offsets)
 
     def gather_blocks(value):
         return [value] + [shifted(value, offset, count_x, count_y) for offset in offsets]
@@ -490,6 +516,10 @@
     inverse = inverse_mass.reshape(tiles, 1, lanes)
     parts = partners.reshape(tiles, -1)
     count = jnp.sum((parts >= 0).astype(jnp.int32), axis=1)
+    parts = jnp.where(parts < 0, cfg["pool"], parts)
+    parts = jnp.pad(
+        parts, ((0, 0), (0, -parts.shape[1] % GROUP)), constant_values=cfg["pool"]
+    )
 
     def line(axis, rows, count):
         at = lax.axis_index(axis)

time: 213 us -> 118 us (0.55)
  Pallas kernels: 153 us -> 55.5 us
    pallas_call x4, Pallas kernels: 153 us -> 55.5 us  [step_call(): pl.pallas_call(functools.partial(step_kernel, cfg, moment), grid=(1,), ou...]
    unnamed x69 -> x67, local copies, waits for them, and re-layouts: 6.09 us -> 6.73 us
  transfers between devices with their start and end apart: 20 -> 20, of which waited for: 10 -> 11; matrix products, arithmetic and copies ran while one was open for 3% -> 6% of each run, Pallas kernels for 0% -> 0%
where the time goes in v1:
time: 118 us; the launch traced here: 117 us
  Pallas kernels  55.5 us (47%)
  starting transfers between devices  22.8 us (19%)
  waiting for transfers between devices  19.3 us (16%)
  local copies, waits for them, and re-layouts  13.7 us (12%)
  other arithmetic  3.36 us (3%)
  between operations  2.87 us (2%)
    pallas_call x4, Pallas kernels, step_call(): pl.pallas_call(functools.partial(step_kernel, cfg, moment), grid=(1,), ou...  55.5 us
    ppermute x18, starting transfers between devices, shifted(): return lax.ppermute(value, ('gx', 'gy'), pairs)  13.1 us
    ppermute x18, waiting for transfers between devices, shifted(): return lax.ppermute(value, ('gx', 'gy'), pairs)  11 us
    all_to_all x2, starting transfers between devices, picked(): lax.all_to_all(jnp.broadcast_to(value, (peers,) + value.shape), 'walker',...  9.7 us
    all_to_all x2, waiting for transfers between devices, picked(): lax.all_to_all(jnp.broadcast_to(value, (peers,) + value.shape), 'walker',...  8.29 us
    unnamed x67, local copies, waits for them, and re-layouts  6.73 us
  transfers between devices with their start and end apart: 20, of which 11 were waited for; matrix products, arithmetic and copies ran while one was open for 6% of the time, Pallas kernels for 0%

profile of v1, /device:TPU:0, one launch (start us, length us, event | category | flops | bytes accessed | tf_op | source)
XLA Modules:
  0.0 117.5 jit_solution(8613819978558576648)
XLA Ops:
  0.6 0.7 fusion.12
  1.4 0.7 copy-done.26
  2.1 2.5 %collective-permute-start.3 = (f32[16,4,128]{2,1,0:T(4,128)S(1)}, f32[16,4,128]{2,1,0:T(4,128)S(1)}, u32[]{:S(2)}, u32[]{:S(2)}) collective-permute-start(f32[16,4,128]{2,1,0:T(4,128)S(1)} %pad_maximum_fusion.1.refs_7_), channel_id=1, source_target_pairs={{3,0},{2,1},{1,2},{0,3},{7,4},{6,5},{5,6},{4,7},{11,8},{10,9},{9,1... | collective-permute-start | bytes 98312 | tf_op jit(solution)/shard_map/ppermute | solution.py:53
  4.6 0.6 collective-permute-start.4
  5.3 0.7 broadcast_in_dim.101
  6.0 6.2 %all-to-all-start.1 = ((f32[8,16,3,128]{3,1,2,0:T(8,128)}), f32[8,16,3,128]{3,1,2,0:T(8,128)S(1)}, u32[]{:S(2)}, u32[]{:S(2)}) async-start(f32[8,16,3,128]{3,1,2,0:T(8,128)} %broadcast_in_dim.101), calls=%async_computation.1 | async-start | bytes 393216 | tf_op jit(solution)/shard_map/all_to_all | solution.py:505
  12.2 0.7 copy-done.23
  12.9 0.1 reshape.75
  13.1 0.7 copy-done.21
  13.7 0.1 convert_reduce_fusion
  13.9 6.6 %all-to-all-done.1 = f32[8,16,3,128]{3,1,2,0:T(8,128)S(1)} async-done(((f32[8,16,3,128]{3,1,2,0:T(8,128)}), f32[8,16,3,128]{3,1,2,0:T(8,128)S(1)}, u32[]{:S(2)}, u32[]{:S(2)}) %all-to-all-start.1) | async-done | bytes 196640 | tf_op jit(solution)/shard_map/all_to_all | solution.py:505
  20.5 0.7 broadcast_in_dim.99
  21.3 3.5 %all-to-all-start = ((f32[8,16,4,128]{3,2,1,0:T(4,128)}), f32[8,16,4,128]{3,2,1,0:T(4,128)S(1)}, u32[]{:S(2)}, u32[]{:S(2)}) async-start(f32[8,16,4,128]{3,2,1,0:T(4,128)} %broadcast_in_dim.99), calls=%async_computation | async-start | bytes 524288 | tf_op jit(solution)/shard_map/all_to_all | solution.py:505
  24.8 0.6 copy-done.30
  25.5 0.6 dynamic_slice.11
  27.4 0.1 stack_reshape.12
  27.5 0.1 stack_reshape.13
  27.7 0.1 stack_reshape.14
  27.8 0.1 stack_reshape.15
  27.8 0.7 copy.33
  28.6 0.6 reduce_sum.66.refs_0_
  29.8 0.6 pad_maximum_fusion.4.refs_2_
  30.4 0.6 compare_select_fusion.refs_1_
  31.0 0.6 copy.38
  31.6 1.6 %all-to-all-done = f32[8,16,4,128]{3,2,1,0:T(4,128)S(1)} async-done(((f32[8,16,4,128]{3,2,1,0:T(4,128)}), f32[8,16,4,128]{3,2,1,0:T(4,128)S(1)}, u32[]{:S(2)}, u32[]{:S(2)}) %all-to-all-start) | async-done | bytes 262176 | tf_op jit(solution)/shard_map/all_to_all | solution.py:505
  33.3 1.5 %collective-permute-start.1 = (f32[16,4,128]{2,1,0:T(4,128)S(1)}, f32[16,4,128]{2,1,0:T(4,128)S(1)}, u32[]{:S(2)}, u32[]{:S(2)}) collective-permute-start(f32[16,4,128]{2,1,0:T(4,128)S(1)} %dynamic-slice_bitcast_fusion.refs_3_), channel_id=1, source_target_pairs={{2,0},{3,1},{0,2},{1,3},{6,4},{7,5},{4,6},{5,7},{10,8},{11,9},{8,1... | collective-permute-start | bytes 98312 | tf_op jit(solution)/shard_map/ppermute | solution.py:53
  34.7 0.4 collective-permute-start.2
  35.2 0.1 broadcast_in_dim.102
  35.3 1.6 %collective-permute-done.refs_4_ = f32[16,4,128]{2,1,0:T(4,128)S(1)} collective-permute-done((f32[16,4,128]{2,1,0:T(4,128)S(1)}, f32[16,4,128]{2,1,0:T(4,128)S(1)}, u32[]{:S(2)}, u32[]{:S(2)}) %collective-permute-start) | collective-permute-done | bytes 32800 | tf_op jit(solution)/shard_map/ppermute | solution.py:53
  36.9 0.4 collective-permute-done.1.refs_5_
  37.3 0.7 broadcast_in_dim.103.refs_13_
  38.0 0.7 broadcast_in_dim.105.refs_15_
  38.7 0.6 broadcast_9_refs_11_.2.refs_11_
  39.3 13.9 %langevin_step.4 = (f32[16,4,128]{2,1,0:T(4,128)}, f32[16,3,128]{2,1,0:T(4,128)}, f32[2,4,8,128]{3,2,1,0:T(8,128)}) custom-call(s32[16]{0:T(128)} %reduce_sum.66.refs_0_, s32[16,9]{1,0:T(8,128)} %compare_select_fusion.refs_1_, f32[4,36]{1,0:T(4,128)} %pad_maximum_fusion.4.refs_2_, f32[16,4,128]{2,1,0:T(4,128)} %copy-done.4, f32[16,4,128]{2,1,0:T(4,128)} %copy-done.8, ...), custom_call_target="tpu_custom_call" | custom-call | tf_op jit(solution)/shard_map/langevin_step/pallas_call | solution.py:421
  53.2 0.9 collective-permute-start.6
  54.1 1.0 collective-permute-start.7
  55.1 1.6 %collective-permute-done.6.refs_4_ = f32[16,4,128]{2,1,0:T(4,128)S(1)} collective-permute-done((f32[16,4,128]{2,1,0:T(4,128)}, f32[16,4,128]{2,1,0:T(4,128)S(1)}, u32[]{:S(2)}, u32[]{:S(2)}) %collective-permute-start.6) | collective-permute-done | bytes 32800 | tf_op jit(solution)/shard_map/ppermute | solution.py:53
  56.7 1.5 %collective-permute-done.7.refs_5_ = f32[16,4,128]{2,1,0:T(4,128)S(1)} collective-permute-done((f32[16,4,128]{2,1,0:T(4,128)}, f32[16,4,128]{2,1,0:T(4,128)S(1)}, u32[]{:S(2)}, u32[]{:S(2)}) %collective-permute-start.7) | collective-permute-done | bytes 32800 | tf_op jit(solution)/shard_map/ppermute | solution.py:53
  58.3 0.6 copy-done.17
  58.9 13.9 %langevin_step.5 = (f32[16,4,128]{2,1,0:T(4,128)}, f32[16,3,128]{2,1,0:T(4,128)}, f32[2,4,8,128]{3,2,1,0:T(8,128)}) custom-call(s32[16]{0:T(128)} %reduce_sum.66.refs_0_, s32[16,9]{1,0:T(8,128)} %compare_select_fusion.refs_1_, f32[4,36]{1,0:T(4,128)} %pad_maximum_fusion.4.refs_2_, f32[16,4,128]{2,1,0:T(4,128)} %get-tuple-element.16.refs_3_, ...), custom_call_target="tpu_custom_call" | custom-call | tf_op jit(solution)/shard_map/langevin_step/pallas_call | solution.py:421
  72.8 1.0 collective-permute-start.10
  73.7 1.1 collective-permute-start.9
  74.9 2.0 %collective-permute-done.10.refs_5_ = f32[16,4,128]{2,1,0:T(4,128)S(1)} collective-permute-done((f32[16,4,128]{2,1,0:T(4,128)}, f32[16,4,128]{2,1,0:T(4,128)S(1)}, u32[]{:S(2)}, u32[]{:S(2)}) %collective-permute-start.10) | collective-permute-done | bytes 32800 | tf_op jit(solution)/shard_map/ppermute | solution.py:53
  76.9 0.4 collective-permute-done.9.refs_4_
  77.3 0.2 copy-done.14
  77.5 0.4 copy-done.18
  77.9 13.9 %langevin_step.6 = (f32[16,4,128]{2,1,0:T(4,128)}, f32[16,3,128]{2,1,0:T(4,128)}, f32[2,4,8,128]{3,2,1,0:T(8,128)}) custom-call(s32[16]{0:T(128)} %reduce_sum.66.refs_0_, s32[16,9]{1,0:T(8,128)} %compare_select_fusion.refs_1_, f32[4,36]{1,0:T(4,128)} %pad_maximum_fusion.4.refs_2_, f32[16,4,128]{2,1,0:T(4,128)} %get-tuple-element.19.refs_3_, ...), custom_call_target="tpu_custom_call" | custom-call | tf_op jit(solution)/shard_map/langevin_step/pallas_call | solution.py:421
  91.8 1.2 collective-permute-start.12
  92.9 1.0 collective-permute-start.13
  93.9 1.4 %collective-permute-done.12.refs_4_ = f32[16,4,128]{2,1,0:T(4,128)S(1)} collective-permute-done((f32[16,4,128]{2,1,0:T(4,128)}, f32[16,4,128]{2,1,0:T(4,128)S(1)}, u32[]{:S(2)}, u32[]{:S(2)}) %collective-permute-start.12) | collective-permute-done | bytes 32800 | tf_op jit(solution)/shard_map/ppermute | solution.py:53
  95.3 1.7 %collective-permute-done.13.refs_5_ = f32[16,4,128]{2,1,0:T(4,128)S(1)} collective-permute-done((f32[16,4,128]{2,1,0:T(4,128)}, f32[16,4,128]{2,1,0:T(4,128)S(1)}, u32[]{:S(2)}, u32[]{:S(2)}) %collective-permute-start.13) | collective-permute-done | bytes 32800 | tf_op jit(solution)/shard_map/ppermute | solution.py:53
  97.1 0.6 copy-done.11
  97.7 13.9 %langevin_step.7 = (f32[16,4,128]{2,1,0:T(4,128)}, f32[16,3,128]{2,1,0:T(4,128)}, f32[2,4,8,128]{3,2,1,0:T(8,128)}) custom-call(s32[16]{0:T(128)} %reduce_sum.66.refs_0_, s32[16,9]{1,0:T(8,128)} %compare_select_fusion.refs_1_, f32[4,36]{1,0:T(4,128)} %pad_maximum_fusion.4.refs_2_, f32[16,4,128]{2,1,0:T(4,128)} %get-tuple-element.22.refs_3_, ...), custom_call_target="tpu_custom_call" | custom-call | tf_op jit(solution)/shard_map/langevin_step/pallas_call | solution.py:421
  111.6 0.8 copy.34
  112.4 1.1 collective-permute-start.16
  113.5 0.8 collective-permute-start.17
  114.3 0.1 fusion.2
  114.4 0.6 copy.35
  115.0 0.1 copy-done.20
  115.2 0.6 copy.36
  115.8 0.3 collective-permute-done.16
  116.1 0.1 select_reduce_fusion.3
  116.5 0.3 fusion.8
  116.8 0.7 slice_reduce_fusion
  (94 shorter events, 0.8 us)
Async XLA Ops:
  0.6 0.7 copy-start.27
  1.4 0.7 copy-start.26
  2.1 3.2 %copy-start.22 = (f32[1,4,4,3,128]{4,2,3,1,0:T(4,128)S(1)}, f32[1,4,4,3,128]{4,2,3,1,0:T(4,128)}, u32[]{:S(2)}) copy-start(f32[1,4,4,3,128]{4,2,3,1,0:T(4,128)} %param.14) | copy-start | bytes 73732
  2.1 3.9 %copy-start = (f32[16,4,128]{2,1,0:T(4,128)}, f32[16,4,128]{2,1,0:T(4,128)S(1)}, u32[]{:S(2)}) copy-start(f32[16,4,128]{2,1,0:T(4,128)S(1)} %pad_maximum_fusion.1.refs_7_) | copy-start | bytes 98308
  2.1 32.6 %collective-permute-start.3 = (f32[16,4,128]{2,1,0:T(4,128)S(1)}, f32[16,4,128]{2,1,0:T(4,128)S(1)}, u32[]{:S(2)}, u32[]{:S(2)}) collective-permute-start(f32[16,4,128]{2,1,0:T(4,128)S(1)} %pad_maximum_fusion.1.refs_7_), channel_id=1, source_target_pairs={{3,0},{2,1},{1,2},{0,3},{7,4},{6,5},{5,6},{4,7},{11,8},{10,9},{9,1... | collective-permute-start | bytes 98312 | tf_op jit(solution)/shard_map/ppermute | solution.py:53
  4.6 30.6 %collective-permute-start.4 = (f32[16,4,128]{2,1,0:T(4,128)S(1)}, f32[16,4,128]{2,1,0:T(4,128)S(1)}, u32[]{:S(2)}, u32[]{:S(2)}) collective-permute-start(f32[16,4,128]{2,1,0:T(4,128)S(1)} %pad_maximum_fusion.1.refs_7_), channel_id=1, source_target_pairs={{2,0},{3,1},{0,2},{1,3},{6,4},{7,5},{4,6},{5,7},{10,8},{11,9},{8,1... | collective-permute-start | bytes 98312 | tf_op jit(solution)/shard_map/ppermute | solution.py:53
  5.3 30.0 %collective-permute-start.5 = (f32[16,4,128]{2,1,0:T(4,128)S(1)}, f32[16,4,128]{2,1,0:T(4,128)S(1)}, u32[]{:S(2)}, u32[]{:S(2)}) collective-permute-start(f32[16,4,128]{2,1,0:T(4,128)S(1)} %pad_maximum_fusion.1.refs_7_), channel_id=1, source_target_pairs={{1,0},{0,1},{3,2},{2,3},{5,4},{4,5},{7,6},{6,7},{9,8},{8,9},{11,10... | collective-permute-start | bytes 98312 | tf_op jit(solution)/shard_map/ppermute | solution.py:53
  6.0 6.2 %copy-start.28 = (f32[1,4,8]{2,1,0:T(4,128)S(1)}, f32[1,4,8]{2,1,0:T(4,128)}, u32[]{:S(2)}) copy-start(f32[1,4,8]{2,1,0:T(4,128)} %param.16) | copy-start | bytes 388
  6.0 6.2 %copy-start.29 = (f32[1,4,8]{2,1,0:T(4,128)S(1)}, f32[1,4,8]{2,1,0:T(4,128)}, u32[]{:S(2)}) copy-start(f32[1,4,8]{2,1,0:T(4,128)} %param.15) | copy-start | bytes 388
  6.0 14.5 %all-to-all-start.1 = ((f32[8,16,3,128]{3,1,2,0:T(8,128)}), f32[8,16,3,128]{3,1,2,0:T(8,128)S(1)}, u32[]{:S(2)}, u32[]{:S(2)}) async-start(f32[8,16,3,128]{3,1,2,0:T(8,128)} %broadcast_in_dim.101), calls=%async_computation.1 | async-start | bytes 393216 | tf_op jit(solution)/shard_map/all_to_all | solution.py:505
  12.2 0.7 copy-start.23
  13.0 0.7 copy-start.21
  21.3 6.6 %copy-start.7 = (f32[1,4,4,4,3,128]{5,3,4,2,1,0:T(4,128)S(1)}, f32[1,4,4,4,3,128]{5,3,4,2,1,0:T(4,128)}, u32[]{:S(2)}) copy-start(f32[1,4,4,4,3,128]{5,3,4,2,1,0:T(4,128)} %param.18) | copy-start | bytes 294916
  21.3 12.0 %all-to-all-start = ((f32[8,16,4,128]{3,2,1,0:T(4,128)}), f32[8,16,4,128]{3,2,1,0:T(4,128)S(1)}, u32[]{:S(2)}, u32[]{:S(2)}) async-start(f32[8,16,4,128]{3,2,1,0:T(4,128)} %broadcast_in_dim.99), calls=%async_computation | async-start | bytes 524288 | tf_op jit(solution)/shard_map/all_to_all | solution.py:505
  24.8 0.7 copy-start.30
  33.3 6.0 %copy-start.4 = (f32[16,4,128]{2,1,0:T(4,128)}, f32[16,4,128]{2,1,0:T(4,128)S(1)}, u32[]{:S(2)}) copy-start(f32[16,4,128]{2,1,0:T(4,128)S(1)} %dynamic-slice_bitcast_fusion.refs_3_) | copy-start | bytes 98308
  33.3 3.6 %collective-permute-start = (f32[16,4,128]{2,1,0:T(4,128)S(1)}, f32[16,4,128]{2,1,0:T(4,128)S(1)}, u32[]{:S(2)}, u32[]{:S(2)}) collective-permute-start(f32[16,4,128]{2,1,0:T(4,128)S(1)} %dynamic-slice_bitcast_fusion.refs_3_), channel_id=1, source_target_pairs={{3,0},{2,1},{1,2},{0,3},{7,4},{6,5},{5,6},{4,7},{11,8},{10,9},{9,1... | collective-permute-start | bytes 98312 | tf_op jit(solution)/shard_map/ppermute | solution.py:53
  33.3 4.0 %collective-permute-start.1 = (f32[16,4,128]{2,1,0:T(4,128)S(1)}, f32[16,4,128]{2,1,0:T(4,128)S(1)}, u32[]{:S(2)}, u32[]{:S(2)}) collective-permute-start(f32[16,4,128]{2,1,0:T(4,128)S(1)} %dynamic-slice_bitcast_fusion.refs_3_), channel_id=1, source_target_pairs={{2,0},{3,1},{0,2},{1,3},{6,4},{7,5},{4,6},{5,7},{10,8},{11,9},{8,1... | collective-permute-start | bytes 98312 | tf_op jit(solution)/shard_map/ppermute | solution.py:53
  34.7 4.0 %copy-start.1 = (f32[16,4,128]{2,1,0:T(4,128)}, f32[16,4,128]{2,1,0:T(4,128)S(1)}, u32[]{:S(2)}) copy-start(f32[16,4,128]{2,1,0:T(4,128)S(1)} %collective-permute-done.3.refs_8_) | copy-start | bytes 98308
  34.7 2.5 %collective-permute-start.2 = (f32[16,4,128]{2,1,0:T(4,128)S(1)}, f32[16,4,128]{2,1,0:T(4,128)S(1)}, u32[]{:S(2)}, u32[]{:S(2)}) collective-permute-start(f32[16,4,128]{2,1,0:T(4,128)S(1)} %dynamic-slice_bitcast_fusion.refs_3_), channel_id=1, source_target_pairs={{1,0},{0,1},{3,2},{2,3},{5,4},{4,5},{7,6},{6,7},{9,8},{8,9},{11,10... | collective-permute-start | bytes 98312 | tf_op jit(solution)/shard_map/ppermute | solution.py:53
  35.2 3.5 %copy-start.2 = (f32[16,4,128]{2,1,0:T(4,128)}, f32[16,4,128]{2,1,0:T(4,128)S(1)}, u32[]{:S(2)}) copy-start(f32[16,4,128]{2,1,0:T(4,128)S(1)} %collective-permute-done.4.refs_9_) | copy-start | bytes 98308
  35.3 3.5 %copy-start.3 = (f32[16,4,128]{2,1,0:T(4,128)}, f32[16,4,128]{2,1,0:T(4,128)S(1)}, u32[]{:S(2)}) copy-start(f32[16,4,128]{2,1,0:T(4,128)S(1)} %collective-permute-done.5.refs_10_) | copy-start | bytes 98308
  36.9 2.4 %copy-start.8 = (f32[16,4,128]{2,1,0:T(4,128)}, f32[16,4,128]{2,1,0:T(4,128)S(1)}, u32[]{:S(2)}) copy-start(f32[16,4,128]{2,1,0:T(4,128)S(1)} %collective-permute-done.refs_4_) | copy-start | bytes 98308
  37.3 2.1 %copy-start.9 = (f32[16,4,128]{2,1,0:T(4,128)}, f32[16,4,128]{2,1,0:T(4,128)S(1)}, u32[]{:S(2)}) copy-start(f32[16,4,128]{2,1,0:T(4,128)S(1)} %collective-permute-done.1.refs_5_) | copy-start | bytes 98308
  37.3 2.1 %copy-start.12 = (f32[16,4,128]{2,1,0:T(4,128)}, f32[16,4,128]{2,1,0:T(4,128)S(1)}, u32[]{:S(2)}) copy-start(f32[16,4,128]{2,1,0:T(4,128)S(1)} %collective-permute-done.2.refs_6_) | copy-start | bytes 98308
  37.3 0.7 copy-start.24
  53.2 3.6 %collective-permute-start.6 = (f32[16,4,128]{2,1,0:T(4,128)}, f32[16,4,128]{2,1,0:T(4,128)S(1)}, u32[]{:S(2)}, u32[]{:S(2)}) collective-permute-start(f32[16,4,128]{2,1,0:T(4,128)} %get-tuple-element.16.refs_3_), channel_id=1, source_target_pairs={{3,0},{2,1},{1,2},{0,3},{7,4},{6,5},{5,6},{4,7},{11,8},{10,9},{9,1... | collective-permute-start | bytes 98312 | tf_op jit(solution)/shard_map/ppermute | solution.py:53
  54.1 4.2 %collective-permute-start.7 = (f32[16,4,128]{2,1,0:T(4,128)}, f32[16,4,128]{2,1,0:T(4,128)S(1)}, u32[]{:S(2)}, u32[]{:S(2)}) collective-permute-start(f32[16,4,128]{2,1,0:T(4,128)} %get-tuple-element.16.refs_3_), channel_id=1, source_target_pairs={{2,0},{3,1},{0,2},{1,3},{6,4},{7,5},{4,6},{5,7},{10,8},{11,9},{8,1... | collective-permute-start | bytes 98312 | tf_op jit(solution)/shard_map/ppermute | solution.py:53
  55.1 3.2 %collective-permute-start.8 = (f32[16,4,128]{2,1,0:T(4,128)}, f32[16,4,128]{2,1,0:T(4,128)S(1)}, u32[]{:S(2)}, u32[]{:S(2)}) collective-permute-start(f32[16,4,128]{2,1,0:T(4,128)} %get-tuple-element.16.refs_3_), channel_id=1, source_target_pairs={{1,0},{0,1},{3,2},{2,3},{5,4},{4,5},{7,6},{6,7},{9,8},{8,9},{11,10... | collective-permute-start | bytes 98312 | tf_op jit(solution)/shard_map/ppermute | solution.py:53
  56.7 1.5 %copy-start.15 = (f32[16,4,128]{2,1,0:T(4,128)}, f32[16,4,128]{2,1,0:T(4,128)S(1)}, u32[]{:S(2)}) copy-start(f32[16,4,128]{2,1,0:T(4,128)S(1)} %collective-permute-done.6.refs_4_) | copy-start | bytes 98308
  58.3 0.6 copy-start.17
  58.3 0.6 copy-start.19
  72.8 4.1 %collective-permute-start.10 = (f32[16,4,128]{2,1,0:T(4,128)}, f32[16,4,128]{2,1,0:T(4,128)S(1)}, u32[]{:S(2)}, u32[]{:S(2)}) collective-permute-start(f32[16,4,128]{2,1,0:T(4,128)} %get-tuple-element.19.refs_3_), channel_id=1, source_target_pairs={{2,0},{3,1},{0,2},{1,3},{6,4},{7,5},{4,6},{5,7},{10,8},{11,9},{8,1... | collective-permute-start | bytes 98312 | tf_op jit(solution)/shard_map/ppermute | solution.py:53
  73.7 3.1 %collective-permute-start.11 = (f32[16,4,128]{2,1,0:T(4,128)}, f32[16,4,128]{2,1,0:T(4,128)S(1)}, u32[]{:S(2)}, u32[]{:S(2)}) collective-permute-start(f32[16,4,128]{2,1,0:T(4,128)} %get-tuple-element.19.refs_3_), channel_id=1, source_target_pairs={{1,0},{0,1},{3,2},{2,3},{5,4},{4,5},{7,6},{6,7},{9,8},{8,9},{11,10... | collective-permute-start | bytes 98312 | tf_op jit(solution)/shard_map/ppermute | solution.py:53
  73.7 3.6 %collective-permute-start.9 = (f32[16,4,128]{2,1,0:T(4,128)}, f32[16,4,128]{2,1,0:T(4,128)S(1)}, u32[]{:S(2)}, u32[]{:S(2)}) collective-permute-start(f32[16,4,128]{2,1,0:T(4,128)} %get-tuple-element.19.refs_3_), channel_id=1, source_target_pairs={{3,0},{2,1},{1,2},{0,3},{7,4},{6,5},{5,6},{4,7},{11,8},{10,9},{9,1... | collective-permute-start | bytes 98312 | tf_op jit(solution)/shard_map/ppermute | solution.py:53
  76.9 0.6 copy-start.14
  76.9 0.6 copy-start.16
  77.3 0.6 copy-start.18
  91.8 3.6 %collective-permute-start.12 = (f32[16,4,128]{2,1,0:T(4,128)}, f32[16,4,128]{2,1,0:T(4,128)S(1)}, u32[]{:S(2)}, u32[]{:S(2)}) collective-permute-start(f32[16,4,128]{2,1,0:T(4,128)} %get-tuple-element.22.refs_3_), channel_id=1, source_target_pairs={{3,0},{2,1},{1,2},{0,3},{7,4},{6,5},{5,6},{4,7},{11,8},{10,9},{9,1... | collective-permute-start | bytes 98312 | tf_op jit(solution)/shard_map/ppermute | solution.py:53
  92.9 4.1 %collective-permute-start.13 = (f32[16,4,128]{2,1,0:T(4,128)}, f32[16,4,128]{2,1,0:T(4,128)S(1)}, u32[]{:S(2)}, u32[]{:S(2)}) collective-permute-start(f32[16,4,128]{2,1,0:T(4,128)} %get-tuple-element.22.refs_3_), channel_id=1, source_target_pairs={{2,0},{3,1},{0,2},{1,3},{6,4},{7,5},{4,6},{5,7},{10,8},{11,9},{8,1... | collective-permute-start | bytes 98312 | tf_op jit(solution)/shard_map/ppermute | solution.py:53
  93.9 3.1 %collective-permute-start.14 = (f32[16,4,128]{2,1,0:T(4,128)}, f32[16,4,128]{2,1,0:T(4,128)S(1)}, u32[]{:S(2)}, u32[]{:S(2)}) collective-permute-start(f32[16,4,128]{2,1,0:T(4,128)} %get-tuple-element.22.refs_3_), channel_id=1, source_target_pairs={{1,0},{0,1},{3,2},{2,3},{5,4},{4,5},{7,6},{6,7},{9,8},{8,9},{11,10... | collective-permute-start | bytes 98312 | tf_op jit(solution)/shard_map/ppermute | solution.py:53
  95.3 1.7 %copy-start.10 = (f32[16,4,128]{2,1,0:T(4,128)}, f32[16,4,128]{2,1,0:T(4,128)S(1)}, u32[]{:S(2)}) copy-start(f32[16,4,128]{2,1,0:T(4,128)S(1)} %collective-permute-done.12.refs_4_) | copy-start | bytes 98308
  97.1 0.6 copy-start.11
  97.1 0.6 copy-start.13
  111.6 2.7 %copy-start.5 = (f32[16,4,128]{2,1,0:T(4,128)S(1)}, f32[16,4,128]{2,1,0:T(4,128)}, u32[]{:S(2)}) copy-start(f32[16,4,128]{2,1,0:T(4,128)} %copy-done.4) | copy-start | bytes 98308
  111.6 2.7 %copy-start.6 = (f32[16,4,128]{2,1,0:T(4,128)S(1)}, f32[16,4,128]{2,1,0:T(4,128)}, u32[]{:S(2)}) copy-start(f32[16,4,128]{2,1,0:T(4,128)} %get-tuple-element.25) | copy-start | bytes 98308
  112.4 1.9 %copy-start.25 = (f32[2,4,8,128]{3,2,1,0:T(8,128)S(1)}, f32[2,4,8,128]{3,2,1,0:T(8,128)}, u32[]{:S(2)}) copy-start(f32[2,4,8,128]{3,2,1,0:T(8,128)} %get-tuple-element.27) | copy-start | bytes 98308
  112.4 3.4 %collective-permute-start.15 = (f32[8,128]{1,0:T(8,128)S(1)}, f32[8,128]{1,0:T(8,128)S(1)}, u32[]{:S(2)}, u32[]{:S(2)}) collective-permute-start(f32[8,128]{1,0:T(8,128)S(1)} %slice_bitcast_fusion.1), channel_id=1, source_target_pairs={{3,0},{2,1},{1,2},{0,3},{7,4},{6,5},{5,6},{4,7},{11,8},{10,9},{9,1... | collective-permute-start | bytes 12296 | tf_op jit(solution)/shard_map/ppermute | solution.py:53
  112.4 3.7 %collective-permute-start.16 = (f32[8,128]{1,0:T(8,128)S(1)}, f32[8,128]{1,0:T(8,128)S(1)}, u32[]{:S(2)}, u32[]{:S(2)}) collective-permute-start(f32[8,128]{1,0:T(8,128)S(1)} %slice_bitcast_fusion.1), channel_id=1, source_target_pairs={{2,0},{3,1},{0,2},{1,3},{6,4},{7,5},{4,6},{5,7},{10,8},{11,9},{8,1... | collective-permute-start | bytes 12296 | tf_op jit(solution)/shard_map/ppermute | solution.py:53
  113.5 2.6 %collective-permute-start.17 = (f32[8,128]{1,0:T(8,128)S(1)}, f32[8,128]{1,0:T(8,128)S(1)}, u32[]{:S(2)}, u32[]{:S(2)}) collective-permute-start(f32[8,128]{1,0:T(8,128)S(1)} %slice_bitcast_fusion.1), channel_id=1, source_target_pairs={{1,0},{0,1},{3,2},{2,3},{5,4},{4,5},{7,6},{6,7},{9,8},{8,9},{11,10... | collective-permute-start | bytes 12296 | tf_op jit(solution)/shard_map/ppermute | solution.py:53
  114.4 0.8 copy-start.20

commit v2 on v1

--- a/solution.py
+++ b/solution.py
@@ -22,7 +22,6 @@
 MIDDLE_Z = 1.0
 REACH = 1.49
 FAR = 2.0**126
-GROUP = 9
 ROWS = 16
 
 X, Y, Z, LAM, CHG, STR, GRP, SIT = range(8)
@@ -95,42 +94,112 @@
     return angles + step_size * speeds, speeds
 
 
+def lane_column(row, first, sub_iota):
+    lane = lax.broadcasted_iota(jnp.int32, sub_iota.shape, 1)
+    hit = lane == lax.broadcasted_iota(jnp.int32, sub_iota.shape, 0) + first
+    return jnp.broadcast_to(
+        jnp.sum(jnp.where(hit, row, 0.0), axis=1, keepdims=True), sub_iota.shape
+    )
+
+
+def noise_table(anoise_ref, moment, sub_iota):
+    tables = []
+    for site in range(NSITE):
+        table = jnp.zeros_like(sub_iota)
+        for sub in range(NSUB):
+            table = jnp.where(sub_iota == float(sub), anoise_ref[0, moment, site, sub], table)
+        tables.append(table)
+    return jnp.stack(tables)
+
+
+def packed_totals(blocks, sub_iota):
+    packed = blocks[0]
+    for block in blocks[1:]:
+        packed = packed + block
+    return packed
+
+
 def step_kernel(cfg, moment, *refs):
     nb = cfg["blocks"]
-    tiles, pool = cfg["tiles"], cfg["pool"]
     lanes = cfg["lanes"]
-    count_ref, part_ref, off_ref = refs[:3]
-    refs = refs[1:]
-    coord_refs = refs[2 : 2 + nb]
-    stat_refs = refs[2 + nb : 2 + 2 * nb]
-    tot_ref, vel_ref, ang_ref, noise_ref, anoise_ref, inv_ref = refs[2 + 2 * nb : 8 + 2 * nb]
-    pay_ref, velo_ref, ango_ref = refs[8 + 2 * nb : 11 + 2 * nb]
-    pool_ref, col_ref, fcol_ref, sum_ref, feat_ref, wide_ref, rhs_ref, coef_ref = refs[11 + 2 * nb :]
-
-    angles, aspeeds = ang_ref[0], ang_ref[1]
-    if moment > 0:
+    refs = list(refs)
+
+    def take(n):
+        taken, refs[:n] = refs[:n], []
+        return taken
+
+    part_ref, at_ref, anoise_ref = take(3)
+    coord_refs = take(nb)
+    (stat_ref,) = take(1) if moment > 0 else (None,)
+    (tot_ref,) = take(1) if moment > 0 and not cfg["covered"] else (None,)
+    vel_ref, noise_ref, inv_ref = take(3)
+    (ang_ref,) = take(1) if moment > 0 else (None,)
+    last = moment == STEPS - 1
+    (start_ref,) = take(1) if last else (None,)
+    (out_ref,) = take(1)
+    velo_ref, ango_ref = take(2)
+    (stato_ref,) = take(1) if moment == 0 else (None,)
+    (sumo_ref,) = take(1) if last else (None,)
+    pool_ref, col_ref, fcol_ref, sum_ref, feat_ref, wide_ref, rhs_ref, coef_ref, off_ref = take(9)
+
+    sub_iota = lax.broadcasted_iota(jnp.int32, (NSUB, lanes), 0).astype(jnp.float32)
+    if moment == 0:
+        row = coord_refs[0][0, 3:4, :]
+        angles, aspeeds = (
+            jnp.stack(
+                [
+                    lane_column(row, (kind * NSITE + site) * NSUB, sub_iota)
+                    for site in range(NSITE)
+                ]
+            )
+            for kind in range(2)
+        )
+    else:
+        angles, aspeeds = ang_ref[0], ang_ref[1]
         if cfg["covered"]:
-            packed = coord_refs[0][0:NSUB, 3, :]
-            for ref in coord_refs[1:]:
-                packed = packed + ref[0:NSUB, 3, :]
+            packed = packed_totals([ref[0:NSUB, 3, :] for ref in coord_refs], sub_iota)
         else:
             packed = tot_ref[...]
         angles, aspeeds = angle_step(
-            angles, aspeeds, packed, anoise_ref[moment - 1], cfg["angle_mass"]
+            angles, aspeeds, packed, noise_table(anoise_ref, moment - 1, sub_iota),
+            cfg["angle_mass"],
         )
     ango_ref[0] = angles
     ango_ref[1] = aspeeds
     lambdas = softmax_angles(angles)
 
-    sub_iota = lax.broadcasted_iota(jnp.int32, (NSUB, lanes), 0).astype(jnp.float32)
+    def line(axis, rows, count):
+        at = at_ref[axis]
+        middle = at.astype(jnp.float32) * rows + 0.5 * rows
+        shifts, cells = [], []
+        for ring in range(rows + 2):
+            turn = 0.0
+            if ring == 0:
+                turn = jnp.where(at == 0, -float(rows * count), 0.0)
+            if ring == rows + 1:
+                turn = jnp.where(at == count - 1, float(rows * count), 0.0)
+            shifts.append(turn - middle)
+            cells.append(turn - middle - (ring - 0.5 - 0.5 * rows))
+        return shifts, cells
+
+    shift_x, cell_x = line(0, cfg["rows_x"], cfg["count_x"])
+    shift_y, cell_y = line(1, cfg["rows_y"], cfg["count_y"])
     worst = jnp.zeros((3, lanes), jnp.float32)
     row3 = lax.broadcasted_iota(jnp.int32, (3, lanes), 0)
     for index, (block, tile) in enumerate(cfg["sources"]):
-        stat = stat_refs[block][tile]
-        cell = jnp.where(row3 == 0, off_ref[2, index], off_ref[3, index])
+        pi, pj = index // (cfg["rows_y"] + 2), index % (cfg["rows_y"] + 2)
+        off_ref[0, index] = shift_x[pi]
+        off_ref[1, index] = shift_y[pj]
+        if moment == 0:
+            stat = coord_refs[block][tile, 4:8, :]
+            stato_ref[index] = stat
+        else:
+            stat = stat_ref[index]
+        cell = jnp.where(row3 == 0, cell_x[pi], cell_y[pj])
         cell = jnp.where(row3 == 2, -MIDDLE_Z, cell)
-        worst = jnp.maximum(worst, jnp.abs(coord_refs[block][tile, 0:3, :] + cell))
-        pool_ref[index, 0:3, :] = coord_refs[block][tile, 0:3, :]
+        coords = coord_refs[block][tile, 0:3, :]
+        worst = jnp.maximum(worst, jnp.abs(coords + cell))
+        pool_ref[index, 0:3, :] = coords
         pool_ref[index, 4:8, :] = stat
         group = stat[2:3, :]
         lam = jnp.zeros((NSUB, lanes), jnp.float32)
@@ -142,22 +211,33 @@
     stray = jnp.max(worst * jnp.where(row3 == 2, 0.5, 1.0))
     sum_ref[...] = jnp.zeros_like(sum_ref)
     fcol_ref[...] = jnp.zeros_like(fcol_ref)
-    ins = (vel_ref, noise_ref, inv_ref)
-    outs = (pay_ref, velo_ref, sum_ref)
+    ins = (vel_ref, noise_ref, inv_ref, start_ref)
+    outs = (out_ref, velo_ref, sum_ref)
     near = cfg["roomy"] & (stray < REACH)
 
     @pl.when(near)
     def _():
         near_forces(
-            cfg, lambdas, count_ref, part_ref, off_ref, pool_ref, feat_ref, wide_ref, rhs_ref,
+            cfg, lambdas, part_ref, off_ref, pool_ref, feat_ref, wide_ref, rhs_ref,
             coef_ref, ins, outs, sub_iota,
         )
 
     @pl.when(jnp.logical_not(near))
     def _():
-        any_forces(cfg, count_ref, part_ref, pool_ref, col_ref, fcol_ref, ins, outs, sub_iota)
-
-    pay_sums(cfg, pay_ref, sum_ref)
+        any_forces(cfg, part_ref, pool_ref, col_ref, fcol_ref, ins, outs, sub_iota)
+
+    packed = pack_sums(cfg, sum_ref)
+    if last:
+        sumo_ref[...] = packed
+    else:
+        for tile in range(cfg["tiles"]):
+            out_ref[tile, 3:4, :] = (
+                packed[tile : tile + 1, :] if tile < NSUB else jnp.zeros((1, lanes), jnp.float32)
+            )
+
+
+def part_of(part_ref, cfg, tile, k):
+    return part_ref[tile // cfg["rows_y"], tile % cfg["rows_y"], k]
 
 
 def split3(value):
@@ -175,7 +255,7 @@
 
 
 def near_forces(
-    cfg, lambdas, count_ref, part_ref, off_ref, pool_ref, feat_ref, wide_ref, rhs_ref,
+    cfg, lambdas, part_ref, off_ref, pool_ref, feat_ref, wide_ref, rhs_ref,
     coef_ref, ins, outs, sub_iota,
 ):
     lanes = cfg["lanes"]
@@ -265,7 +345,8 @@
             ).astype(jnp.bfloat16)
 
         def some_partners(k, sums):
-            indices = [part_ref[tile, GROUP * k + u] for u in range(GROUP)]
+            indices = [part_of(part_ref, cfg, tile, k + u) for u in range(cfg["slots"])]
+            indices = [jnp.where(index < 0, cfg["pool"], index) for index in indices]
             outs = [table_dot(feat_ref[index], rhs_ref) for index in indices]
             moments, fd = sums
             for index, out in zip(indices, outs):
@@ -291,10 +372,7 @@
                 )
             return moments, fd
 
-        groups = (count_ref[tile] + GROUP - 1) // GROUP
-        moments, fd = lax.fori_loop(
-            0, groups, some_partners, (jnp.zeros((32, lanes), jnp.float32), nothing)
-        )
+        moments, fd = some_partners(0, (jnp.zeros((32, lanes), jnp.float32), nothing))
         moments = moments[0:8] + moments[8:16] + moments[16:24]
         fd = jnp.sum(fd, axis=0, keepdims=True)
         forces = moved[0:3, :] * moments[6:7, :] - moments[0:3, :]
@@ -309,7 +387,7 @@
     lax.fori_loop(0, cfg["tiles"], one_tile, 0)
 
 
-def any_forces(cfg, count_ref, part_ref, pool_ref, col_ref, fcol_ref, ins, outs, sub_iota):
+def any_forces(cfg, part_ref, pool_ref, col_ref, fcol_ref, ins, outs, sub_iota):
     tiles, lanes = cfg["tiles"], cfg["lanes"]
     chunk = 32
 
@@ -317,7 +395,9 @@
         own = (tile // cfg["rows_y"] + 1) * (cfg["rows_y"] + 2) + tile % cfg["rows_y"] + 1
         block = pool_ref[own]
         col_ref[...] = block.T
-        count = count_ref[tile]
+        count = jnp.int32(0)
+        for k in range(cfg["slots"]):
+            count += (part_of(part_ref, cfg, tile, k) >= 0).astype(jnp.int32)
 
         def one_chunk(c, carry):
             start = pl.multiple_of(c * chunk, chunk)
@@ -327,7 +407,7 @@
 
             def one_partner(k, sums):
                 fx, fy, fz, fd = sums
-                index = part_ref[tile, k]
+                index = part_of(part_ref, cfg, tile, k)
                 other = pool_ref[index]
 
                 def own_col(row):
@@ -377,23 +457,29 @@
 
 
 def finish_tile(cfg, tile, forces, drive, block, ins, outs, sub_iota):
-    vel_ref, noise_ref, inv_ref = ins
-    pay_ref, velo_ref, sum_ref = outs
+    vel_ref, noise_ref, inv_ref, start_ref = ins
+    out_ref, velo_ref, sum_ref = outs
+    i, j = tile // cfg["rows_y"], tile % cfg["rows_y"]
     damping = math.exp(-friction_rate * step_size)
-    inverse = inv_ref[tile]
+    inverse = inv_ref[i, pl.ds(j, 1), :]
     speeds = (
         damping * vel_ref[tile, 0:3, :]
         + step_size * forces * inverse
-        + jnp.sqrt((1.0 - damping**2) * inverse) * noise_ref[0, tile]
-    )
-    velo_ref[tile] = speeds
-    pay_ref[tile, 0:3, :] = block[0:3, :] + step_size * speeds
+        + jnp.sqrt((1.0 - damping**2) * inverse) * noise_ref[0, 0, i, j]
+    )
+    coords = block[0:3, :] + step_size * speeds
+    if start_ref is None:
+        velo_ref[tile, 0:3, :] = speeds
+        out_ref[tile, 0:3, :] = coords
+    else:
+        velo_ref[0, i, j] = speeds
+        out_ref[0, i, j] = coords - start_ref[tile, 0:3, :]
     group = block[GRP : GRP + 1, :]
     for site in range(NSITE):
         sum_ref[site] += jnp.where(group == sub_iota + float(site * NSUB), drive, 0.0)
 
 
-def pay_sums(cfg, pay_ref, sum_ref):
+def pack_sums(cfg, sum_ref):
     lanes = cfg["lanes"]
     share = lanes // NSITE
     lane_site = lax.broadcasted_iota(jnp.int32, (NSUB, lanes), 1) // share
@@ -405,51 +491,128 @@
             width //= 2
             folded = folded + pltpu.roll(folded, width, 1)
         packed = packed + jnp.where(lane_site == site, folded, 0.0)
-    for sub in range(cfg["tiles"]):
-        pay_ref[sub, 3:4, :] = (
-            packed[sub : sub + 1, :] if sub < NSUB else jnp.zeros((1, lanes), jnp.float32)
-        )
-
-
-def step_call(cfg, moment, count, parts, places, blocks, stats, totals, vel, ang, noise, anoise, inverse):
-    tiles, lanes = cfg["tiles"], cfg["lanes"]
-    nb = cfg["blocks"]
+    return packed
+
+
+def step_call(cfg, moment, parts, at, anoise, blocks, stat, totals, vel, noise, inverse, ang, start):
+    tiles, lanes, pool = cfg["tiles"], cfg["lanes"], cfg["pool"]
+    rows_x, rows_y = cfg["rows_x"], cfg["rows_y"]
+    last = moment == STEPS - 1
     vmem = pl.BlockSpec(memory_space=pltpu.VMEM)
     smem = pl.BlockSpec(memory_space=pltpu.SMEM)
-    noise_spec = pl.BlockSpec((1, tiles, 3, lanes), lambda i: (moment, 0, 0, 0))
-
+    noise_spec = pl.BlockSpec(
+        (1, 1, rows_x, rows_y, 3, lanes), lambda i: (0, moment, 0, 0, 0, 0)
+    )
+    args = [(parts, smem), (at, smem), (anoise, smem)] + [(block, vmem) for block in blocks]
+    if moment > 0:
+        args.append((stat, vmem))
+    if totals is not None:
+        args.append((totals, vmem))
+    args += [(vel, vmem), (noise, noise_spec), (inverse, vmem)]
+    if moment > 0:
+        args.append((ang, vmem))
+    if last:
+        args.append((start, vmem))
+    whole = (1, rows_x, rows_y, 3, lanes)
+    shapes = [whole, whole] if last else [(tiles, 4, lanes), (tiles, 4, lanes)]
+    shapes.append((2, NSITE, NSUB, lanes))
+    if moment == 0:
+        shapes.append((pool, 4, lanes))
+    if last:
+        shapes.append((NSUB, lanes))
+    depth = cfg["depth"]
     return pl.pallas_call(
         functools.partial(step_kernel, cfg, moment),
         grid=(1,),
-        out_shape=(
-            jax.ShapeDtypeStruct((tiles, 4, lanes), jnp.float32),
-            jax.ShapeDtypeStruct((tiles, 3, lanes), jnp.float32),
-            jax.ShapeDtypeStruct((2, NSITE, NSUB, lanes), jnp.float32),
-        ),
-        in_specs=[smem, smem, smem] + [vmem] * (2 * nb + 3) + [noise_spec, vmem, vmem],
-        out_specs=(vmem, vmem, vmem),
+        out_shape=tuple(jax.ShapeDtypeStruct(shape, jnp.float32) for shape in shapes),
+        in_specs=[spec for _, spec in args],
+        out_specs=(vmem,) * len(shapes),
         scratch_shapes=[
-            pltpu.VMEM((cfg["pool"], 8, lanes), jnp.float32),
+            pltpu.VMEM((pool, 8, lanes), jnp.float32),
             pltpu.VMEM((lanes, 8), jnp.float32),
             pltpu.VMEM((lanes, 8), jnp.float32),
             pltpu.VMEM((NSITE, NSUB, lanes), jnp.float32),
-            pltpu.VMEM((cfg["pool"] + 1, lanes, cfg["depth"]), jnp.bfloat16),
-            pltpu.VMEM((cfg["pool"] + 1, lanes, lanes), jnp.float32),
-            pltpu.VMEM((4, cfg["depth"], lanes), jnp.bfloat16),
-            pltpu.VMEM((cfg["pool"] + 1, 32, 2 * lanes), jnp.bfloat16),
+            pltpu.VMEM((pool + 1, lanes, depth), jnp.bfloat16),
+            pltpu.VMEM((pool + 1, lanes, lanes), jnp.float32),
+            pltpu.VMEM((4, depth, lanes), jnp.bfloat16),
+            pltpu.VMEM((pool + 1, 32, 2 * lanes), jnp.bfloat16),
+            pltpu.SMEM((2, pool), jnp.float32),
         ],
         name="langevin_step",
-    )(count, parts, places, *blocks, *stats, totals, vel, ang, noise, anoise, inverse)
-
-
-def make_cfg(rows_x, rows_y, lanes, count_x, count_y, offsets):
+    )(*[value for value, _ in args])
+
+
+def angle_kernel(cfg, *refs):
+    anoise_ref, ang_ref = refs[:2]
+    tot_refs, (theta_ref, speed_ref) = refs[2:-2], refs[-2:]
+    lanes = cfg["lanes"]
+    sub_iota = lax.broadcasted_iota(jnp.int32, (NSUB, lanes), 0).astype(jnp.float32)
+    packed = packed_totals([ref[...] for ref in tot_refs], sub_iota)
+    results = angle_step(
+        ang_ref[0], ang_ref[1], packed, noise_table(anoise_ref, STEPS - 1, sub_iota),
+        cfg["angle_mass"],
+    )
+    hit = lax.broadcasted_iota(jnp.int32, (NSUB, lanes), 1) == lax.broadcasted_iota(
+        jnp.int32, (NSUB, lanes), 0
+    )
+    for ref, result in zip((theta_ref, speed_ref), results):
+        for site in range(NSITE):
+            row = jnp.sum(jnp.where(hit, result[site], 0.0), axis=0, keepdims=True)
+            ref[0, site : site + 1, :] = row[:, 0:NSUB]
+
+
+def angle_call(cfg, anoise, ang, totals):
+    vmem = pl.BlockSpec(memory_space=pltpu.VMEM)
+    shape = jax.ShapeDtypeStruct((1, NSITE, NSUB), jnp.float32)
+    return pl.pallas_call(
+        functools.partial(angle_kernel, cfg),
+        out_shape=(shape, shape),
+        in_specs=[pl.BlockSpec(memory_space=pltpu.SMEM)] + [vmem] * (1 + len(totals)),
+        out_specs=(vmem, vmem),
+        name="last_angles",
+    )(anoise, ang, *totals)
+
+
+def clone(message, source_slot):
+    peers = lax.axis_size("walker")
+    me = lax.axis_index("walker")
+    width = 2 if peers % 2 == 0 else 1
+    sets = peers // width
+    mine = message
+    if width == 2:
+        other = lax.ppermute(message, "walker", [(w, w ^ 1) for w in range(peers)])
+        odd = me % 2 == 1
+    else:
+        other, odd = message, me < 0
+
+    def held(slot):
+        return jnp.where((slot % 2 == 1) == odd, mine, other) if width == 2 else mine
+
+    source = source_slot[me]
+    result = held(source)
+    hop = (me // width - source // width) % sets
+    for k in range(1, sets):
+        target = (me + k * width) % peers
+        sent = held(source_slot[target])
+        got = lax.ppermute(
+            sent, "walker", [(w, (w + k * width) % peers) for w in range(peers)]
+        )
+        result = jnp.where(hop == k, got, result)
+    return result
+
+
+def make_cfg(rows_x, rows_y, lanes, count_x, count_y, slots, offsets):
     tiles = rows_x * rows_y
     return dict(
         blocks=1 + len(offsets),
         covered=1 + len(offsets) == count_x * count_y,
         tiles=tiles,
         lanes=lanes,
+        rows_x=rows_x,
         rows_y=rows_y,
+        count_x=count_x,
+        count_y=count_y,
+        slots=slots,
         pool=(rows_x + 2) * (rows_y + 2),
         sources=pool_sources(rows_x, rows_y, count_x, count_y, offsets),
         depth=128,
@@ -477,11 +640,10 @@
     partners,
 ):
     count_x, count_y = lax.axis_size("gx"), lax.axis_size("gy")
-    peers = lax.axis_size("walker")
     rows_x, rows_y, lanes = charges.shape
     tiles = rows_x * rows_y
     offsets = neighbour_offsets(count_x, count_y)
-    cfg = make_cfg(rows_x, rows_y, lanes, count_x, count_y, offsets)
+    cfg = make_cfg(rows_x, rows_y, lanes, count_x, count_y, partners.shape[-1], offsets)
 
     def gather_blocks(value):
         return [value] + [shifted(value, offset, count_x, count_y) for offset in offsets]
@@ -492,78 +654,43 @@
     stat = jnp.stack(
         [charges, strengths, groups.astype(jnp.float32), sites.astype(jnp.float32)], axis=2
     ).reshape(tiles, 4, lanes)
-    stats = gather_blocks(stat)
-
-    mine = source_slot[lax.axis_index("walker")]
+
     angles = jnp.stack([lambda_theta[0], theta_velocity[0]]).reshape(1, 2 * NSITE * NSUB)
     angles = jnp.pad(angles, ((0, 0), (0, lanes - 2 * NSITE * NSUB)))
     extra = jnp.broadcast_to(angles[:, None, :], (tiles, 1, lanes))
-    first = jnp.concatenate([positions.reshape(tiles, 3, lanes), extra], axis=1)
-    second = velocities.reshape(tiles, 3, lanes)
-
-    def picked(value):
-        everyone = lax.all_to_all(
-            jnp.broadcast_to(value, (peers,) + value.shape), "walker", 0, 0, tiled=True
-        )
-        return lax.dynamic_index_in_dim(everyone, mine, 0, keepdims=False)
-
-    start = picked(first)
-    vel = picked(second)
-    ang = start[0, 3, : 2 * NSITE * NSUB].reshape(2, NSITE, NSUB, 1)
-    ang = jnp.broadcast_to(ang, (2, NSITE, NSUB, lanes))
-    anoise = jnp.broadcast_to(theta_noise[0][..., None], (STEPS, NSITE, NSUB, lanes))
-    noise = atom_noise.reshape(STEPS, tiles, 3, lanes)
-    inverse = inverse_mass.reshape(tiles, 1, lanes)
-    parts = partners.reshape(tiles, -1)
-    count = jnp.sum((parts >= 0).astype(jnp.int32), axis=1)
-    parts = jnp.where(parts < 0, cfg["pool"], parts)
-    parts = jnp.pad(
-        parts, ((0, 0), (0, -parts.shape[1] % GROUP)), constant_values=cfg["pool"]
-    )
-
-    def line(axis, rows, count):
-        at = lax.axis_index(axis)
-        ring = jnp.arange(rows + 2)
-        turn = jnp.where(ring == 0, jnp.where(at == 0, -1.0, 0.0), 0.0)
-        turn = jnp.where(ring == rows + 1, jnp.where(at == count - 1, 1.0, 0.0), turn)
-        middle = at.astype(jnp.float32) * rows + 0.5 * rows
-        shift = turn * (rows * count) - middle
-        return shift, shift - (ring.astype(jnp.float32) - 0.5 - 0.5 * rows)
-
-    shift_x, cell_x = line("gx", rows_x, count_x)
-    shift_y, cell_y = line("gy", rows_y, count_y)
-    places = jnp.stack(
+    message = jnp.concatenate(
         [
-            jnp.broadcast_to(value, (rows_x + 2, rows_y + 2)).reshape(-1)
-            for value in (shift_x[:, None], shift_y, cell_x[:, None], cell_y)
-        ]
-    )
-
-    pay = start
+            positions.reshape(tiles, 3, lanes),
+            extra,
+            velocities.reshape(tiles, 3, lanes),
+            jnp.zeros((tiles, 1, lanes), jnp.float32),
+        ],
+        axis=1,
+    )
+    start = clone(message, source_slot)
+    vel = start[:, 4:8, :]
+    at = jnp.stack([lax.axis_index("gx"), lax.axis_index("gy")])
+    pay = jnp.concatenate([start[:, 0:4, :], stat], axis=1)
+    first = pay
+    ang = pool_stat = None
     for moment in range(STEPS):
-        blocks = gather_blocks(pay)
+        totals = None
         if moment > 0 and not cfg["covered"]:
             totals = lax.psum(pay[:NSUB, 3, :], ("gx", "gy"))
-        else:
-            totals = jnp.zeros((NSUB, lanes), jnp.float32)
-        pay, vel, ang = step_call(
-            cfg, moment, count, parts, places, blocks, stats, totals, vel, ang, noise, anoise, inverse
+        outs = step_call(
+            cfg, moment, partners, at, theta_noise, gather_blocks(pay), pool_stat, totals, vel,
+            atom_noise, inverse_mass, ang, first,
         )
-    packed = pay[:NSUB, 3, :]
+        pay, vel, ang = outs[:3]
+        if moment == 0:
+            pool_stat = outs[3]
+    packed = outs[3]
     if cfg["covered"]:
-        totals = packed
-        for offset in offsets:
-            totals = totals + shifted(packed, offset, count_x, count_y)
+        totals = gather_blocks(packed)
     else:
-        totals = lax.psum(packed, ("gx", "gy"))
-    angles, aspeeds = angle_step(ang[0], ang[1], totals, anoise[STEPS - 1], cfg["angle_mass"])
-    displacement = (pay[:, 0:3, :] - start[:, 0:3, :]).reshape(positions.shape)
-    return (
-        displacement,
-        vel.reshape(velocities.shape),
-        angles[None, :, :, 0],
-        aspeeds[None, :, :, 0],
-    )
+        totals = [lax.psum(packed, ("gx", "gy"))]
+    theta, theta_speed = angle_call(cfg, theta_noise, ang, totals)
+    return pay, vel, theta, theta_speed
 
 
 def solution(mesh):

time: 118 us -> 108 us (0.915)
  between operations: 2.87 us -> 9.32 us
  waiting for transfers between devices: 19.3 us -> 13 us
  starting transfers between devices: 22.8 us -> 18 us
  local copies, waits for them, and re-layouts: 13.7 us -> 9.31 us
  other arithmetic: 3.36 us -> 1.41 us
    all_to_all x2 -> x0, starting transfers between devices: 9.7 us -> none  [picked(): lax.all_to_all(jnp.broadcast_to(value, (peers,) + value.shape), 'walker',...]
    ppermute x0 -> x4, starting transfers between devices: none -> 8.56 us  [the longest x3 5.57 us: clone(): lax.ppermute(sent, 'walker', [(w, (w + k * width) % peers) for w in range...]
    all_to_all x2 -> x0, waiting for transfers between devices: 8.29 us -> none  [picked(): lax.all_to_all(jnp.broadcast_to(value, (peers,) + value.shape), 'walker',...]
    ppermute x18 -> x15, starting transfers between devices: 13.1 us -> 9.4 us  [shifted(): return lax.ppermute(value, ('gx', 'gy'), pairs)]
    broadcast_in_dim x9 -> x0, local copies, waits for them, and re-layouts: 3.05 us -> none  [the longest x2 1.42 us: picked(): jnp.broadcast_to(value, (peers,) + value.shape)]
    ppermute x18 -> x15, waiting for transfers between devices: 11 us -> 13 us  [shifted(): return lax.ppermute(value, ('gx', 'gy'), pairs)]
    pallas_call x0 -> x1, Pallas kernels: none -> 1.62 us  [angle_call(): pl.pallas_call(functools.partial(angle_kernel, cfg), out_shape=(shape, sh...]
    another operation x9 -> x0, local copies, waits for them, and re-layouts: 1.19 us -> none
  transfers between devices with their start and end apart: 20 -> 19, of which waited for: 11 -> 10; matrix products, arithmetic and copies ran while one was open for 6% -> 4% of each run, Pallas kernels for 0% -> 0%
where the time goes in v2:
time: 108 us; the launch traced here: 107 us
  Pallas kernels  56.4 us (52%)
  starting transfers between devices  18 us (17%)
  waiting for transfers between devices  13 us (12%)
  between operations  9.32 us (9%)
  local copies, waits for them, and re-layouts  9.31 us (9%)
  other arithmetic  1.41 us (1%)
    pallas_call x4, Pallas kernels, step_call(): pl.pallas_call(functools.partial(step_kernel, cfg, moment), grid=(1,), ou...  54.8 us
    ppermute x15, waiting for transfers between devices, shifted(): return lax.ppermute(value, ('gx', 'gy'), pairs)  13 us
    ppermute x15, starting transfers between devices, shifted(): return lax.ppermute(value, ('gx', 'gy'), pairs)  9.4 us
    unnamed x53, local copies, waits for them, and re-layouts  7.85 us
    ppermute x3, starting transfers between devices, clone(): lax.ppermute(sent, 'walker', [(w, (w + k * width) % peers) for w in range...  5.57 us
    ppermute x1, starting transfers between devices, clone(): other = lax.ppermute(message, 'walker', [(w, w ^ 1) for w in range(peers)])  2.99 us
  transfers between devices with their start and end apart: 19, of which 10 were waited for; matrix products, arithmetic and copies ran while one was open for 4% of the time, Pallas kernels for 0%

profile of v2, /device:TPU:0, one launch (start us, length us, event | category | flops | bytes accessed | tf_op | source)
XLA Modules:
  0.0 107.4 jit_solution(5111483175912248985)
XLA Ops:
  0.6 0.7 pad_maximum_fusion
  1.3 0.1 reshape.30
  1.4 0.8 copy.17
  2.2 0.1 pad.8.clone
  2.3 0.1 maximum_maximum_fusion
  2.4 3.0 %collective-permute-start = (f32[16,8,128]{2,1,0:T(8,128)S(1)}, f32[16,8,128]{2,1,0:T(8,128)S(1)}, u32[]{:S(2)}, u32[]{:S(2)}) collective-permute-start(f32[16,8,128]{2,1,0:T(8,128)S(1)} %maximum_maximum_fusion), channel_id=1, source_target_pairs={{0,4},{4,0},{8,12},{12,8},{16,20},{20,16},{24,28},{28,24},{1,5},{5... | collective-permute-start | bytes 196616 | tf_op jit(solution)/shard_map/ppermute | solution.py:583
  5.4 0.7 copy-done.18
  6.0 0.6 fusion.3
  12.5 0.0 collective-permute-done
  12.5 0.0 copy-start.19
  12.5 0.0 copy-start.20
  12.6 0.0 copy-start.1
  12.6 1.6 %collective-permute-start.3 = (f32[16,8,128]{2,1,0:T(8,128)S(1)}, f32[16,8,128]{2,1,0:T(8,128)S(1)}, u32[]{:S(2)}, u32[]{:S(2)}) collective-permute-start(f32[16,8,128]{2,1,0:T(8,128)S(1)} %get-tuple-element.40), channel_id=1, source_target_pairs={{0,8},{4,12},{8,16},{12,20},{16,24},{20,28},{24,0},{28,4},{1,9},{5... | collective-permute-start | bytes 196616 | tf_op jit(solution)/shard_map/ppermute | solution.py:597
  14.2 2.6 %collective-permute-start.2 = (f32[16,8,128]{2,1,0:T(8,128)S(1)}, f32[16,8,128]{2,1,0:T(8,128)S(1)}, u32[]{:S(2)}, u32[]{:S(2)}) collective-permute-start(f32[16,8,128]{2,1,0:T(8,128)S(1)} %get-tuple-element.41), channel_id=1, source_target_pairs={{0,16},{4,20},{8,24},{12,28},{16,0},{20,4},{24,8},{28,12},{1,17},{... | collective-permute-start | bytes 196616 | tf_op jit(solution)/shard_map/ppermute | solution.py:597
  16.8 1.3 %collective-permute-start.1 = (f32[16,8,128]{2,1,0:T(8,128)S(1)}, f32[16,8,128]{2,1,0:T(8,128)S(1)}, u32[]{:S(2)}, u32[]{:S(2)}) collective-permute-start(f32[16,8,128]{2,1,0:T(8,128)S(1)} %get-tuple-element.42), channel_id=1, source_target_pairs={{0,24},{4,28},{8,0},{12,4},{16,8},{20,12},{24,16},{28,20},{1,25},{... | collective-permute-start | bytes 196616 | tf_op jit(solution)/shard_map/ppermute | solution.py:597
  20.8 0.7 copy.19.refs_8_.refs_9_
  21.5 0.0 collective-permute-done.2
  21.6 0.0 copy-start.17
  21.6 0.6 fusion.2
  22.2 0.1 copy-done.17
  22.3 0.6 copy-done.16
  22.9 0.1 concatenate.9.refs_3_.refs_12_
  23.0 0.1 collective-permute-start.6
  23.1 1.6 %collective-permute-start.5 = (f32[16,8,128]{2,1,0:T(8,128)S(1)}, f32[16,8,128]{2,1,0:T(8,128)S(1)}, u32[]{:S(2)}, u32[]{:S(2)}) collective-permute-start(f32[16,8,128]{2,1,0:T(8,128)S(1)} %concatenate.9.refs_3_.refs_12_), channel_id=1, source_target_pairs={{2,0},{3,1},{0,2},{1,3},{6,4},{7,5},{4,6},{5,7},{10,8},{11,9},{8,1... | collective-permute-start | bytes 196616 | tf_op jit(solution)/shard_map/ppermute | solution.py:52
  24.7 0.3 collective-permute-start.4
  24.9 0.6 pad_add_fusion.refs_1_
  25.5 2.1 %collective-permute-done.5.refs_5_ = f32[16,8,128]{2,1,0:T(8,128)S(1)} collective-permute-done((f32[16,8,128]{2,1,0:T(8,128)S(1)}, f32[16,8,128]{2,1,0:T(8,128)S(1)}, u32[]{:S(2)}, u32[]{:S(2)}) %collective-permute-start.5) | collective-permute-done | bytes 65568 | tf_op jit(solution)/shard_map/ppermute | solution.py:52
  27.6 1.1 %collective-permute-done.4.refs_4_ = f32[16,8,128]{2,1,0:T(8,128)S(1)} collective-permute-done((f32[16,8,128]{2,1,0:T(8,128)S(1)}, f32[16,8,128]{2,1,0:T(8,128)S(1)}, u32[]{:S(2)}, u32[]{:S(2)}) %collective-permute-start.4) | collective-permute-done | bytes 65568 | tf_op jit(solution)/shard_map/ppermute | solution.py:52
  28.7 0.6 copy-done.4
  29.3 13.7 %langevin_step.4 = (f32[16,4,128]{2,1,0:T(4,128)}, f32[16,4,128]{2,1,0:T(4,128)}, f32[2,4,8,128]{3,2,1,0:T(8,128)}, f32[36,4,128]{2,1,0:T(4,128)}) custom-call(s32[4,4,9]{2,1,0:T(4,128)} %refs_0_.8, s32[2]{0:T(128)} %pad_add_fusion.refs_1_, f32[1,4,4,8]{3,2,1,0:T(4,128)} %refs_0_.9, f32[16,8,128]{2,1,0:T(8,128)} %copy-done, f32[16,8,128]{2,1,0:T(8,128)} %copy-done.4, ...), custom_call_target="tpu_custom_call" | custom-call | tf_op jit(solution)/shard_map/langevin_step/pallas_call | solution.py:524
  43.0 0.2 collective-permute-start.9
  43.2 1.4 %collective-permute-start.8 = (f32[16,4,128]{2,1,0:T(4,128)}, f32[16,4,128]{2,1,0:T(4,128)S(1)}, u32[]{:S(2)}, u32[]{:S(2)}) collective-permute-start(f32[16,4,128]{2,1,0:T(4,128)} %get-tuple-element.20.refs_3_), channel_id=1, source_target_pairs={{2,0},{3,1},{0,2},{1,3},{6,4},{7,5},{4,6},{5,7},{10,8},{11,9},{8,1... | collective-permute-start | bytes 98312 | tf_op jit(solution)/shard_map/ppermute | solution.py:52
  44.6 0.3 collective-permute-start.7
  44.9 2.4 %collective-permute-done.8.refs_5_ = f32[16,4,128]{2,1,0:T(4,128)S(1)} collective-permute-done((f32[16,4,128]{2,1,0:T(4,128)}, f32[16,4,128]{2,1,0:T(4,128)S(1)}, u32[]{:S(2)}, u32[]{:S(2)}) %collective-permute-start.8) | collective-permute-done | bytes 32800 | tf_op jit(solution)/shard_map/ppermute | solution.py:52
  47.3 1.2 %collective-permute-done.7.refs_4_ = f32[16,4,128]{2,1,0:T(4,128)S(1)} collective-permute-done((f32[16,4,128]{2,1,0:T(4,128)}, f32[16,4,128]{2,1,0:T(4,128)S(1)}, u32[]{:S(2)}, u32[]{:S(2)}) %collective-permute-start.7) | collective-permute-done | bytes 32800 | tf_op jit(solution)/shard_map/ppermute | solution.py:52
  48.5 0.6 copy-done.13
  49.1 13.7 %langevin_step.5 = (f32[16,4,128]{2,1,0:T(4,128)}, f32[16,4,128]{2,1,0:T(4,128)}, f32[2,4,8,128]{3,2,1,0:T(8,128)}) custom-call(s32[4,4,9]{2,1,0:T(4,128)} %refs_0_.8, s32[2]{0:T(128)} %pad_add_fusion.refs_1_, f32[1,4,4,8]{3,2,1,0:T(4,128)} %refs_0_.9, f32[16,4,128]{2,1,0:T(4,128)} %get-tuple-element.20.refs_3_, f32[16,4,128]{2,1,0:T(4,128)} %copy-done.13, ...), custom_call_target="tpu_custom_call" | custom-call | tf_op jit(solution)/shard_map/langevin_step/pallas_call | solution.py:524
  62.8 0.1 collective-permute-start.12
  62.9 0.6 collective-permute-start.11
  63.5 1.1 %collective-permute-start.10 = (f32[16,4,128]{2,1,0:T(4,128)}, f32[16,4,128]{2,1,0:T(4,128)S(1)}, u32[]{:S(2)}, u32[]{:S(2)}) collective-permute-start(f32[16,4,128]{2,1,0:T(4,128)} %get-tuple-element.24.refs_3_), channel_id=1, source_target_pairs={{3,0},{2,1},{1,2},{0,3},{7,4},{6,5},{5,6},{4,7},{11,8},{10,9},{9,1... | collective-permute-start | bytes 98312 | tf_op jit(solution)/shard_map/ppermute | solution.py:52
  64.7 2.7 %collective-permute-done.11.refs_5_ = f32[16,4,128]{2,1,0:T(4,128)S(1)} collective-permute-done((f32[16,4,128]{2,1,0:T(4,128)}, f32[16,4,128]{2,1,0:T(4,128)S(1)}, u32[]{:S(2)}, u32[]{:S(2)}) %collective-permute-start.11) | collective-permute-done | bytes 32800 | tf_op jit(solution)/shard_map/ppermute | solution.py:52
  67.3 0.1 collective-permute-done.10.refs_4_
  67.4 0.5 copy-done.12
  67.9 0.1 copy-done.14
  68.0 13.7 %langevin_step.6 = (f32[16,4,128]{2,1,0:T(4,128)}, f32[16,4,128]{2,1,0:T(4,128)}, f32[2,4,8,128]{3,2,1,0:T(8,128)}) custom-call(s32[4,4,9]{2,1,0:T(4,128)} %refs_0_.8, s32[2]{0:T(128)} %pad_add_fusion.refs_1_, f32[1,4,4,8]{3,2,1,0:T(4,128)} %refs_0_.9, f32[16,4,128]{2,1,0:T(4,128)} %get-tuple-element.24.refs_3_, f32[16,4,128]{2,1,0:T(4,128)} %copy-done.14, ...), custom_call_target="tpu_custom_call" | custom-call | tf_op jit(solution)/shard_map/langevin_step/pallas_call | solution.py:524
  81.7 0.1 collective-permute-start.15
  81.8 1.2 %collective-permute-start.14 = (f32[16,4,128]{2,1,0:T(4,128)}, f32[16,4,128]{2,1,0:T(4,128)S(1)}, u32[]{:S(2)}, u32[]{:S(2)}) collective-permute-start(f32[16,4,128]{2,1,0:T(4,128)} %get-tuple-element.27.refs_3_), channel_id=1, source_target_pairs={{2,0},{3,1},{0,2},{1,3},{6,4},{7,5},{4,6},{5,7},{10,8},{11,9},{8,1... | collective-permute-start | bytes 98312 | tf_op jit(solution)/shard_map/ppermute | solution.py:52
  83.0 0.6 collective-permute-start.13
  83.6 2.3 %collective-permute-done.14.refs_5_ = f32[16,4,128]{2,1,0:T(4,128)S(1)} collective-permute-done((f32[16,4,128]{2,1,0:T(4,128)}, f32[16,4,128]{2,1,0:T(4,128)S(1)}, u32[]{:S(2)}, u32[]{:S(2)}) %collective-permute-start.14) | collective-permute-done | bytes 32800 | tf_op jit(solution)/shard_map/ppermute | solution.py:52
  85.9 0.7 collective-permute-done.13.refs_4_
  86.6 0.6 copy-done.7
  87.2 13.7 %langevin_step.7 = (f32[1,4,4,3,128]{4,3,2,1,0:T(4,128)}, f32[1,4,4,3,128]{4,3,2,1,0:T(4,128)}, f32[2,4,8,128]{3,2,1,0:T(8,128)}, f32[8,128]{1,0:T(8,128)}) custom-call(s32[4,4,9]{2,1,0:T(4,128)} %refs_0_.8, s32[2]{0:T(128)} %pad_add_fusion.refs_1_, f32[1,4,4,8]{3,2,1,0:T(4,128)} %refs_0_.9, f32[16,4,128]{2,1,0:T(4,128)} %get-tuple-element.27.refs_3_, ...), custom_call_target="tpu_custom_call" | custom-call | tf_op jit(solution)/shard_map/langevin_step/pallas_call | solution.py:524
  100.9 0.1 collective-permute-start.18
  101.0 0.9 collective-permute-start.17
  102.0 0.8 collective-permute-start.16
  102.8 1.4 %copy.23 = f32[1,4,4,3,128]{4,2,3,1,0:T(4,128)} copy(f32[1,4,4,3,128]{4,3,2,1,0:T(4,128)} %get-tuple-element.36) | data formatting | bytes 49152
  104.2 0.6 copy.24
  104.8 0.0 collective-permute-done.18.refs_5_
  104.8 0.1 collective-permute-done.17.refs_4_
  104.9 0.3 collective-permute-done.16.refs_3_
  105.2 0.2 copy-done.21
  105.4 0.1 copy-done.22
  105.5 0.3 copy-done.23
  105.8 1.6 %last_angles.1 = (f32[1,4,8]{2,1,0:T(4,128)}, f32[1,4,8]{2,1,0:T(4,128)}) custom-call(f32[1,4,4,8]{3,2,1,0:T(4,128)} %refs_0_.9, f32[2,4,8,128]{3,2,1,0:T(8,128)} %get-tuple-element.32.refs_1_, f32[8,128]{1,0:T(8,128)} %get-tuple-element.33.refs_2_, f32[8,128]{1,0:T(8,128)} %copy-done.23, f32[8,128]{1,0:T(8,128)} %copy-done.22, f32[8,128]{1,0:T(8,128)} %copy-done.21), custom_call_target="tpu_custom_call" | custom-call | tf_op jit(solution)/shard_map/last_angles/pallas_call | solution.py:567
  (45 shorter events, 0.1 us)
Async XLA Ops:
  1.4 0.8 copy-start.15
  2.4 10.1 %collective-permute-start = (f32[16,8,128]{2,1,0:T(8,128)S(1)}, f32[16,8,128]{2,1,0:T(8,128)S(1)}, u32[]{:S(2)}, u32[]{:S(2)}) collective-permute-start(f32[16,8,128]{2,1,0:T(8,128)S(1)} %maximum_maximum_fusion), channel_id=1, source_target_pairs={{0,4},{4,0},{8,12},{12,8},{16,20},{20,16},{24,28},{28,24},{1,5},{5... | collective-permute-start | bytes 196616 | tf_op jit(solution)/shard_map/ppermute | solution.py:583
  5.4 0.7 copy-start.18
  12.5 5.6 %copy-start.19 = (s32[4,4,128]{2,1,0:T(4,128)S(1)}, s32[4,4,128]{2,1,0:T(4,128)}, u32[]{:S(2)}) copy-start(s32[4,4,128]{2,1,0:T(4,128)} %param.23) | copy-start | bytes 24580
  12.5 5.6 %copy-start.20 = (s32[4,4,128]{2,1,0:T(4,128)S(1)}, s32[4,4,128]{2,1,0:T(4,128)}, u32[]{:S(2)}) copy-start(s32[4,4,128]{2,1,0:T(4,128)} %param.24) | copy-start | bytes 24580
  12.6 8.3 %copy-start.1 = (f32[1,4,4,4,3,128]{5,3,4,2,1,0:T(4,128)S(1)}, f32[1,4,4,4,3,128]{5,3,4,2,1,0:T(4,128)}, u32[]{:S(2)}) copy-start(f32[1,4,4,4,3,128]{5,3,4,2,1,0:T(4,128)} %param.18) | copy-start | bytes 294916
  12.6 8.9 %collective-permute-start.3 = (f32[16,8,128]{2,1,0:T(8,128)S(1)}, f32[16,8,128]{2,1,0:T(8,128)S(1)}, u32[]{:S(2)}, u32[]{:S(2)}) collective-permute-start(f32[16,8,128]{2,1,0:T(8,128)S(1)} %get-tuple-element.40), channel_id=1, source_target_pairs={{0,8},{4,12},{8,16},{12,20},{16,24},{20,28},{24,0},{28,4},{1,9},{5... | collective-permute-start | bytes 196616 | tf_op jit(solution)/shard_map/ppermute | solution.py:597
  14.2 7.3 %collective-permute-start.2 = (f32[16,8,128]{2,1,0:T(8,128)S(1)}, f32[16,8,128]{2,1,0:T(8,128)S(1)}, u32[]{:S(2)}, u32[]{:S(2)}) collective-permute-start(f32[16,8,128]{2,1,0:T(8,128)S(1)} %get-tuple-element.41), channel_id=1, source_target_pairs={{0,16},{4,20},{8,24},{12,28},{16,0},{20,4},{24,8},{28,12},{1,17},{... | collective-permute-start | bytes 196616 | tf_op jit(solution)/shard_map/ppermute | solution.py:597
  16.8 4.8 %collective-permute-start.1 = (f32[16,8,128]{2,1,0:T(8,128)S(1)}, f32[16,8,128]{2,1,0:T(8,128)S(1)}, u32[]{:S(2)}, u32[]{:S(2)}) collective-permute-start(f32[16,8,128]{2,1,0:T(8,128)S(1)} %get-tuple-element.42), channel_id=1, source_target_pairs={{0,24},{4,28},{8,0},{12,4},{16,8},{20,12},{24,16},{28,20},{1,25},{... | collective-permute-start | bytes 196616 | tf_op jit(solution)/shard_map/ppermute | solution.py:597
  21.6 0.7 copy-start.17
  22.2 0.7 copy-start.16
  23.0 5.7 %copy-start = (f32[16,8,128]{2,1,0:T(8,128)}, f32[16,8,128]{2,1,0:T(8,128)S(1)}, u32[]{:S(2)}) copy-start(f32[16,8,128]{2,1,0:T(8,128)S(1)} %concatenate.9.refs_3_.refs_12_) | copy-start | bytes 196612
  23.0 2.5 %collective-permute-start.6 = (f32[16,8,128]{2,1,0:T(8,128)S(1)}, f32[16,8,128]{2,1,0:T(8,128)S(1)}, u32[]{:S(2)}, u32[]{:S(2)}) collective-permute-start(f32[16,8,128]{2,1,0:T(8,128)S(1)} %concatenate.9.refs_3_.refs_12_), channel_id=1, source_target_pairs={{1,0},{0,1},{3,2},{2,3},{5,4},{4,5},{7,6},{6,7},{9,8},{8,9},{11,10... | collective-permute-start | bytes 196616 | tf_op jit(solution)/shard_map/ppermute | solution.py:52
  23.1 4.5 %collective-permute-start.5 = (f32[16,8,128]{2,1,0:T(8,128)S(1)}, f32[16,8,128]{2,1,0:T(8,128)S(1)}, u32[]{:S(2)}, u32[]{:S(2)}) collective-permute-start(f32[16,8,128]{2,1,0:T(8,128)S(1)} %concatenate.9.refs_3_.refs_12_), channel_id=1, source_target_pairs={{2,0},{3,1},{0,2},{1,3},{6,4},{7,5},{4,6},{5,7},{10,8},{11,9},{8,1... | collective-permute-start | bytes 196616 | tf_op jit(solution)/shard_map/ppermute | solution.py:52
  24.7 4.1 %collective-permute-start.4 = (f32[16,8,128]{2,1,0:T(8,128)S(1)}, f32[16,8,128]{2,1,0:T(8,128)S(1)}, u32[]{:S(2)}, u32[]{:S(2)}) collective-permute-start(f32[16,8,128]{2,1,0:T(8,128)S(1)} %concatenate.9.refs_3_.refs_12_), channel_id=1, source_target_pairs={{3,0},{2,1},{1,2},{0,3},{7,4},{6,5},{5,6},{4,7},{11,8},{10,9},{9,1... | collective-permute-start | bytes 196616 | tf_op jit(solution)/shard_map/ppermute | solution.py:52
  25.5 3.2 %copy-start.2 = (f32[16,8,128]{2,1,0:T(8,128)}, f32[16,8,128]{2,1,0:T(8,128)S(1)}, u32[]{:S(2)}) copy-start(f32[16,8,128]{2,1,0:T(8,128)S(1)} %collective-permute-done.6.refs_6_) | copy-start | bytes 196612
  27.6 1.2 %copy-start.3 = (f32[16,8,128]{2,1,0:T(8,128)}, f32[16,8,128]{2,1,0:T(8,128)S(1)}, u32[]{:S(2)}) copy-start(f32[16,8,128]{2,1,0:T(8,128)S(1)} %collective-permute-done.5.refs_5_) | copy-start | bytes 196612
  28.7 0.6 copy-start.4
  43.0 1.9 %collective-permute-start.9 = (f32[16,4,128]{2,1,0:T(4,128)}, f32[16,4,128]{2,1,0:T(4,128)S(1)}, u32[]{:S(2)}, u32[]{:S(2)}) collective-permute-start(f32[16,4,128]{2,1,0:T(4,128)} %get-tuple-element.20.refs_3_), channel_id=1, source_target_pairs={{1,0},{0,1},{3,2},{2,3},{5,4},{4,5},{7,6},{6,7},{9,8},{8,9},{11,10... | collective-permute-start | bytes 98312 | tf_op jit(solution)/shard_map/ppermute | solution.py:52
  43.2 4.1 %collective-permute-start.8 = (f32[16,4,128]{2,1,0:T(4,128)}, f32[16,4,128]{2,1,0:T(4,128)S(1)}, u32[]{:S(2)}, u32[]{:S(2)}) collective-permute-start(f32[16,4,128]{2,1,0:T(4,128)} %get-tuple-element.20.refs_3_), channel_id=1, source_target_pairs={{2,0},{3,1},{0,2},{1,3},{6,4},{7,5},{4,6},{5,7},{10,8},{11,9},{8,1... | collective-permute-start | bytes 98312 | tf_op jit(solution)/shard_map/ppermute | solution.py:52
  44.6 3.9 %collective-permute-start.7 = (f32[16,4,128]{2,1,0:T(4,128)}, f32[16,4,128]{2,1,0:T(4,128)S(1)}, u32[]{:S(2)}, u32[]{:S(2)}) collective-permute-start(f32[16,4,128]{2,1,0:T(4,128)} %get-tuple-element.20.refs_3_), channel_id=1, source_target_pairs={{3,0},{2,1},{1,2},{0,3},{7,4},{6,5},{5,6},{4,7},{11,8},{10,9},{9,1... | collective-permute-start | bytes 98312 | tf_op jit(solution)/shard_map/ppermute | solution.py:52
  44.9 3.6 %copy-start.9 = (f32[16,4,128]{2,1,0:T(4,128)}, f32[16,4,128]{2,1,0:T(4,128)S(1)}, u32[]{:S(2)}) copy-start(f32[16,4,128]{2,1,0:T(4,128)S(1)} %collective-permute-done.9.refs_6_) | copy-start | bytes 98308
  47.3 1.2 %copy-start.11 = (f32[16,4,128]{2,1,0:T(4,128)}, f32[16,4,128]{2,1,0:T(4,128)S(1)}, u32[]{:S(2)}) copy-start(f32[16,4,128]{2,1,0:T(4,128)S(1)} %collective-permute-done.8.refs_5_) | copy-start | bytes 98308
  48.5 0.6 copy-start.13
  62.8 1.9 %collective-permute-start.12 = (f32[16,4,128]{2,1,0:T(4,128)}, f32[16,4,128]{2,1,0:T(4,128)S(1)}, u32[]{:S(2)}, u32[]{:S(2)}) collective-permute-start(f32[16,4,128]{2,1,0:T(4,128)} %get-tuple-element.24.refs_3_), channel_id=1, source_target_pairs={{1,0},{0,1},{3,2},{2,3},{5,4},{4,5},{7,6},{6,7},{9,8},{8,9},{11,10... | collective-permute-start | bytes 98312 | tf_op jit(solution)/shard_map/ppermute | solution.py:52
  62.9 4.4 %collective-permute-start.11 = (f32[16,4,128]{2,1,0:T(4,128)}, f32[16,4,128]{2,1,0:T(4,128)S(1)}, u32[]{:S(2)}, u32[]{:S(2)}) collective-permute-start(f32[16,4,128]{2,1,0:T(4,128)} %get-tuple-element.24.refs_3_), channel_id=1, source_target_pairs={{2,0},{3,1},{0,2},{1,3},{6,4},{7,5},{4,6},{5,7},{10,8},{11,9},{8,1... | collective-permute-start | bytes 98312 | tf_op jit(solution)/shard_map/ppermute | solution.py:52
  63.5 3.9 %collective-permute-start.10 = (f32[16,4,128]{2,1,0:T(4,128)}, f32[16,4,128]{2,1,0:T(4,128)S(1)}, u32[]{:S(2)}, u32[]{:S(2)}) collective-permute-start(f32[16,4,128]{2,1,0:T(4,128)} %get-tuple-element.24.refs_3_), channel_id=1, source_target_pairs={{3,0},{2,1},{1,2},{0,3},{7,4},{6,5},{5,6},{4,7},{11,8},{10,9},{9,1... | collective-permute-start | bytes 98312 | tf_op jit(solution)/shard_map/ppermute | solution.py:52
  64.7 2.8 %copy-start.10 = (f32[16,4,128]{2,1,0:T(4,128)}, f32[16,4,128]{2,1,0:T(4,128)S(1)}, u32[]{:S(2)}) copy-start(f32[16,4,128]{2,1,0:T(4,128)S(1)} %collective-permute-done.12.refs_6_) | copy-start | bytes 98308
  67.3 0.6 copy-start.12
  67.4 0.6 copy-start.14
  81.7 1.9 %collective-permute-start.15 = (f32[16,4,128]{2,1,0:T(4,128)}, f32[16,4,128]{2,1,0:T(4,128)S(1)}, u32[]{:S(2)}, u32[]{:S(2)}) collective-permute-start(f32[16,4,128]{2,1,0:T(4,128)} %get-tuple-element.27.refs_3_), channel_id=1, source_target_pairs={{1,0},{0,1},{3,2},{2,3},{5,4},{4,5},{7,6},{6,7},{9,8},{8,9},{11,10... | collective-permute-start | bytes 98312 | tf_op jit(solution)/shard_map/ppermute | solution.py:52
  81.8 4.1 %collective-permute-start.14 = (f32[16,4,128]{2,1,0:T(4,128)}, f32[16,4,128]{2,1,0:T(4,128)S(1)}, u32[]{:S(2)}, u32[]{:S(2)}) collective-permute-start(f32[16,4,128]{2,1,0:T(4,128)} %get-tuple-element.27.refs_3_), channel_id=1, source_target_pairs={{2,0},{3,1},{0,2},{1,3},{6,4},{7,5},{4,6},{5,7},{10,8},{11,9},{8,1... | collective-permute-start | bytes 98312 | tf_op jit(solution)/shard_map/ppermute | solution.py:52
  83.0 3.7 %collective-permute-start.13 = (f32[16,4,128]{2,1,0:T(4,128)}, f32[16,4,128]{2,1,0:T(4,128)S(1)}, u32[]{:S(2)}, u32[]{:S(2)}) collective-permute-start(f32[16,4,128]{2,1,0:T(4,128)} %get-tuple-element.27.refs_3_), channel_id=1, source_target_pairs={{3,0},{2,1},{1,2},{0,3},{7,4},{6,5},{5,6},{4,7},{11,8},{10,9},{9,1... | collective-permute-start | bytes 98312 | tf_op jit(solution)/shard_map/ppermute | solution.py:52
  83.6 3.0 %copy-start.5 = (f32[16,4,128]{2,1,0:T(4,128)}, f32[16,4,128]{2,1,0:T(4,128)S(1)}, u32[]{:S(2)}) copy-start(f32[16,4,128]{2,1,0:T(4,128)S(1)} %collective-permute-done.15.refs_6_) | copy-start | bytes 98308
  85.9 0.7 copy-start.6
  86.6 0.6 copy-start.7
  100.9 3.3 %copy-start.8 = (f32[1,4,4,3,128]{4,3,2,1,0:T(4,128)S(1)}, f32[1,4,4,3,128]{4,3,2,1,0:T(4,128)}, u32[]{:S(2)}) copy-start(f32[1,4,4,3,128]{4,3,2,1,0:T(4,128)} %get-tuple-element.37) | copy-start | bytes 73732
  100.9 3.9 %collective-permute-start.18 = (f32[8,128]{1,0:T(8,128)}, f32[8,128]{1,0:T(8,128)S(1)}, u32[]{:S(2)}, u32[]{:S(2)}) collective-permute-start(f32[8,128]{1,0:T(8,128)} %get-tuple-element.33.refs_2_), channel_id=1, source_target_pairs={{1,0},{0,1},{3,2},{2,3},{5,4},{4,5},{7,6},{6,7},{9,8},{8,9},{11,10... | collective-permute-start | bytes 12296 | tf_op jit(solution)/shard_map/ppermute | solution.py:52
  101.0 3.8 %collective-permute-start.17 = (f32[8,128]{1,0:T(8,128)}, f32[8,128]{1,0:T(8,128)S(1)}, u32[]{:S(2)}, u32[]{:S(2)}) collective-permute-start(f32[8,128]{1,0:T(8,128)} %get-tuple-element.33.refs_2_), channel_id=1, source_target_pairs={{2,0},{3,1},{0,2},{1,3},{6,4},{7,5},{4,6},{5,7},{10,8},{11,9},{8,1... | collective-permute-start | bytes 12296 | tf_op jit(solution)/shard_map/ppermute | solution.py:52
  102.0 3.2 %collective-permute-start.16 = (f32[8,128]{1,0:T(8,128)}, f32[8,128]{1,0:T(8,128)S(1)}, u32[]{:S(2)}, u32[]{:S(2)}) collective-permute-start(f32[8,128]{1,0:T(8,128)} %get-tuple-element.33.refs_2_), channel_id=1, source_target_pairs={{3,0},{2,1},{1,2},{0,3},{7,4},{6,5},{5,6},{4,7},{11,8},{10,9},{9,1... | collective-permute-start | bytes 12296 | tf_op jit(solution)/shard_map/ppermute | solution.py:52
  104.8 0.6 copy-start.21
  104.9 0.6 copy-start.22
  105.2 0.6 copy-start.23

commit v3 on v2

--- a/solution.py
+++ b/solution.py
@@ -22,6 +22,7 @@
 MIDDLE_Z = 1.0
 REACH = 1.49
 FAR = 2.0**126
+SMALL = 4 * 2**20
 ROWS = 16
 
 X, Y, Z, LAM, CHG, STR, GRP, SIT = range(8)
@@ -94,12 +95,26 @@
     return angles + step_size * speeds, speeds
 
 
-def lane_column(row, first, sub_iota):
+def extra_row(cfg, number):
+    return number // cfg["rows_y"], number % cfg["rows_y"]
+
+
+def angle_row(ref, cfg, kind, site):
+    i, j = extra_row(cfg, kind * NSITE + site)
+    return ref[i, 3, j : j + 1, :]
+
+
+def lane_column(row, sub_iota):
     lane = lax.broadcasted_iota(jnp.int32, sub_iota.shape, 1)
-    hit = lane == lax.broadcasted_iota(jnp.int32, sub_iota.shape, 0) + first
+    hit = lane == lax.broadcasted_iota(jnp.int32, sub_iota.shape, 0)
     return jnp.broadcast_to(
         jnp.sum(jnp.where(hit, row, 0.0), axis=1, keepdims=True), sub_iota.shape
     )
+
+
+def block_rows(ref, cfg, tile, first, last):
+    i, j = tile // cfg["rows_y"], tile % cfg["rows_y"]
+    return jnp.concatenate([ref[i, row, j : j + 1, :] for row in range(first, last)], axis=0)
 
 
 def noise_table(anoise_ref, moment, sub_iota):
@@ -112,7 +127,12 @@
     return jnp.stack(tables)
 
 
-def packed_totals(blocks, sub_iota):
+def packed_rows(ref, cfg):
+    rows_y = cfg["rows_y"]
+    return jnp.concatenate([ref[i, 3] for i in range(-(-NSUB // rows_y))], axis=0)[0:NSUB]
+
+
+def packed_totals(blocks):
     packed = blocks[0]
     for block in blocks[1:]:
         packed = packed + block
@@ -128,7 +148,7 @@
         taken, refs[:n] = refs[:n], []
         return taken
 
-    part_ref, at_ref, anoise_ref = take(3)
+    part_ref, anoise_ref = take(2)
     coord_refs = take(nb)
     (stat_ref,) = take(1) if moment > 0 else (None,)
     (tot_ref,) = take(1) if moment > 0 and not cfg["covered"] else (None,)
@@ -140,24 +160,20 @@
     velo_ref, ango_ref = take(2)
     (stato_ref,) = take(1) if moment == 0 else (None,)
     (sumo_ref,) = take(1) if last else (None,)
-    pool_ref, col_ref, fcol_ref, sum_ref, feat_ref, wide_ref, rhs_ref, coef_ref, off_ref = take(9)
+    pool_ref, col_ref, fcol_ref, sum_ref, feat_ref, wide_ref, rhs_ref, coef_ref, off_ref, io_ref = take(10)
 
     sub_iota = lax.broadcasted_iota(jnp.int32, (NSUB, lanes), 0).astype(jnp.float32)
     if moment == 0:
-        row = coord_refs[0][0, 3:4, :]
         angles, aspeeds = (
             jnp.stack(
-                [
-                    lane_column(row, (kind * NSITE + site) * NSUB, sub_iota)
-                    for site in range(NSITE)
-                ]
+                [lane_column(angle_row(coord_refs[0], cfg, kind, site), sub_iota) for site in range(NSITE)]
             )
             for kind in range(2)
         )
     else:
         angles, aspeeds = ang_ref[0], ang_ref[1]
         if cfg["covered"]:
-            packed = packed_totals([ref[0:NSUB, 3, :] for ref in coord_refs], sub_iota)
+            packed = packed_totals([packed_rows(ref, cfg) for ref in coord_refs])
         else:
             packed = tot_ref[...]
         angles, aspeeds = angle_step(
@@ -169,7 +185,7 @@
     lambdas = softmax_angles(angles)
 
     def line(axis, rows, count):
-        at = at_ref[axis]
+        at = lax.axis_index(axis)
         middle = at.astype(jnp.float32) * rows + 0.5 * rows
         shifts, cells = [], []
         for ring in range(rows + 2):
@@ -182,8 +198,8 @@
             cells.append(turn - middle - (ring - 0.5 - 0.5 * rows))
         return shifts, cells
 
-    shift_x, cell_x = line(0, cfg["rows_x"], cfg["count_x"])
-    shift_y, cell_y = line(1, cfg["rows_y"], cfg["count_y"])
+    shift_x, cell_x = line("gx", cfg["rows_x"], cfg["count_x"])
+    shift_y, cell_y = line("gy", cfg["rows_y"], cfg["count_y"])
     worst = jnp.zeros((3, lanes), jnp.float32)
     row3 = lax.broadcasted_iota(jnp.int32, (3, lanes), 0)
     for index, (block, tile) in enumerate(cfg["sources"]):
@@ -191,13 +207,13 @@
         off_ref[0, index] = shift_x[pi]
         off_ref[1, index] = shift_y[pj]
         if moment == 0:
-            stat = coord_refs[block][tile, 4:8, :]
+            stat = block_rows(coord_refs[block], cfg, tile, 4, 8)
             stato_ref[index] = stat
         else:
             stat = stat_ref[index]
         cell = jnp.where(row3 == 0, cell_x[pi], cell_y[pj])
         cell = jnp.where(row3 == 2, -MIDDLE_Z, cell)
-        coords = coord_refs[block][tile, 0:3, :]
+        coords = block_rows(coord_refs[block], cfg, tile, 0, 3)
         worst = jnp.maximum(worst, jnp.abs(coords + cell))
         pool_ref[index, 0:3, :] = coords
         pool_ref[index, 4:8, :] = stat
@@ -209,10 +225,17 @@
         pool_ref[index, 3:4, :] = jnp.where(group >= 0.0, lam, 1.0)
 
     stray = jnp.max(worst * jnp.where(row3 == 2, 0.5, 1.0))
+    for tile in range(cfg["tiles"]):
+        i, j = tile // cfg["rows_y"], tile % cfg["rows_y"]
+        for row in range(3):
+            io_ref[tile, row : row + 1, :] = vel_ref[i, row, j : j + 1, :]
+            io_ref[tile, 4 + row : 5 + row, :] = noise_ref[0, 0, i, row, j : j + 1, :]
+        io_ref[tile, 3:4, :] = inv_ref[i, j : j + 1, :]
+
     sum_ref[...] = jnp.zeros_like(sum_ref)
     fcol_ref[...] = jnp.zeros_like(fcol_ref)
-    ins = (vel_ref, noise_ref, inv_ref, start_ref)
-    outs = (out_ref, velo_ref, sum_ref)
+    ins = io_ref
+    outs = (io_ref, sum_ref)
     near = cfg["roomy"] & (stray < REACH)
 
     @pl.when(near)
@@ -227,13 +250,21 @@
         any_forces(cfg, part_ref, pool_ref, col_ref, fcol_ref, ins, outs, sub_iota)
 
     packed = pack_sums(cfg, sum_ref)
+    for tile in range(cfg["tiles"]):
+        i, j = tile // cfg["rows_y"], tile % cfg["rows_y"]
+        here = slice(j, j + 1)
+        for row in range(3):
+            coord = io_ref[tile, row : row + 1, :]
+            if last:
+                coord = coord - start_ref[i, row, here, :]
+            out_ref[i, row, here, :] = coord
+            velo_ref[i, row, here, :] = io_ref[tile, 4 + row : 5 + row, :]
+        if not last:
+            out_ref[i, 3, here, :] = (
+                packed[tile : tile + 1, :] if tile < NSUB else jnp.zeros((1, lanes), jnp.float32)
+            )
     if last:
         sumo_ref[...] = packed
-    else:
-        for tile in range(cfg["tiles"]):
-            out_ref[tile, 3:4, :] = (
-                packed[tile : tile + 1, :] if tile < NSUB else jnp.zeros((1, lanes), jnp.float32)
-            )
 
 
 def part_of(part_ref, cfg, tile, k):
@@ -457,23 +488,17 @@
 
 
 def finish_tile(cfg, tile, forces, drive, block, ins, outs, sub_iota):
-    vel_ref, noise_ref, inv_ref, start_ref = ins
-    out_ref, velo_ref, sum_ref = outs
-    i, j = tile // cfg["rows_y"], tile % cfg["rows_y"]
+    _, sum_ref = outs
     damping = math.exp(-friction_rate * step_size)
-    inverse = inv_ref[i, pl.ds(j, 1), :]
+    rows = ins[tile]
+    inverse = rows[3:4, :]
     speeds = (
-        damping * vel_ref[tile, 0:3, :]
+        damping * rows[0:3, :]
         + step_size * forces * inverse
-        + jnp.sqrt((1.0 - damping**2) * inverse) * noise_ref[0, 0, i, j]
-    )
-    coords = block[0:3, :] + step_size * speeds
-    if start_ref is None:
-        velo_ref[tile, 0:3, :] = speeds
-        out_ref[tile, 0:3, :] = coords
-    else:
-        velo_ref[0, i, j] = speeds
-        out_ref[0, i, j] = coords - start_ref[tile, 0:3, :]
+        + jnp.sqrt((1.0 - damping**2) * inverse) * rows[4:7, :]
+    )
+    ins[tile, 0:3, :] = block[0:3, :] + step_size * speeds
+    ins[tile, 4:7, :] = speeds
     group = block[GRP : GRP + 1, :]
     for site in range(NSITE):
         sum_ref[site] += jnp.where(group == sub_iota + float(site * NSUB), drive, 0.0)
@@ -494,16 +519,16 @@
     return packed
 
 
-def step_call(cfg, moment, parts, at, anoise, blocks, stat, totals, vel, noise, inverse, ang, start):
+def step_call(cfg, moment, parts, anoise, blocks, stat, totals, vel, noise, inverse, ang, start):
     tiles, lanes, pool = cfg["tiles"], cfg["lanes"], cfg["pool"]
     rows_x, rows_y = cfg["rows_x"], cfg["rows_y"]
     last = moment == STEPS - 1
     vmem = pl.BlockSpec(memory_space=pltpu.VMEM)
     smem = pl.BlockSpec(memory_space=pltpu.SMEM)
     noise_spec = pl.BlockSpec(
-        (1, 1, rows_x, rows_y, 3, lanes), lambda i: (0, moment, 0, 0, 0, 0)
-    )
-    args = [(parts, smem), (at, smem), (anoise, smem)] + [(block, vmem) for block in blocks]
+        (1, 1, rows_x, 3, rows_y, lanes), lambda i: (0, moment, 0, 0, 0, 0)
+    )
+    args = [(parts, smem), (anoise, smem)] + [(block, vmem) for block in blocks]
     if moment > 0:
         args.append((stat, vmem))
     if totals is not None:
@@ -513,8 +538,8 @@
         args.append((ang, vmem))
     if last:
         args.append((start, vmem))
-    whole = (1, rows_x, rows_y, 3, lanes)
-    shapes = [whole, whole] if last else [(tiles, 4, lanes), (tiles, 4, lanes)]
+    vectors = (rows_x, 3, rows_y, lanes)
+    shapes = [vectors if last else (rows_x, 4, rows_y, lanes), vectors]
     shapes.append((2, NSITE, NSUB, lanes))
     if moment == 0:
         shapes.append((pool, 4, lanes))
@@ -537,7 +562,9 @@
             pltpu.VMEM((4, depth, lanes), jnp.bfloat16),
             pltpu.VMEM((pool + 1, 32, 2 * lanes), jnp.bfloat16),
             pltpu.SMEM((2, pool), jnp.float32),
+            pltpu.VMEM((tiles, 8, lanes), jnp.float32),
         ],
+        compiler_params=pltpu.CompilerParams(vmem_limit_bytes=4 * SMALL),
         name="langevin_step",
     )(*[value for value, _ in args])
 
@@ -547,7 +574,7 @@
     tot_refs, (theta_ref, speed_ref) = refs[2:-2], refs[-2:]
     lanes = cfg["lanes"]
     sub_iota = lax.broadcasted_iota(jnp.int32, (NSUB, lanes), 0).astype(jnp.float32)
-    packed = packed_totals([ref[...] for ref in tot_refs], sub_iota)
+    packed = packed_totals([ref[...] for ref in tot_refs])
     results = angle_step(
         ang_ref[0], ang_ref[1], packed, noise_table(anoise_ref, STEPS - 1, sub_iota),
         cfg["angle_mass"],
@@ -570,35 +597,85 @@
         in_specs=[pl.BlockSpec(memory_space=pltpu.SMEM)] + [vmem] * (1 + len(totals)),
         out_specs=(vmem, vmem),
         name="last_angles",
+        compiler_params=pltpu.CompilerParams(vmem_limit_bytes=SMALL),
     )(anoise, ang, *totals)
 
 
-def clone(message, source_slot):
+def send_kernel(width, sets, slot_ref, mine_ref, other_ref, *out_refs):
+    me = lax.axis_index("walker")
+    for k, ref in enumerate(out_refs, 1):
+        wanted = slot_ref[lax.rem(me + k * width, width * sets)]
+        own = lax.rem(wanted, width) == lax.rem(me, width)
+
+        @pl.when(own)
+        def _():
+            ref[...] = mine_ref[...]
+
+        @pl.when(jnp.logical_not(own))
+        def _():
+            ref[...] = other_ref[...]
+
+
+def pick_kernel(width, sets, slot_ref, *refs):
+    block_refs = refs[: sets + 1]
+    charge_ref, strength_ref, site_ref, sub_ref, pay_ref, vel_ref = refs[sets + 1 :]
+    me = lax.axis_index("walker")
+    source = slot_ref[me]
+    hop = lax.rem(me // width - source // width + sets, sets)
+    choice = jnp.where(hop > 0, hop + 1, (lax.rem(source, width) != lax.rem(me, width)).astype(jnp.int32))
+    for k, ref in enumerate(block_refs):
+
+        @pl.when(choice == k)
+        def _():
+            pay_ref[:, 0:4] = ref[:, 0:4]
+            vel_ref[...] = ref[:, 4:7]
+
+    site, sub = site_ref[...], sub_ref[...]
+    grouped = site < NSITE
+    pay_ref[:, 4] = charge_ref[...]
+    pay_ref[:, 5] = strength_ref[...]
+    pay_ref[:, 6] = jnp.where(grouped, site * NSUB + sub, -1).astype(jnp.float32)
+    pay_ref[:, 7] = jnp.where(grouped, site, -1).astype(jnp.float32)
+
+
+def clone(cfg, message, source_slot, charges, strengths, atom_site, atom_sub):
     peers = lax.axis_size("walker")
-    me = lax.axis_index("walker")
     width = 2 if peers % 2 == 0 else 1
     sets = peers // width
-    mine = message
+    rows_x, rows_y, lanes = charges.shape
+    vmem = pl.BlockSpec(memory_space=pltpu.VMEM)
+    smem = pl.BlockSpec(memory_space=pltpu.SMEM)
+    other = message
     if width == 2:
         other = lax.ppermute(message, "walker", [(w, w ^ 1) for w in range(peers)])
-        odd = me % 2 == 1
-    else:
-        other, odd = message, me < 0
-
-    def held(slot):
-        return jnp.where((slot % 2 == 1) == odd, mine, other) if width == 2 else mine
-
-    source = source_slot[me]
-    result = held(source)
-    hop = (me // width - source // width) % sets
-    for k in range(1, sets):
-        target = (me + k * width) % peers
-        sent = held(source_slot[target])
-        got = lax.ppermute(
-            sent, "walker", [(w, (w + k * width) % peers) for w in range(peers)]
-        )
-        result = jnp.where(hop == k, got, result)
-    return result
+    blocks = [message, other]
+    if sets > 1:
+        shape = jax.ShapeDtypeStruct(message.shape, jnp.float32)
+        sent = pl.pallas_call(
+            functools.partial(send_kernel, width, sets),
+            out_shape=(shape,) * (sets - 1),
+            in_specs=[smem, vmem, vmem],
+            out_specs=(vmem,) * (sets - 1),
+            name="choose_sent",
+        compiler_params=pltpu.CompilerParams(vmem_limit_bytes=SMALL),
+        )(source_slot, message, other)
+        for k, value in enumerate(sent, 1):
+            blocks.append(
+                lax.ppermute(
+                    value, "walker", [(w, (w + k * width) % peers) for w in range(peers)]
+                )
+            )
+    return pl.pallas_call(
+        functools.partial(pick_kernel, width, sets),
+        out_shape=(
+            jax.ShapeDtypeStruct((rows_x, 8, rows_y, lanes), jnp.float32),
+            jax.ShapeDtypeStruct((rows_x, 3, rows_y, lanes), jnp.float32),
+        ),
+        in_specs=[smem] + [vmem] * (len(blocks) + 4),
+        out_specs=(vmem, vmem),
+        name="choose_received",
+        compiler_params=pltpu.CompilerParams(vmem_limit_bytes=SMALL),
+    )(source_slot, *blocks, charges, strengths, atom_site, atom_sub)
 
 
 def make_cfg(rows_x, rows_y, lanes, count_x, count_y, slots, offsets):
@@ -648,38 +725,27 @@
     def gather_blocks(value):
         return [value] + [shifted(value, offset, count_x, count_y) for offset in offsets]
 
-    is_group = atom_site < NSITE
-    groups = jnp.where(is_group, atom_site * NSUB + atom_sub, -1)
-    sites = jnp.where(is_group, atom_site, -1)
-    stat = jnp.stack(
-        [charges, strengths, groups.astype(jnp.float32), sites.astype(jnp.float32)], axis=2
-    ).reshape(tiles, 4, lanes)
-
-    angles = jnp.stack([lambda_theta[0], theta_velocity[0]]).reshape(1, 2 * NSITE * NSUB)
-    angles = jnp.pad(angles, ((0, 0), (0, lanes - 2 * NSITE * NSUB)))
-    extra = jnp.broadcast_to(angles[:, None, :], (tiles, 1, lanes))
+    angles = jnp.concatenate([lambda_theta[0], theta_velocity[0]], axis=0)
+    angles = jnp.pad(angles, ((0, tiles - angles.shape[0]), (0, lanes - NSUB)))
     message = jnp.concatenate(
         [
-            positions.reshape(tiles, 3, lanes),
-            extra,
-            velocities.reshape(tiles, 3, lanes),
-            jnp.zeros((tiles, 1, lanes), jnp.float32),
+            positions[0].transpose(0, 2, 1, 3),
+            angles.reshape(rows_x, 1, rows_y, lanes),
+            velocities[0].transpose(0, 2, 1, 3),
         ],
         axis=1,
     )
-    start = clone(message, source_slot)
-    vel = start[:, 4:8, :]
-    at = jnp.stack([lax.axis_index("gx"), lax.axis_index("gy")])
-    pay = jnp.concatenate([start[:, 0:4, :], stat], axis=1)
+    pay, vel = clone(cfg, message, source_slot, charges, strengths, atom_site, atom_sub)
+    noise = atom_noise.transpose(0, 1, 2, 4, 3, 5)
     first = pay
     ang = pool_stat = None
     for moment in range(STEPS):
         totals = None
         if moment > 0 and not cfg["covered"]:
-            totals = lax.psum(pay[:NSUB, 3, :], ("gx", "gy"))
+            totals = lax.psum(pay[:, 3].reshape(tiles, lanes)[:NSUB], ("gx", "gy"))
         outs = step_call(
-            cfg, moment, partners, at, theta_noise, gather_blocks(pay), pool_stat, totals, vel,
-            atom_noise, inverse_mass, ang, first,
+            cfg, moment, partners, theta_noise, gather_blocks(pay), pool_stat, totals, vel,
+            noise, inverse_mass, ang, first,
         )
         pay, vel, ang = outs[:3]
         if moment == 0:
@@ -690,7 +756,8 @@
     else:
         totals = [lax.psum(packed, ("gx", "gy"))]
     theta, theta_speed = angle_call(cfg, theta_noise, ang, totals)
-    return pay, vel, theta, theta_speed
+    back = lambda value: value.transpose(0, 2, 1, 3)[None]
+    return back(pay), back(vel), theta, theta_speed
 
 
 def solution(mesh):

time: 108 us -> 95.9 us (0.89)
  local copies, waits for them, and re-layouts: 9.31 us -> 0.72 us
  between operations: 9.32 us -> 0.75 us
  waiting for transfers between devices: 13 us -> 19.9 us
  Pallas kernels: 56.4 us -> 54.3 us
    unnamed x53 -> x20, local copies, waits for them, and re-layouts: 7.85 us -> 0.72 us
    pallas_call x4, Pallas kernels: 54.8 us -> 51.7 us  [step_call(): pl.pallas_call(functools.partial(step_kernel, cfg, moment), grid=(1,), ou...]
    ppermute x3, waiting for transfers between devices: 0.05 us -> 2.83 us  [clone(): lax.ppermute(value, 'walker', [(w, (w + k * width) % peers) for w in rang...]
    ppermute x1, waiting for transfers between devices: 0.01 us -> 2.16 us  [clone(): other = lax.ppermute(message, 'walker', [(w, w ^ 1) for w in range(peers)])]
    ppermute x15, waiting for transfers between devices: 13 us -> 14.9 us  [shifted(): return lax.ppermute(value, ('gx', 'gy'), pairs)]
    concatenate x1 -> x2, other arithmetic: 0.08 us -> 1.47 us  [the longest x1 0.78 us: per_device(): jnp.concatenate([positions[0].transpose(0, 2, 1, 3), angles.reshape(rows_...]
    another operation x2 -> x0, other arithmetic: 1.29 us -> none  [the longest x1 0.7 us: per_device(): jnp.stack([lambda_theta[0], theta_velocity[0]]).reshape(1, 2 * NSITE * NSUB)]
    pallas_call x0 -> x2, Pallas kernels: none -> 1.21 us  [the longest x1 0.61 us: clone(): pl.pallas_call(functools.partial(send_kernel, width, sets), out_shape=(sh...]
  transfers between devices with their start and end apart: 19 -> 19, of which waited for: 10 -> 14; matrix products, arithmetic and copies ran while one was open for 4% -> 0% of each run, Pallas kernels for 0% -> 0%
where the time goes in v3:
time: 95.9 us; the launch traced here: 95.6 us
  Pallas kernels  54.3 us (57%)
  waiting for transfers between devices  19.9 us (21%)
  starting transfers between devices  18.5 us (19%)
  other arithmetic  1.47 us (2%)
    pallas_call x4, Pallas kernels, step_call(): pl.pallas_call(functools.partial(step_kernel, cfg, moment), grid=(1,), ou...  51.7 us
    ppermute x15, waiting for transfers between devices, shifted(): return lax.ppermute(value, ('gx', 'gy'), pairs)  14.9 us
    ppermute x15, starting transfers between devices, shifted(): return lax.ppermute(value, ('gx', 'gy'), pairs)  9.39 us
    ppermute x3, starting transfers between devices, clone(): lax.ppermute(value, 'walker', [(w, (w + k * width) % peers) for w in rang...  6.1 us
    ppermute x1, starting transfers between devices, clone(): other = lax.ppermute(message, 'walker', [(w, w ^ 1) for w in range(peers)])  3.03 us
    ppermute x3, waiting for transfers between devices, clone(): lax.ppermute(value, 'walker', [(w, (w + k * width) % peers) for w in rang...  2.83 us
    ppermute x1, waiting for transfers between devices, clone(): other = lax.ppermute(message, 'walker', [(w, w ^ 1) for w in range(peers)])  2.16 us
  transfers between devices with their start and end apart: 19, of which 14 were waited for; matrix products, arithmetic and copies ran while one was open for 0% of the time, Pallas kernels for 0%

profile of v3, /device:TPU:0, one launch (start us, length us, event | category | flops | bytes accessed | tf_op | source)
XLA Modules:
  0.0 95.6 jit_solution(18178805626617058029)
XLA Ops:
  0.6 0.0 copy-start.9
  0.6 0.7 copy-done.9
  1.3 0.7 select_maximum_fusion
  2.0 0.0 copy-start.8
  2.0 0.8 pad_maximum_fusion.mine_ref.refs_0_
  2.8 3.0 %collective-permute-start = (f32[4,7,4,128]{3,2,1,0:T(4,128)S(1)}, f32[4,7,4,128]{3,2,1,0:T(4,128)S(1)}, u32[]{:S(2)}, u32[]{:S(2)}) collective-permute-start(f32[4,7,4,128]{3,2,1,0:T(4,128)S(1)} %pad_maximum_fusion.mine_ref.refs_0_), channel_id=1, source_target_pairs={{0,4},{4,0},{8,12},{12,8},{16,20},{20,16},{24,28},{28,24},{1,5},{5... | collective-permute-start | bytes 172040 | tf_op jit(solution)/shard_map/ppermute | solution.py:650
  5.8 2.2 %collective-permute-done.other_ref.refs_1_ = f32[4,7,4,128]{3,2,1,0:T(4,128)S(1)} collective-permute-done((f32[4,7,4,128]{3,2,1,0:T(4,128)S(1)}, f32[4,7,4,128]{3,2,1,0:T(4,128)S(1)}, u32[]{:S(2)}, u32[]{:S(2)}) %collective-permute-start) | collective-permute-done | bytes 57376 | tf_op jit(solution)/shard_map/ppermute | solution.py:650
  8.0 0.0 copy-done.8
  8.0 0.0 copy-start.5
  8.0 0.0 copy-start.7
  8.0 0.6 choose_sent.1
  8.6 2.2 %collective-permute-start.1 = (f32[4,7,4,128]{3,2,1,0:T(4,128)S(1)}, f32[4,7,4,128]{3,2,1,0:T(4,128)S(1)}, u32[]{:S(2)}, u32[]{:S(2)}) collective-permute-start(f32[4,7,4,128]{3,2,1,0:T(4,128)S(1)} %get-tuple-element.25), channel_id=1, source_target_pairs={{0,8},{4,12},{8,16},{12,20},{16,24},{20,28},{24,0},{28,4},{1,9},{5... | collective-permute-start | bytes 172040 | tf_op jit(solution)/shard_map/ppermute | solution.py:664
  10.8 2.6 %collective-permute-start.2 = (f32[4,7,4,128]{3,2,1,0:T(4,128)S(1)}, f32[4,7,4,128]{3,2,1,0:T(4,128)S(1)}, u32[]{:S(2)}, u32[]{:S(2)}) collective-permute-start(f32[4,7,4,128]{3,2,1,0:T(4,128)S(1)} %get-tuple-element.26), channel_id=1, source_target_pairs={{0,16},{4,20},{8,24},{12,28},{16,0},{20,4},{24,8},{28,12},{1,17},{... | collective-permute-start | bytes 172040 | tf_op jit(solution)/shard_map/ppermute | solution.py:664
  13.4 1.3 %collective-permute-start.3 = (f32[4,7,4,128]{3,2,1,0:T(4,128)S(1)}, f32[4,7,4,128]{3,2,1,0:T(4,128)S(1)}, u32[]{:S(2)}, u32[]{:S(2)}) collective-permute-start(f32[4,7,4,128]{3,2,1,0:T(4,128)S(1)} %get-tuple-element.27), channel_id=1, source_target_pairs={{0,24},{4,28},{8,0},{12,4},{16,8},{20,12},{24,16},{28,20},{1,25},{... | collective-permute-start | bytes 172040 | tf_op jit(solution)/shard_map/ppermute | solution.py:664
  14.7 0.8 collective-permute-done.1.refs_2_
  15.5 0.6 collective-permute-done.2.refs_3_
  16.1 1.4 %collective-permute-done.3.refs_4_ = f32[4,7,4,128]{3,2,1,0:T(4,128)S(1)} collective-permute-done((f32[4,7,4,128]{3,2,1,0:T(4,128)S(1)}, f32[4,7,4,128]{3,2,1,0:T(4,128)S(1)}, u32[]{:S(2)}, u32[]{:S(2)}) %collective-permute-start.3) | collective-permute-done | bytes 57376 | tf_op jit(solution)/shard_map/ppermute | solution.py:664
  17.6 0.0 copy-done.4
  17.6 0.0 copy-done.5
  17.6 0.0 copy-done.6
  17.6 0.0 copy-done.7
  17.6 0.0 copy-start.1
  17.6 0.0 copy-start.2
  17.6 0.0 copy-start.3
  17.6 0.6 choose_received.1
  18.2 0.1 collective-permute-start.6
  18.3 1.6 %collective-permute-start.5 = (f32[4,8,4,128]{3,2,1,0:T(4,128)S(1)}, f32[4,8,4,128]{3,2,1,0:T(4,128)S(1)}, u32[]{:S(2)}, u32[]{:S(2)}) collective-permute-start(f32[4,8,4,128]{3,2,1,0:T(4,128)S(1)} %get-tuple-element.28.refs_2_.refs_11_), channel_id=1, source_target_pairs={{2,0},{3,1},{0,2},{1,3},{6,4},{7,5},{4,6},{5,7},{10,8},{11,9},{8,1... | collective-permute-start | bytes 196616 | tf_op jit(solution)/shard_map/ppermute | solution.py:53
  19.9 0.3 collective-permute-start.4
  20.1 0.0 collective-permute-done.6.refs_5_
  20.1 2.6 %collective-permute-done.5.refs_4_ = f32[4,8,4,128]{3,2,1,0:T(4,128)S(1)} collective-permute-done((f32[4,8,4,128]{3,2,1,0:T(4,128)S(1)}, f32[4,8,4,128]{3,2,1,0:T(4,128)S(1)}, u32[]{:S(2)}, u32[]{:S(2)}) %collective-permute-start.5) | collective-permute-done | bytes 65568 | tf_op jit(solution)/shard_map/ppermute | solution.py:53
  22.8 1.1 %collective-permute-done.4.refs_3_ = f32[4,8,4,128]{3,2,1,0:T(4,128)S(1)} collective-permute-done((f32[4,8,4,128]{3,2,1,0:T(4,128)S(1)}, f32[4,8,4,128]{3,2,1,0:T(4,128)S(1)}, u32[]{:S(2)}, u32[]{:S(2)}) %collective-permute-start.4) | collective-permute-done | bytes 65568 | tf_op jit(solution)/shard_map/ppermute | solution.py:53
  23.9 0.0 copy-done
  23.9 0.0 copy-done.1
  23.9 0.0 copy-done.2
  24.0 0.0 copy-done.3
  24.0 12.8 %langevin_step.4 = (f32[4,4,4,128]{3,2,1,0:T(4,128)S(1)}, f32[4,3,4,128]{3,2,1,0:T(4,128)S(1)}, f32[2,4,8,128]{3,2,1,0:T(8,128)S(1)}, f32[36,4,128]{2,1,0:T(4,128)S(1)}) custom-call(s32[4,4,9]{2,1,0:T(4,128)S(1)} %copy-done.2, f32[1,4,4,8]{3,2,1,0:T(4,128)S(1)} %copy-done.1, f32[4,8,4,128]{3,2,1,0:T(4,128)S(1)} %get-tuple-element.28.refs_2_.refs_11_, ...), custom_call_target="tpu_custom_call" | custom-call | tf_op jit(solution)/shard_map/langevin_step/pallas_call | solution.py:549
  36.8 0.2 collective-permute-start.9
  37.0 1.4 %collective-permute-start.8 = (f32[4,4,4,128]{3,2,1,0:T(4,128)S(1)}, f32[4,4,4,128]{3,2,1,0:T(4,128)S(1)}, u32[]{:S(2)}, u32[]{:S(2)}) collective-permute-start(f32[4,4,4,128]{3,2,1,0:T(4,128)S(1)} %get-tuple-element.30.refs_2_), channel_id=1, source_target_pairs={{2,0},{3,1},{0,2},{1,3},{6,4},{7,5},{4,6},{5,7},{10,8},{11,9},{8,1... | collective-permute-start | bytes 98312 | tf_op jit(solution)/shard_map/ppermute | solution.py:53
  38.4 0.3 collective-permute-start.7
  38.7 0.0 collective-permute-done.9.refs_5_
  38.7 2.2 %collective-permute-done.8.refs_4_ = f32[4,4,4,128]{3,2,1,0:T(4,128)S(1)} collective-permute-done((f32[4,4,4,128]{3,2,1,0:T(4,128)S(1)}, f32[4,4,4,128]{3,2,1,0:T(4,128)S(1)}, u32[]{:S(2)}, u32[]{:S(2)}) %collective-permute-start.8) | collective-permute-done | bytes 32800 | tf_op jit(solution)/shard_map/ppermute | solution.py:53
  40.9 1.2 %collective-permute-done.7.refs_3_ = f32[4,4,4,128]{3,2,1,0:T(4,128)S(1)} collective-permute-done((f32[4,4,4,128]{3,2,1,0:T(4,128)S(1)}, f32[4,4,4,128]{3,2,1,0:T(4,128)S(1)}, u32[]{:S(2)}, u32[]{:S(2)}) %collective-permute-start.7) | collective-permute-done | bytes 32800 | tf_op jit(solution)/shard_map/ppermute | solution.py:53
  42.1 12.8 %langevin_step.5 = (f32[4,4,4,128]{3,2,1,0:T(4,128)S(1)}, f32[4,3,4,128]{3,2,1,0:T(4,128)S(1)}, f32[2,4,8,128]{3,2,1,0:T(8,128)S(1)}) custom-call(s32[4,4,9]{2,1,0:T(4,128)S(1)} %copy-done.2, f32[1,4,4,8]{3,2,1,0:T(4,128)S(1)} %copy-done.1, f32[4,4,4,128]{3,2,1,0:T(4,128)S(1)} %get-tuple-element.30.refs_2_, ...), custom_call_target="tpu_custom_call" | custom-call | tf_op jit(solution)/shard_map/langevin_step/pallas_call | solution.py:549
  54.8 0.2 collective-permute-start.12
  55.0 0.7 collective-permute-start.11
  55.6 1.1 %collective-permute-start.10 = (f32[4,4,4,128]{3,2,1,0:T(4,128)S(1)}, f32[4,4,4,128]{3,2,1,0:T(4,128)S(1)}, u32[]{:S(2)}, u32[]{:S(2)}) collective-permute-start(f32[4,4,4,128]{3,2,1,0:T(4,128)S(1)} %get-tuple-element.34.refs_2_), channel_id=1, source_target_pairs={{3,0},{2,1},{1,2},{0,3},{7,4},{6,5},{5,6},{4,7},{11,8},{10,9},{9,1... | collective-permute-start | bytes 98312 | tf_op jit(solution)/shard_map/ppermute | solution.py:53
  56.7 0.0 collective-permute-done.12.refs_5_
  56.7 2.5 %collective-permute-done.11.refs_4_ = f32[4,4,4,128]{3,2,1,0:T(4,128)S(1)} collective-permute-done((f32[4,4,4,128]{3,2,1,0:T(4,128)S(1)}, f32[4,4,4,128]{3,2,1,0:T(4,128)S(1)}, u32[]{:S(2)}, u32[]{:S(2)}) %collective-permute-start.11) | collective-permute-done | bytes 32800 | tf_op jit(solution)/shard_map/ppermute | solution.py:53
  59.2 0.2 collective-permute-done.10.refs_3_
  59.3 12.7 %langevin_step.6 = (f32[4,4,4,128]{3,2,1,0:T(4,128)S(1)}, f32[4,3,4,128]{3,2,1,0:T(4,128)S(1)}, f32[2,4,8,128]{3,2,1,0:T(8,128)S(1)}) custom-call(s32[4,4,9]{2,1,0:T(4,128)S(1)} %copy-done.2, f32[1,4,4,8]{3,2,1,0:T(4,128)S(1)} %copy-done.1, f32[4,4,4,128]{3,2,1,0:T(4,128)S(1)} %get-tuple-element.34.refs_2_, ...), custom_call_target="tpu_custom_call" | custom-call | tf_op jit(solution)/shard_map/langevin_step/pallas_call | solution.py:549
  72.1 0.1 collective-permute-start.15
  72.2 1.2 %collective-permute-start.14 = (f32[4,4,4,128]{3,2,1,0:T(4,128)S(1)}, f32[4,4,4,128]{3,2,1,0:T(4,128)S(1)}, u32[]{:S(2)}, u32[]{:S(2)}) collective-permute-start(f32[4,4,4,128]{3,2,1,0:T(4,128)S(1)} %get-tuple-element.37.refs_2_), channel_id=1, source_target_pairs={{2,0},{3,1},{0,2},{1,3},{6,4},{7,5},{4,6},{5,7},{10,8},{11,9},{8,1... | collective-permute-start | bytes 98312 | tf_op jit(solution)/shard_map/ppermute | solution.py:53
  73.4 0.6 collective-permute-start.13
  74.0 0.0 collective-permute-done.15.refs_5_
  74.0 2.2 %collective-permute-done.14.refs_4_ = f32[4,4,4,128]{3,2,1,0:T(4,128)S(1)} collective-permute-done((f32[4,4,4,128]{3,2,1,0:T(4,128)S(1)}, f32[4,4,4,128]{3,2,1,0:T(4,128)S(1)}, u32[]{:S(2)}, u32[]{:S(2)}) %collective-permute-start.14) | collective-permute-done | bytes 32800 | tf_op jit(solution)/shard_map/ppermute | solution.py:53
  76.1 0.7 collective-permute-done.13.refs_3_
  76.8 13.4 %langevin_step.7 = (f32[4,3,4,128]{3,2,1,0:T(4,128)}, f32[4,3,4,128]{3,2,1,0:T(4,128)}, f32[2,4,8,128]{3,2,1,0:T(8,128)S(1)}, f32[8,128]{1,0:T(8,128)S(1)}) custom-call(s32[4,4,9]{2,1,0:T(4,128)S(1)} %copy-done.2, f32[1,4,4,8]{3,2,1,0:T(4,128)S(1)} %copy-done.1, f32[4,4,4,128]{3,2,1,0:T(4,128)S(1)} %get-tuple-element.37.refs_2_, ...), custom_call_target="tpu_custom_call" | custom-call | tf_op jit(solution)/shard_map/langevin_step/pallas_call | solution.py:549
  90.1 0.1 collective-permute-start.18
  90.3 1.0 %collective-permute-start.17 = (f32[8,128]{1,0:T(8,128)S(1)}, f32[8,128]{1,0:T(8,128)S(1)}, u32[]{:S(2)}, u32[]{:S(2)}) collective-permute-start(f32[8,128]{1,0:T(8,128)S(1)} %get-tuple-element.43.refs_2_), channel_id=1, source_target_pairs={{2,0},{3,1},{0,2},{1,3},{6,4},{7,5},{4,6},{5,7},{10,8},{11,9},{8,1... | collective-permute-start | bytes 12296 | tf_op jit(solution)/shard_map/ppermute | solution.py:53
  91.2 0.8 collective-permute-start.16
  92.0 0.0 collective-permute-done.18.refs_5_
  92.0 1.9 %collective-permute-done.17.refs_4_ = f32[8,128]{1,0:T(8,128)S(1)} collective-permute-done((f32[8,128]{1,0:T(8,128)S(1)}, f32[8,128]{1,0:T(8,128)S(1)}, u32[]{:S(2)}, u32[]{:S(2)}) %collective-permute-start.17) | collective-permute-done | bytes 4128 | tf_op jit(solution)/shard_map/ppermute | solution.py:53
  93.9 0.4 collective-permute-done.16.refs_3_
  94.3 1.4 %last_angles.1 = (f32[1,4,8]{2,1,0:T(4,128)}, f32[1,4,8]{2,1,0:T(4,128)}) custom-call(f32[1,4,4,8]{3,2,1,0:T(4,128)S(1)} %copy-done.1, f32[2,4,8,128]{3,2,1,0:T(8,128)S(1)} %get-tuple-element.42.refs_1_, f32[8,128]{1,0:T(8,128)S(1)} %get-tuple-element.43.refs_2_, f32[8,128]{1,0:T(8,128)S(1)} %collective-permute-done.16.refs_3_, ...), custom_call_target="tpu_custom_call" | custom-call | tf_op jit(solution)/shard_map/last_angles/pallas_call | solution.py:594
  (3 shorter events, 0.0 us)
Async XLA Ops:
  0.6 0.7 copy-start.9
  2.0 6.0 %copy-start.8 = (s32[8]{0:T(128)S(1)}, s32[8]{0:T(128)}, u32[]{:S(2)}) copy-start(s32[8]{0:T(128)} %slot_ref.3) | copy-start | bytes 100
  2.8 5.2 %collective-permute-start = (f32[4,7,4,128]{3,2,1,0:T(4,128)S(1)}, f32[4,7,4,128]{3,2,1,0:T(4,128)S(1)}, u32[]{:S(2)}, u32[]{:S(2)}) collective-permute-start(f32[4,7,4,128]{3,2,1,0:T(4,128)S(1)} %pad_maximum_fusion.mine_ref.refs_0_), channel_id=1, source_target_pairs={{0,4},{4,0},{8,12},{12,8},{16,20},{20,16},{24,28},{28,24},{1,5},{5... | collective-permute-start | bytes 172040 | tf_op jit(solution)/shard_map/ppermute | solution.py:650
  8.0 9.6 %copy-start.4 = (f32[4,4,128]{2,1,0:T(4,128)S(1)}, f32[4,4,128]{2,1,0:T(4,128)}, u32[]{:S(2)}) copy-start(f32[4,4,128]{2,1,0:T(4,128)} %refs_5_.1) | copy-start | bytes 24580
  8.0 9.6 %copy-start.5 = (f32[4,4,128]{2,1,0:T(4,128)S(1)}, f32[4,4,128]{2,1,0:T(4,128)}, u32[]{:S(2)}) copy-start(f32[4,4,128]{2,1,0:T(4,128)} %refs_6_.1) | copy-start | bytes 24580
  8.0 9.6 %copy-start.6 = (s32[4,4,128]{2,1,0:T(4,128)S(1)}, s32[4,4,128]{2,1,0:T(4,128)}, u32[]{:S(2)}) copy-start(s32[4,4,128]{2,1,0:T(4,128)} %refs_7_.1) | copy-start | bytes 24580
  8.0 9.6 %copy-start.7 = (s32[4,4,128]{2,1,0:T(4,128)S(1)}, s32[4,4,128]{2,1,0:T(4,128)}, u32[]{:S(2)}) copy-start(s32[4,4,128]{2,1,0:T(4,128)} %refs_8_.2) | copy-start | bytes 24580
  8.6 6.9 %collective-permute-start.1 = (f32[4,7,4,128]{3,2,1,0:T(4,128)S(1)}, f32[4,7,4,128]{3,2,1,0:T(4,128)S(1)}, u32[]{:S(2)}, u32[]{:S(2)}) collective-permute-start(f32[4,7,4,128]{3,2,1,0:T(4,128)S(1)} %get-tuple-element.25), channel_id=1, source_target_pairs={{0,8},{4,12},{8,16},{12,20},{16,24},{20,28},{24,0},{28,4},{1,9},{5... | collective-permute-start | bytes 172040 | tf_op jit(solution)/shard_map/ppermute | solution.py:664
  10.8 5.4 %collective-permute-start.2 = (f32[4,7,4,128]{3,2,1,0:T(4,128)S(1)}, f32[4,7,4,128]{3,2,1,0:T(4,128)S(1)}, u32[]{:S(2)}, u32[]{:S(2)}) collective-permute-start(f32[4,7,4,128]{3,2,1,0:T(4,128)S(1)} %get-tuple-element.26), channel_id=1, source_target_pairs={{0,16},{4,20},{8,24},{12,28},{16,0},{20,4},{24,8},{28,12},{1,17},{... | collective-permute-start | bytes 172040 | tf_op jit(solution)/shard_map/ppermute | solution.py:664
  13.4 10.6 %copy-start = (f32[1,4,4,4,3,128]{5,3,4,2,1,0:T(4,128)S(1)}, f32[1,4,4,4,3,128]{5,3,4,2,1,0:T(4,128)}, u32[]{:S(2)}) copy-start(f32[1,4,4,4,3,128]{5,3,4,2,1,0:T(4,128)} %param.18) | copy-start | bytes 294916
  13.4 4.2 %collective-permute-start.3 = (f32[4,7,4,128]{3,2,1,0:T(4,128)S(1)}, f32[4,7,4,128]{3,2,1,0:T(4,128)S(1)}, u32[]{:S(2)}, u32[]{:S(2)}) collective-permute-start(f32[4,7,4,128]{3,2,1,0:T(4,128)S(1)} %get-tuple-element.27), channel_id=1, source_target_pairs={{0,24},{4,28},{8,0},{12,4},{16,8},{20,12},{24,16},{28,20},{1,25},{... | collective-permute-start | bytes 172040 | tf_op jit(solution)/shard_map/ppermute | solution.py:664
  17.6 6.4 %copy-start.1 = (f32[1,4,4,8]{3,2,1,0:T(4,128)S(1)}, f32[1,4,4,8]{3,2,1,0:T(4,128)}, u32[]{:S(2)}) copy-start(f32[1,4,4,8]{3,2,1,0:T(4,128)} %refs_0_.9) | copy-start | bytes 1540
  17.6 6.4 %copy-start.2 = (s32[4,4,9]{2,1,0:T(4,128)S(1)}, s32[4,4,9]{2,1,0:T(4,128)}, u32[]{:S(2)}) copy-start(s32[4,4,9]{2,1,0:T(4,128)} %refs_0_.8) | copy-start | bytes 1732
  17.6 6.4 %copy-start.3 = (f32[4,4,128]{2,1,0:T(4,128)S(1)}, f32[4,4,128]{2,1,0:T(4,128)}, u32[]{:S(2)}) copy-start(f32[4,4,128]{2,1,0:T(4,128)} %refs_9_.5) | copy-start | bytes 24580
  18.2 1.9 %collective-permute-start.6 = (f32[4,8,4,128]{3,2,1,0:T(4,128)S(1)}, f32[4,8,4,128]{3,2,1,0:T(4,128)S(1)}, u32[]{:S(2)}, u32[]{:S(2)}) collective-permute-start(f32[4,8,4,128]{3,2,1,0:T(4,128)S(1)} %get-tuple-element.28.refs_2_.refs_11_), channel_id=1, source_target_pairs={{1,0},{0,1},{3,2},{2,3},{5,4},{4,5},{7,6},{6,7},{9,8},{8,9},{11,10... | collective-permute-start | bytes 196616 | tf_op jit(solution)/shard_map/ppermute | solution.py:53
  18.3 4.5 %collective-permute-start.5 = (f32[4,8,4,128]{3,2,1,0:T(4,128)S(1)}, f32[4,8,4,128]{3,2,1,0:T(4,128)S(1)}, u32[]{:S(2)}, u32[]{:S(2)}) collective-permute-start(f32[4,8,4,128]{3,2,1,0:T(4,128)S(1)} %get-tuple-element.28.refs_2_.refs_11_), channel_id=1, source_target_pairs={{2,0},{3,1},{0,2},{1,3},{6,4},{7,5},{4,6},{5,7},{10,8},{11,9},{8,1... | collective-permute-start | bytes 196616 | tf_op jit(solution)/shard_map/ppermute | solution.py:53
  19.9 4.1 %collective-permute-start.4 = (f32[4,8,4,128]{3,2,1,0:T(4,128)S(1)}, f32[4,8,4,128]{3,2,1,0:T(4,128)S(1)}, u32[]{:S(2)}, u32[]{:S(2)}) collective-permute-start(f32[4,8,4,128]{3,2,1,0:T(4,128)S(1)} %get-tuple-element.28.refs_2_.refs_11_), channel_id=1, source_target_pairs={{3,0},{2,1},{1,2},{0,3},{7,4},{6,5},{5,6},{4,7},{11,8},{10,9},{9,1... | collective-permute-start | bytes 196616 | tf_op jit(solution)/shard_map/ppermute | solution.py:53
  36.8 1.9 %collective-permute-start.9 = (f32[4,4,4,128]{3,2,1,0:T(4,128)S(1)}, f32[4,4,4,128]{3,2,1,0:T(4,128)S(1)}, u32[]{:S(2)}, u32[]{:S(2)}) collective-permute-start(f32[4,4,4,128]{3,2,1,0:T(4,128)S(1)} %get-tuple-element.30.refs_2_), channel_id=1, source_target_pairs={{1,0},{0,1},{3,2},{2,3},{5,4},{4,5},{7,6},{6,7},{9,8},{8,9},{11,10... | collective-permute-start | bytes 98312 | tf_op jit(solution)/shard_map/ppermute | solution.py:53
  37.0 3.9 %collective-permute-start.8 = (f32[4,4,4,128]{3,2,1,0:T(4,128)S(1)}, f32[4,4,4,128]{3,2,1,0:T(4,128)S(1)}, u32[]{:S(2)}, u32[]{:S(2)}) collective-permute-start(f32[4,4,4,128]{3,2,1,0:T(4,128)S(1)} %get-tuple-element.30.refs_2_), channel_id=1, source_target_pairs={{2,0},{3,1},{0,2},{1,3},{6,4},{7,5},{4,6},{5,7},{10,8},{11,9},{8,1... | collective-permute-start | bytes 98312 | tf_op jit(solution)/shard_map/ppermute | solution.py:53
  38.4 3.7 %collective-permute-start.7 = (f32[4,4,4,128]{3,2,1,0:T(4,128)S(1)}, f32[4,4,4,128]{3,2,1,0:T(4,128)S(1)}, u32[]{:S(2)}, u32[]{:S(2)}) collective-permute-start(f32[4,4,4,128]{3,2,1,0:T(4,128)S(1)} %get-tuple-element.30.refs_2_), channel_id=1, source_target_pairs={{3,0},{2,1},{1,2},{0,3},{7,4},{6,5},{5,6},{4,7},{11,8},{10,9},{9,1... | collective-permute-start | bytes 98312 | tf_op jit(solution)/shard_map/ppermute | solution.py:53
  54.8 1.9 %collective-permute-start.12 = (f32[4,4,4,128]{3,2,1,0:T(4,128)S(1)}, f32[4,4,4,128]{3,2,1,0:T(4,128)S(1)}, u32[]{:S(2)}, u32[]{:S(2)}) collective-permute-start(f32[4,4,4,128]{3,2,1,0:T(4,128)S(1)} %get-tuple-element.34.refs_2_), channel_id=1, source_target_pairs={{1,0},{0,1},{3,2},{2,3},{5,4},{4,5},{7,6},{6,7},{9,8},{8,9},{11,10... | collective-permute-start | bytes 98312 | tf_op jit(solution)/shard_map/ppermute | solution.py:53
  55.0 4.2 %collective-permute-start.11 = (f32[4,4,4,128]{3,2,1,0:T(4,128)S(1)}, f32[4,4,4,128]{3,2,1,0:T(4,128)S(1)}, u32[]{:S(2)}, u32[]{:S(2)}) collective-permute-start(f32[4,4,4,128]{3,2,1,0:T(4,128)S(1)} %get-tuple-element.34.refs_2_), channel_id=1, source_target_pairs={{2,0},{3,1},{0,2},{1,3},{6,4},{7,5},{4,6},{5,7},{10,8},{11,9},{8,1... | collective-permute-start | bytes 98312 | tf_op jit(solution)/shard_map/ppermute | solution.py:53
  55.6 3.7 %collective-permute-start.10 = (f32[4,4,4,128]{3,2,1,0:T(4,128)S(1)}, f32[4,4,4,128]{3,2,1,0:T(4,128)S(1)}, u32[]{:S(2)}, u32[]{:S(2)}) collective-permute-start(f32[4,4,4,128]{3,2,1,0:T(4,128)S(1)} %get-tuple-element.34.refs_2_), channel_id=1, source_target_pairs={{3,0},{2,1},{1,2},{0,3},{7,4},{6,5},{5,6},{4,7},{11,8},{10,9},{9,1... | collective-permute-start | bytes 98312 | tf_op jit(solution)/shard_map/ppermute | solution.py:53
  72.1 1.9 %collective-permute-start.15 = (f32[4,4,4,128]{3,2,1,0:T(4,128)S(1)}, f32[4,4,4,128]{3,2,1,0:T(4,128)S(1)}, u32[]{:S(2)}, u32[]{:S(2)}) collective-permute-start(f32[4,4,4,128]{3,2,1,0:T(4,128)S(1)} %get-tuple-element.37.refs_2_), channel_id=1, source_target_pairs={{1,0},{0,1},{3,2},{2,3},{5,4},{4,5},{7,6},{6,7},{9,8},{8,9},{11,10... | collective-permute-start | bytes 98312 | tf_op jit(solution)/shard_map/ppermute | solution.py:53
  72.2 3.9 %collective-permute-start.14 = (f32[4,4,4,128]{3,2,1,0:T(4,128)S(1)}, f32[4,4,4,128]{3,2,1,0:T(4,128)S(1)}, u32[]{:S(2)}, u32[]{:S(2)}) collective-permute-start(f32[4,4,4,128]{3,2,1,0:T(4,128)S(1)} %get-tuple-element.37.refs_2_), channel_id=1, source_target_pairs={{2,0},{3,1},{0,2},{1,3},{6,4},{7,5},{4,6},{5,7},{10,8},{11,9},{8,1... | collective-permute-start | bytes 98312 | tf_op jit(solution)/shard_map/ppermute | solution.py:53
  73.4 3.4 %collective-permute-start.13 = (f32[4,4,4,128]{3,2,1,0:T(4,128)S(1)}, f32[4,4,4,128]{3,2,1,0:T(4,128)S(1)}, u32[]{:S(2)}, u32[]{:S(2)}) collective-permute-start(f32[4,4,4,128]{3,2,1,0:T(4,128)S(1)} %get-tuple-element.37.refs_2_), channel_id=1, source_target_pairs={{3,0},{2,1},{1,2},{0,3},{7,4},{6,5},{5,6},{4,7},{11,8},{10,9},{9,1... | collective-permute-start | bytes 98312 | tf_op jit(solution)/shard_map/ppermute | solution.py:53
  90.1 1.9 %collective-permute-start.18 = (f32[8,128]{1,0:T(8,128)S(1)}, f32[8,128]{1,0:T(8,128)S(1)}, u32[]{:S(2)}, u32[]{:S(2)}) collective-permute-start(f32[8,128]{1,0:T(8,128)S(1)} %get-tuple-element.43.refs_2_), channel_id=1, source_target_pairs={{1,0},{0,1},{3,2},{2,3},{5,4},{4,5},{7,6},{6,7},{9,8},{8,9},{11,10... | collective-permute-start | bytes 12296 | tf_op jit(solution)/shard_map/ppermute | solution.py:53
  90.3 3.6 %collective-permute-start.17 = (f32[8,128]{1,0:T(8,128)S(1)}, f32[8,128]{1,0:T(8,128)S(1)}, u32[]{:S(2)}, u32[]{:S(2)}) collective-permute-start(f32[8,128]{1,0:T(8,128)S(1)} %get-tuple-element.43.refs_2_), channel_id=1, source_target_pairs={{2,0},{3,1},{0,2},{1,3},{6,4},{7,5},{4,6},{5,7},{10,8},{11,9},{8,1... | collective-permute-start | bytes 12296 | tf_op jit(solution)/shard_map/ppermute | solution.py:53
  91.2 3.0 %collective-permute-start.16 = (f32[8,128]{1,0:T(8,128)S(1)}, f32[8,128]{1,0:T(8,128)S(1)}, u32[]{:S(2)}, u32[]{:S(2)}) collective-permute-start(f32[8,128]{1,0:T(8,128)S(1)} %get-tuple-element.43.refs_2_), channel_id=1, source_target_pairs={{3,0},{2,1},{1,2},{0,3},{7,4},{6,5},{5,6},{4,7},{11,8},{10,9},{9,1... | collective-permute-start | bytes 12296 | tf_op jit(solution)/shard_map/ppermute | solution.py:53

commit v4 on v3

--- a/solution.py
+++ b/solution.py
@@ -53,6 +53,26 @@
     return lax.ppermute(value, ("gx", "gy"), pairs)
 
 
+def window(offset, rows_x, rows_y):
+    def part(step, rows):
+        return tuple(range(rows)) if step == 0 or rows <= 2 else (0, rows - 1)
+
+    return part(offset[0], rows_x), part(offset[1], rows_y)
+
+
+def sum_rows(shape):
+    nr, nc = shape
+    places = []
+    for row in range(NSUB):
+        extra, at = row // (nr * nc), row % (nr * nc)
+        places.append((at // nc, 3 + extra, at % nc))
+    return places
+
+
+def components(shape):
+    return 3 + -(-NSUB // (shape[0] * shape[1]))
+
+
 def pool_sources(rows_x, rows_y, count_x, count_y, offsets):
     sources = []
     for pi in range(rows_x + 2):
@@ -61,8 +81,9 @@
             dj = -1 if pj == 0 else (1 if pj == rows_y + 1 else 0)
             key = (di % count_x, dj % count_y)
             block = 0 if key == (0, 0) else 1 + offsets.index(key)
-            tile = ((pi - 1) % rows_x) * rows_y + (pj - 1) % rows_y
-            sources.append((block, tile))
+            rows, cols = window(key, rows_x, rows_y)
+            place = rows.index((pi - 1) % rows_x), cols.index((pj - 1) % rows_y)
+            sources.append((block, place))
     return sources
 
 
@@ -95,25 +116,16 @@
     return angles + step_size * speeds, speeds
 
 
-def extra_row(cfg, number):
-    return number // cfg["rows_y"], number % cfg["rows_y"]
-
-
-def angle_row(ref, cfg, kind, site):
-    i, j = extra_row(cfg, kind * NSITE + site)
-    return ref[i, 3, j : j + 1, :]
-
-
-def lane_column(row, sub_iota):
+def lane_column(row, first, sub_iota):
     lane = lax.broadcasted_iota(jnp.int32, sub_iota.shape, 1)
-    hit = lane == lax.broadcasted_iota(jnp.int32, sub_iota.shape, 0)
+    hit = lane == lax.broadcasted_iota(jnp.int32, sub_iota.shape, 0) + first
     return jnp.broadcast_to(
         jnp.sum(jnp.where(hit, row, 0.0), axis=1, keepdims=True), sub_iota.shape
     )
 
 
-def block_rows(ref, cfg, tile, first, last):
-    i, j = tile // cfg["rows_y"], tile % cfg["rows_y"]
+def block_rows(ref, place, first, last):
+    i, j = place
     return jnp.concatenate([ref[i, row, j : j + 1, :] for row in range(first, last)], axis=0)
 
 
@@ -127,9 +139,9 @@
     return jnp.stack(tables)
 
 
-def packed_rows(ref, cfg):
-    rows_y = cfg["rows_y"]
-    return jnp.concatenate([ref[i, 3] for i in range(-(-NSUB // rows_y))], axis=0)[0:NSUB]
+def packed_rows(ref):
+    places = sum_rows((ref.shape[0], ref.shape[2]))
+    return jnp.concatenate([ref[i, c, j : j + 1, :] for i, c, j in places], axis=0)
 
 
 def packed_totals(blocks):
@@ -153,10 +165,10 @@
     (stat_ref,) = take(1) if moment > 0 else (None,)
     (tot_ref,) = take(1) if moment > 0 and not cfg["covered"] else (None,)
     vel_ref, noise_ref, inv_ref = take(3)
-    (ang_ref,) = take(1) if moment > 0 else (None,)
+    (ang_ref,) = take(1)
     last = moment == STEPS - 1
     (start_ref,) = take(1) if last else (None,)
-    (out_ref,) = take(1)
+    out_refs = take(1 if last else nb)
     velo_ref, ango_ref = take(2)
     (stato_ref,) = take(1) if moment == 0 else (None,)
     (sumo_ref,) = take(1) if last else (None,)
@@ -166,14 +178,17 @@
     if moment == 0:
         angles, aspeeds = (
             jnp.stack(
-                [lane_column(angle_row(coord_refs[0], cfg, kind, site), sub_iota) for site in range(NSITE)]
+                [
+                    lane_column(ang_ref[site : site + 1, :], kind * NSUB, sub_iota)
+                    for site in range(NSITE)
+                ]
             )
             for kind in range(2)
         )
     else:
         angles, aspeeds = ang_ref[0], ang_ref[1]
         if cfg["covered"]:
-            packed = packed_totals([packed_rows(ref, cfg) for ref in coord_refs])
+            packed = packed_totals([packed_rows(ref) for ref in coord_refs])
         else:
             packed = tot_ref[...]
         angles, aspeeds = angle_step(
@@ -207,13 +222,13 @@
         off_ref[0, index] = shift_x[pi]
         off_ref[1, index] = shift_y[pj]
         if moment == 0:
-            stat = block_rows(coord_refs[block], cfg, tile, 4, 8)
+            stat = block_rows(coord_refs[block], tile, 3, 7)
             stato_ref[index] = stat
         else:
             stat = stat_ref[index]
         cell = jnp.where(row3 == 0, cell_x[pi], cell_y[pj])
         cell = jnp.where(row3 == 2, -MIDDLE_Z, cell)
-        coords = block_rows(coord_refs[block], cfg, tile, 0, 3)
+        coords = block_rows(coord_refs[block], tile, 0, 3)
         worst = jnp.maximum(worst, jnp.abs(coords + cell))
         pool_ref[index, 0:3, :] = coords
         pool_ref[index, 4:8, :] = stat
@@ -254,15 +269,18 @@
         i, j = tile // cfg["rows_y"], tile % cfg["rows_y"]
         here = slice(j, j + 1)
         for row in range(3):
-            coord = io_ref[tile, row : row + 1, :]
-            if last:
-                coord = coord - start_ref[i, row, here, :]
-            out_ref[i, row, here, :] = coord
             velo_ref[i, row, here, :] = io_ref[tile, 4 + row : 5 + row, :]
+    for (rows, cols), ref in zip(cfg["windows"], out_refs):
+        for ri, i in enumerate(rows):
+            for cj, j in enumerate(cols):
+                for row in range(3):
+                    coord = io_ref[i * cfg["rows_y"] + j, row : row + 1, :]
+                    if last:
+                        coord = coord - start_ref[i, row, j : j + 1, :]
+                    ref[ri, row, cj : cj + 1, :] = coord
         if not last:
-            out_ref[i, 3, here, :] = (
-                packed[tile : tile + 1, :] if tile < NSUB else jnp.zeros((1, lanes), jnp.float32)
-            )
+            for row, (i, c, j) in enumerate(sum_rows((len(rows), len(cols)))):
+                ref[i, c, j : j + 1, :] = packed[row : row + 1, :]
     if last:
         sumo_ref[...] = packed
 
@@ -378,7 +396,11 @@
         def some_partners(k, sums):
             indices = [part_of(part_ref, cfg, tile, k + u) for u in range(cfg["slots"])]
             indices = [jnp.where(index < 0, cfg["pool"], index) for index in indices]
-            outs = [table_dot(feat_ref[index], rhs_ref) for index in indices]
+            outs = []
+            for first in range(0, len(indices), 3):
+                some = indices[first : first + 3]
+                out = table_dot(jnp.concatenate([feat_ref[index] for index in some], axis=0), rhs_ref)
+                outs += [out[n * lanes : (n + 1) * lanes] for n in range(len(some))]
             moments, fd = sums
             for index, out in zip(indices, outs):
                 tops, rests = [], []
@@ -415,7 +437,12 @@
         finish_tile(cfg, tile, (4.0 * strength) * forces, drive, block, ins, outs, sub_iota)
         return carry
 
-    lax.fori_loop(0, cfg["tiles"], one_tile, 0)
+    def some_tiles(k, carry):
+        for u in range(4):
+            one_tile(k * 4 + u, carry)
+        return carry
+
+    lax.fori_loop(0, cfg["tiles"] // 4, some_tiles, 0)
 
 
 def any_forces(cfg, part_ref, pool_ref, col_ref, fcol_ref, ins, outs, sub_iota):
@@ -534,12 +561,16 @@
     if totals is not None:
         args.append((totals, vmem))
     args += [(vel, vmem), (noise, noise_spec), (inverse, vmem)]
-    if moment > 0:
-        args.append((ang, vmem))
+    args.append((ang, vmem))
     if last:
         args.append((start, vmem))
     vectors = (rows_x, 3, rows_y, lanes)
-    shapes = [vectors if last else (rows_x, 4, rows_y, lanes), vectors]
+    if last:
+        shapes = [vectors]
+    else:
+        held = [(len(rows), len(cols)) for rows, cols in cfg["windows"]]
+        shapes = [(nr, components((nr, nc)), nc, lanes) for nr, nc in held]
+    shapes.append(vectors)
     shapes.append((2, NSITE, NSUB, lanes))
     if moment == 0:
         shapes.append((pool, 4, lanes))
@@ -616,35 +647,63 @@
             ref[...] = other_ref[...]
 
 
-def pick_kernel(width, sets, slot_ref, *refs):
+def pick_kernel(width, sets, windows, slot_ref, *refs):
     block_refs = refs[: sets + 1]
-    charge_ref, strength_ref, site_ref, sub_ref, pay_ref, vel_ref = refs[sets + 1 :]
+    charge_ref, strength_ref, site_ref, sub_ref = refs[sets + 1 : sets + 5]
+    *pay_refs, vel_ref, ang_ref = refs[sets + 5 :]
+    rows_x = vel_ref.shape[0]
     me = lax.axis_index("walker")
     source = slot_ref[me]
     hop = lax.rem(me // width - source // width + sets, sets)
-    choice = jnp.where(hop > 0, hop + 1, (lax.rem(source, width) != lax.rem(me, width)).astype(jnp.int32))
+    away = (lax.rem(source, width) != lax.rem(me, width)).astype(jnp.int32)
+    choice = jnp.where(hop > 0, hop + 1, away)
+    own_ref = pay_refs[0]
     for k, ref in enumerate(block_refs):
 
         @pl.when(choice == k)
         def _():
-            pay_ref[:, 0:4] = ref[:, 0:4]
-            vel_ref[...] = ref[:, 4:7]
+            for i in range(rows_x):
+                own_ref[i, 0:3] = ref[6 * i : 6 * i + 3]
+                vel_ref[i] = ref[6 * i + 3 : 6 * i + 6]
+            ang_ref[...] = ref[6 * rows_x]
 
     site, sub = site_ref[...], sub_ref[...]
     grouped = site < NSITE
-    pay_ref[:, 4] = charge_ref[...]
-    pay_ref[:, 5] = strength_ref[...]
-    pay_ref[:, 6] = jnp.where(grouped, site * NSUB + sub, -1).astype(jnp.float32)
-    pay_ref[:, 7] = jnp.where(grouped, site, -1).astype(jnp.float32)
-
-
-def clone(cfg, message, source_slot, charges, strengths, atom_site, atom_sub):
+    own_ref[:, 3] = charge_ref[...]
+    own_ref[:, 4] = strength_ref[...]
+    own_ref[:, 5] = jnp.where(grouped, site * NSUB + sub, -1).astype(jnp.float32)
+    own_ref[:, 6] = jnp.where(grouped, site, -1).astype(jnp.float32)
+    for (rows, cols), ref in zip(windows[1:], pay_refs[1:]):
+        for ri, i in enumerate(rows):
+            for cj, j in enumerate(cols):
+                ref[ri, :, cj : cj + 1, :] = own_ref[i, :, j : j + 1, :]
+
+
+def pack_kernel(pos_ref, vel_ref, theta_ref, speed_ref, out_ref):
+    rows_x = pos_ref.shape[0]
+    for i in range(rows_x):
+        out_ref[6 * i : 6 * i + 3] = pos_ref[i]
+        out_ref[6 * i + 3 : 6 * i + 6] = vel_ref[i]
+    out_ref[6 * rows_x] = jnp.zeros(out_ref.shape[1:], jnp.float32)
+    out_ref[6 * rows_x, :, 0:NSUB] = theta_ref[0]
+    out_ref[6 * rows_x, :, NSUB : 2 * NSUB] = speed_ref[0]
+
+
+def clone(cfg, positions, velocities, theta, speed, source_slot, charges, strengths, atom_site, atom_sub):
     peers = lax.axis_size("walker")
     width = 2 if peers % 2 == 0 else 1
     sets = peers // width
     rows_x, rows_y, lanes = charges.shape
     vmem = pl.BlockSpec(memory_space=pltpu.VMEM)
     smem = pl.BlockSpec(memory_space=pltpu.SMEM)
+    message = pl.pallas_call(
+        pack_kernel,
+        out_shape=jax.ShapeDtypeStruct((6 * rows_x + 1, rows_y, lanes), jnp.float32),
+        in_specs=[vmem] * 4,
+        out_specs=vmem,
+        name="pack_walker",
+        compiler_params=pltpu.CompilerParams(vmem_limit_bytes=SMALL),
+    )(positions, velocities, theta, speed)
     other = message
     if width == 2:
         other = lax.ppermute(message, "walker", [(w, w ^ 1) for w in range(peers)])
@@ -665,14 +724,13 @@
                     value, "walker", [(w, (w + k * width) % peers) for w in range(peers)]
                 )
             )
+    shapes = [(len(rows), 7, len(cols), lanes) for rows, cols in cfg["windows"]]
+    shapes += [(rows_x, 3, rows_y, lanes), (rows_y, lanes)]
     return pl.pallas_call(
-        functools.partial(pick_kernel, width, sets),
-        out_shape=(
-            jax.ShapeDtypeStruct((rows_x, 8, rows_y, lanes), jnp.float32),
-            jax.ShapeDtypeStruct((rows_x, 3, rows_y, lanes), jnp.float32),
-        ),
+        functools.partial(pick_kernel, width, sets, cfg["windows"]),
+        out_shape=tuple(jax.ShapeDtypeStruct(shape, jnp.float32) for shape in shapes),
         in_specs=[smem] + [vmem] * (len(blocks) + 4),
-        out_specs=(vmem, vmem),
+        out_specs=(vmem,) * len(shapes),
         name="choose_received",
         compiler_params=pltpu.CompilerParams(vmem_limit_bytes=SMALL),
     )(source_slot, *blocks, charges, strengths, atom_site, atom_sub)
@@ -691,6 +749,7 @@
         count_y=count_y,
         slots=slots,
         pool=(rows_x + 2) * (rows_y + 2),
+        windows=[window(offset, rows_x, rows_y) for offset in [(0, 0)] + offsets],
         sources=pool_sources(rows_x, rows_y, count_x, count_y, offsets),
         depth=128,
         pool_group=next(g for g in (12, 6, 4, 3, 2, 1) if (rows_x + 2) * (rows_y + 2) % g == 0),
@@ -722,42 +781,38 @@
     offsets = neighbour_offsets(count_x, count_y)
     cfg = make_cfg(rows_x, rows_y, lanes, count_x, count_y, partners.shape[-1], offsets)
 
-    def gather_blocks(value):
-        return [value] + [shifted(value, offset, count_x, count_y) for offset in offsets]
-
-    angles = jnp.concatenate([lambda_theta[0], theta_velocity[0]], axis=0)
-    angles = jnp.pad(angles, ((0, tiles - angles.shape[0]), (0, lanes - NSUB)))
-    message = jnp.concatenate(
-        [
-            positions[0].transpose(0, 2, 1, 3),
-            angles.reshape(rows_x, 1, rows_y, lanes),
-            velocities[0].transpose(0, 2, 1, 3),
-        ],
-        axis=1,
-    )
-    pay, vel = clone(cfg, message, source_slot, charges, strengths, atom_site, atom_sub)
+    def gather_blocks(values):
+        return [values[0]] + [
+            shifted(value, offset, count_x, count_y) for value, offset in zip(values[1:], offsets)
+        ]
+
+    *pays, vel, ang = clone(
+        cfg, positions[0].transpose(0, 2, 1, 3), velocities[0].transpose(0, 2, 1, 3),
+        lambda_theta, theta_velocity, source_slot, charges, strengths, atom_site, atom_sub,
+    )
     noise = atom_noise.transpose(0, 1, 2, 4, 3, 5)
-    first = pay
-    ang = pool_stat = None
+    first = pays[0]
+    pool_stat = None
     for moment in range(STEPS):
         totals = None
         if moment > 0 and not cfg["covered"]:
-            totals = lax.psum(pay[:, 3].reshape(tiles, lanes)[:NSUB], ("gx", "gy"))
+            totals = lax.psum(pays[0][:, 3].reshape(tiles, lanes)[:NSUB], ("gx", "gy"))
         outs = step_call(
-            cfg, moment, partners, theta_noise, gather_blocks(pay), pool_stat, totals, vel,
+            cfg, moment, partners, theta_noise, gather_blocks(pays), pool_stat, totals, vel,
             noise, inverse_mass, ang, first,
         )
-        pay, vel, ang = outs[:3]
+        own = cfg["blocks"] if moment < STEPS - 1 else 1
+        pays, (vel, ang, *rest) = outs[:own], outs[own:]
         if moment == 0:
-            pool_stat = outs[3]
-    packed = outs[3]
+            pool_stat = rest[0]
+    packed = rest[0]
     if cfg["covered"]:
-        totals = gather_blocks(packed)
+        totals = gather_blocks([packed] * cfg["blocks"])
     else:
         totals = [lax.psum(packed, ("gx", "gy"))]
     theta, theta_speed = angle_call(cfg, theta_noise, ang, totals)
     back = lambda value: value.transpose(0, 2, 1, 3)[None]
-    return back(pay), back(vel), theta, theta_speed
+    return back(pays[0]), back(vel), theta, theta_speed
 
 
 def solution(mesh):

time: 95.9 us -> 85.3 us (0.89)
  Pallas kernels: 54.3 us -> 45.4 us
  waiting for transfers between devices: 19.9 us -> 16.2 us
  local copies, waits for them, and re-layouts: 0.72 us -> 2.87 us
  other arithmetic: 1.47 us -> 0 us
  starting transfers between devices: 18.5 us -> 19.7 us
    pallas_call x4, Pallas kernels: 51.7 us -> 42.7 us  [step_call(): pl.pallas_call(functools.partial(step_kernel, cfg, moment), grid=(1,), ou...]
    ppermute x15, waiting for transfers between devices: 14.9 us -> 11.4 us  [shifted(): return lax.ppermute(value, ('gx', 'gy'), pairs)]
    unnamed x20 -> x26, local copies, waits for them, and re-layouts: 0.72 us -> 2.87 us
    concatenate x2 -> x0, other arithmetic: 1.47 us -> none  [the longest x1 0.78 us: per_device(): jnp.concatenate([positions[0].transpose(0, 2, 1, 3), angles.reshape(rows_...]
    ppermute x15, starting transfers between devices: 9.39 us -> 10.6 us  [shifted(): return lax.ppermute(value, ('gx', 'gy'), pairs)]
  transfers between devices with their start and end apart: 19 -> 19, of which waited for: 14 -> 10; matrix products, arithmetic and copies ran while one was open for 0% -> 0% of each run, Pallas kernels for 0% -> 0%
where the time goes in v4:
time: 85.3 us; the launch traced here: 85 us
  Pallas kernels  45.4 us (53%)
  starting transfers between devices  19.7 us (23%)
  waiting for transfers between devices  16.2 us (19%)
  local copies, waits for them, and re-layouts  2.87 us (3%)
    pallas_call x4, Pallas kernels, step_call(): pl.pallas_call(functools.partial(step_kernel, cfg, moment), grid=(1,), ou...  42.7 us
    ppermute x15, waiting for transfers between devices, shifted(): return lax.ppermute(value, ('gx', 'gy'), pairs)  11.4 us
    ppermute x15, starting transfers between devices, shifted(): return lax.ppermute(value, ('gx', 'gy'), pairs)  10.6 us
    ppermute x3, starting transfers between devices, clone(): lax.ppermute(value, 'walker', [(w, (w + k * width) % peers) for w in rang...  6.1 us
    ppermute x1, starting transfers between devices, clone(): other = lax.ppermute(message, 'walker', [(w, w ^ 1) for w in range(peers)])  2.97 us
    unnamed x26, local copies, waits for them, and re-layouts  2.87 us
    ppermute x3, waiting for transfers between devices, clone(): lax.ppermute(value, 'walker', [(w, (w + k * width) % peers) for w in rang...  2.76 us
    ppermute x1, waiting for transfers between devices, clone(): other = lax.ppermute(message, 'walker', [(w, w ^ 1) for w in range(peers)])  2.09 us
  transfers between devices with their start and end apart: 19, of which 10 were waited for; matrix products, arithmetic and copies ran while one was open for 0% of the time, Pallas kernels for 0%

profile of v4, /device:TPU:0, one launch (start us, length us, event | category | flops | bytes accessed | tf_op | source)
XLA Modules:
  0.0 85.0 jit_solution(14311553293561287267)
XLA Ops:
  0.6 0.0 copy-start.11
  0.6 0.7 copy-done.11
  1.3 0.7 copy-done.4
  2.1 0.7 copy-done.5
  2.8 0.7 copy-done.12
  3.5 0.1 pack_walker.1.mine_ref.refs_0_
  3.5 3.0 %collective-permute-start = (f32[25,4,128]{2,1,0:T(4,128)S(1)}, f32[25,4,128]{2,1,0:T(4,128)S(1)}, u32[]{:S(2)}, u32[]{:S(2)}) collective-permute-start(f32[25,4,128]{2,1,0:T(4,128)S(1)} %pack_walker.1.mine_ref.refs_0_), channel_id=1, source_target_pairs={{0,4},{4,0},{8,12},{12,8},{16,20},{20,16},{24,28},{28,24},{1,5},{5... | collective-permute-start | bytes 153608 | tf_op jit(solution)/shard_map/ppermute | solution.py:709
  6.5 2.1 %collective-permute-done.other_ref.refs_1_ = f32[25,4,128]{2,1,0:T(4,128)S(1)} collective-permute-done((f32[25,4,128]{2,1,0:T(4,128)S(1)}, f32[25,4,128]{2,1,0:T(4,128)S(1)}, u32[]{:S(2)}, u32[]{:S(2)}) %collective-permute-start) | collective-permute-done | bytes 51232 | tf_op jit(solution)/shard_map/ppermute | solution.py:709
  8.6 0.0 copy-done.10
  8.6 0.0 copy-start.9
  8.6 0.6 choose_sent.1
  9.3 2.2 %collective-permute-start.1 = (f32[25,4,128]{2,1,0:T(4,128)S(1)}, f32[25,4,128]{2,1,0:T(4,128)S(1)}, u32[]{:S(2)}, u32[]{:S(2)}) collective-permute-start(f32[25,4,128]{2,1,0:T(4,128)S(1)} %get-tuple-element.38), channel_id=1, source_target_pairs={{0,8},{4,12},{8,16},{12,20},{16,24},{20,28},{24,0},{28,4},{1,9},{5... | collective-permute-start | bytes 153608 | tf_op jit(solution)/shard_map/ppermute | solution.py:723
  11.4 2.6 %collective-permute-start.2 = (f32[25,4,128]{2,1,0:T(4,128)S(1)}, f32[25,4,128]{2,1,0:T(4,128)S(1)}, u32[]{:S(2)}, u32[]{:S(2)}) collective-permute-start(f32[25,4,128]{2,1,0:T(4,128)S(1)} %get-tuple-element.39), channel_id=1, source_target_pairs={{0,16},{4,20},{8,24},{12,28},{16,0},{20,4},{24,8},{28,12},{1,17},{... | collective-permute-start | bytes 153608 | tf_op jit(solution)/shard_map/ppermute | solution.py:723
  14.0 1.3 %collective-permute-start.3 = (f32[25,4,128]{2,1,0:T(4,128)S(1)}, f32[25,4,128]{2,1,0:T(4,128)S(1)}, u32[]{:S(2)}, u32[]{:S(2)}) collective-permute-start(f32[25,4,128]{2,1,0:T(4,128)S(1)} %get-tuple-element.40), channel_id=1, source_target_pairs={{0,24},{4,28},{8,0},{12,4},{16,8},{20,12},{24,16},{28,20},{1,25},{... | collective-permute-start | bytes 153608 | tf_op jit(solution)/shard_map/ppermute | solution.py:723
  15.4 0.6 collective-permute-done.1.refs_2_
  16.0 0.5 collective-permute-done.2.refs_3_
  16.5 1.6 %collective-permute-done.3.refs_4_ = f32[25,4,128]{2,1,0:T(4,128)S(1)} collective-permute-done((f32[25,4,128]{2,1,0:T(4,128)S(1)}, f32[25,4,128]{2,1,0:T(4,128)S(1)}, u32[]{:S(2)}, u32[]{:S(2)}) %collective-permute-start.3) | collective-permute-done | bytes 51232 | tf_op jit(solution)/shard_map/ppermute | solution.py:723
  18.1 0.0 copy-done.6
  18.1 0.0 copy-done.7
  18.1 0.0 copy-done.8
  18.1 0.0 copy-done.9
  18.1 0.0 copy-start.2
  18.1 0.0 copy-start.3
  18.2 0.6 choose_received.1
  18.8 0.0 copy-start.1
  18.8 1.6 %collective-permute-start.5 = (f32[2,7,4,128]{3,2,1,0:T(4,128)S(1)}, f32[2,7,4,128]{3,2,1,0:T(4,128)S(1)}, u32[]{:S(2)}, u32[]{:S(2)}) collective-permute-start(f32[2,7,4,128]{3,2,1,0:T(4,128)S(1)} %get-tuple-element.43), channel_id=1, source_target_pairs={{2,0},{3,1},{0,2},{1,3},{6,4},{7,5},{4,6},{5,7},{10,8},{11,9},{8,1... | collective-permute-start | bytes 86024 | tf_op jit(solution)/shard_map/ppermute | solution.py:53
  20.4 0.0 collective-permute-start.6
  20.4 0.6 collective-permute-start.4
  21.0 2.5 %collective-permute-done.4.refs_3_ = f32[2,7,2,128]{3,2,1,0:T(2,128)S(1)} collective-permute-done((f32[2,7,2,128]{3,2,1,0:T(2,128)S(1)}, f32[2,7,2,128]{3,2,1,0:T(2,128)S(1)}, u32[]{:S(2)}, u32[]{:S(2)}) %collective-permute-start.4) | collective-permute-done | bytes 14368 | tf_op jit(solution)/shard_map/ppermute | solution.py:53
  23.5 0.0 collective-permute-done.5.refs_4_
  23.5 0.0 collective-permute-done.6.refs_5_
  23.5 0.0 copy-done
  23.6 0.0 copy-done.2
  23.6 0.0 copy-done.3
  23.6 0.0 copy-done.1
  23.6 10.5 %langevin_step.4 = (f32[4,4,4,128]{3,2,1,0:T(4,128)S(1)}, f32[2,5,2,128]{3,2,1,0:T(2,128)S(1)}, f32[2,4,4,128]{3,2,1,0:T(4,128)S(1)}, f32[4,4,2,128]{3,2,1,0:T(2...) custom-call(s32[4,4,9]{2,1,0:T(4,128)S(1)} %copy-done.2, ...), custom_call_target="tpu_custom_call" | custom-call | tf_op jit(solution)/shard_map/langevin_step/pallas_call | solution.py:580
  34.1 0.9 %collective-permute-start.8 = (f32[2,4,4,128]{3,2,1,0:T(4,128)S(1)}, f32[2,4,4,128]{3,2,1,0:T(4,128)S(1)}, u32[]{:S(2)}, u32[]{:S(2)}) collective-permute-start(f32[2,4,4,128]{3,2,1,0:T(4,128)S(1)} %get-tuple-element.49), channel_id=1, source_target_pairs={{2,0},{3,1},{0,2},{1,3},{6,4},{7,5},{4,6},{5,7},{10,8},{11,9},{8,1... | collective-permute-start | bytes 49160 | tf_op jit(solution)/shard_map/ppermute | solution.py:53
  35.0 0.0 collective-permute-start.9
  35.0 1.3 %collective-permute-start.7 = (f32[2,5,2,128]{3,2,1,0:T(2,128)S(1)}, f32[2,5,2,128]{3,2,1,0:T(2,128)S(1)}, u32[]{:S(2)}, u32[]{:S(2)}) collective-permute-start(f32[2,5,2,128]{3,2,1,0:T(2,128)S(1)} %get-tuple-element.48), channel_id=1, source_target_pairs={{3,0},{2,1},{1,2},{0,3},{7,4},{6,5},{5,6},{4,7},{11,8},{10,9},{9,1... | collective-permute-start | bytes 30728 | tf_op jit(solution)/shard_map/ppermute | solution.py:53
  36.3 1.8 %collective-permute-done.7.refs_3_ = f32[2,5,2,128]{3,2,1,0:T(2,128)S(1)} collective-permute-done((f32[2,5,2,128]{3,2,1,0:T(2,128)S(1)}, f32[2,5,2,128]{3,2,1,0:T(2,128)S(1)}, u32[]{:S(2)}, u32[]{:S(2)}) %collective-permute-start.7) | collective-permute-done | bytes 10272 | tf_op jit(solution)/shard_map/ppermute | solution.py:53
  38.1 0.0 collective-permute-done.8.refs_4_
  38.1 0.0 collective-permute-done.9.refs_5_
  38.1 10.5 %langevin_step.5 = (f32[4,4,4,128]{3,2,1,0:T(4,128)S(1)}, f32[2,5,2,128]{3,2,1,0:T(2,128)S(1)}, f32[2,4,4,128]{3,2,1,0:T(4,128)S(1)}, f32[4,4,2,128]{3,2,1,0:T(2...) custom-call(s32[4,4,9]{2,1,0:T(4,128)S(1)} %copy-done.2, f32[1,4,4,8]{3,2,1,0:T(4,128)S(1)} %copy-done.1, ...), custom_call_target="tpu_custom_call" | custom-call | tf_op jit(solution)/shard_map/langevin_step/pallas_call | solution.py:580
  48.6 1.5 %collective-permute-start.11 = (f32[2,4,4,128]{3,2,1,0:T(4,128)S(1)}, f32[2,4,4,128]{3,2,1,0:T(4,128)S(1)}, u32[]{:S(2)}, u32[]{:S(2)}) collective-permute-start(f32[2,4,4,128]{3,2,1,0:T(4,128)S(1)} %get-tuple-element.56), channel_id=1, source_target_pairs={{2,0},{3,1},{0,2},{1,3},{6,4},{7,5},{4,6},{5,7},{10,8},{11,9},{8,1... | collective-permute-start | bytes 49160 | tf_op jit(solution)/shard_map/ppermute | solution.py:53
  50.1 0.0 collective-permute-start.12
  50.1 0.7 collective-permute-start.10
  50.8 2.4 %collective-permute-done.10.refs_3_ = f32[2,5,2,128]{3,2,1,0:T(2,128)S(1)} collective-permute-done((f32[2,5,2,128]{3,2,1,0:T(2,128)S(1)}, f32[2,5,2,128]{3,2,1,0:T(2,128)S(1)}, u32[]{:S(2)}, u32[]{:S(2)}) %collective-permute-start.10) | collective-permute-done | bytes 10272 | tf_op jit(solution)/shard_map/ppermute | solution.py:53
  53.2 0.0 collective-permute-done.11.refs_4_
  53.2 0.0 collective-permute-done.12.refs_5_
  53.2 10.5 %langevin_step.6 = (f32[4,4,4,128]{3,2,1,0:T(4,128)S(1)}, f32[2,5,2,128]{3,2,1,0:T(2,128)S(1)}, f32[2,4,4,128]{3,2,1,0:T(4,128)S(1)}, f32[4,4,2,128]{3,2,1,0:T(2...) custom-call(s32[4,4,9]{2,1,0:T(4,128)S(1)} %copy-done.2, f32[1,4,4,8]{3,2,1,0:T(4,128)S(1)} %copy-done.1, ...), custom_call_target="tpu_custom_call" | custom-call | tf_op jit(solution)/shard_map/langevin_step/pallas_call | solution.py:580
  63.7 0.9 %collective-permute-start.14 = (f32[2,4,4,128]{3,2,1,0:T(4,128)S(1)}, f32[2,4,4,128]{3,2,1,0:T(4,128)S(1)}, u32[]{:S(2)}, u32[]{:S(2)}) collective-permute-start(f32[2,4,4,128]{3,2,1,0:T(4,128)S(1)} %get-tuple-element.62), channel_id=1, source_target_pairs={{2,0},{3,1},{0,2},{1,3},{6,4},{7,5},{4,6},{5,7},{10,8},{11,9},{8,1... | collective-permute-start | bytes 49160 | tf_op jit(solution)/shard_map/ppermute | solution.py:53
  64.5 0.0 collective-permute-start.15
  64.5 1.3 %collective-permute-start.13 = (f32[2,5,2,128]{3,2,1,0:T(2,128)S(1)}, f32[2,5,2,128]{3,2,1,0:T(2,128)S(1)}, u32[]{:S(2)}, u32[]{:S(2)}) collective-permute-start(f32[2,5,2,128]{3,2,1,0:T(2,128)S(1)} %get-tuple-element.61), channel_id=1, source_target_pairs={{3,0},{2,1},{1,2},{0,3},{7,4},{6,5},{5,6},{4,7},{11,8},{10,9},{9,1... | collective-permute-start | bytes 30728 | tf_op jit(solution)/shard_map/ppermute | solution.py:53
  65.9 1.8 %collective-permute-done.13.refs_3_ = f32[2,5,2,128]{3,2,1,0:T(2,128)S(1)} collective-permute-done((f32[2,5,2,128]{3,2,1,0:T(2,128)S(1)}, f32[2,5,2,128]{3,2,1,0:T(2,128)S(1)}, u32[]{:S(2)}, u32[]{:S(2)}) %collective-permute-start.13) | collective-permute-done | bytes 10272 | tf_op jit(solution)/shard_map/ppermute | solution.py:53
  67.6 0.0 collective-permute-done.14.refs_4_
  67.6 0.0 collective-permute-done.15.refs_5_
  67.6 11.2 %langevin_step.7 = (f32[4,3,4,128]{3,2,1,0:T(4,128)}, f32[4,3,4,128]{3,2,1,0:T(4,128)}, f32[2,4,8,128]{3,2,1,0:T(8,128)S(1)}, f32[8,128]{1,0:T(8,128)S(1)}) custom-call(s32[4,4,9]{2,1,0:T(4,128)S(1)} %copy-done.2, f32[1,4,4,8]{3,2,1,0:T(4,128)S(1)} %copy-done.1, f32[4,4,4,128]{3,2,1,0:T(4,128)S(1)} %get-tuple-element.60.refs_2_, ...), custom_call_target="tpu_custom_call" | custom-call | tf_op jit(solution)/shard_map/langevin_step/pallas_call | solution.py:580
  78.9 0.5 collective-permute-start.18
  79.4 1.2 %collective-permute-start.17 = (f32[8,128]{1,0:T(8,128)S(1)}, f32[8,128]{1,0:T(8,128)S(1)}, u32[]{:S(2)}, u32[]{:S(2)}) collective-permute-start(f32[8,128]{1,0:T(8,128)S(1)} %get-tuple-element.69.refs_2_), channel_id=1, source_target_pairs={{2,0},{3,1},{0,2},{1,3},{6,4},{7,5},{4,6},{5,7},{10,8},{11,9},{8,1... | collective-permute-start | bytes 12296 | tf_op jit(solution)/shard_map/ppermute | solution.py:53
  80.6 0.1 collective-permute-start.16
  80.7 0.0 collective-permute-done.18.refs_5_
  80.7 2.2 %collective-permute-done.17.refs_4_ = f32[8,128]{1,0:T(8,128)S(1)} collective-permute-done((f32[8,128]{1,0:T(8,128)S(1)}, f32[8,128]{1,0:T(8,128)S(1)}, u32[]{:S(2)}, u32[]{:S(2)}) %collective-permute-start.17) | collective-permute-done | bytes 4128 | tf_op jit(solution)/shard_map/ppermute | solution.py:53
  83.0 0.7 collective-permute-done.16.refs_3_
  83.6 1.4 %last_angles.1 = (f32[1,4,8]{2,1,0:T(4,128)}, f32[1,4,8]{2,1,0:T(4,128)}) custom-call(f32[1,4,4,8]{3,2,1,0:T(4,128)S(1)} %copy-done.1, f32[2,4,8,128]{3,2,1,0:T(8,128)S(1)} %get-tuple-element.68.refs_1_, f32[8,128]{1,0:T(8,128)S(1)} %get-tuple-element.69.refs_2_, f32[8,128]{1,0:T(8,128)S(1)} %collective-permute-done.16.refs_3_, ...), custom_call_target="tpu_custom_call" | custom-call | tf_op jit(solution)/shard_map/last_angles/pallas_call | solution.py:625
  (8 shorter events, 0.0 us)
Async XLA Ops:
  0.6 0.7 copy-start.11
  1.3 0.7 copy-start.4
  2.1 0.7 copy-start.5
  2.8 0.7 copy-start.12
  3.5 5.1 %copy-start.10 = (s32[8]{0:T(128)S(1)}, s32[8]{0:T(128)}, u32[]{:S(2)}) copy-start(s32[8]{0:T(128)} %slot_ref.3) | copy-start | bytes 100
  3.5 5.1 %collective-permute-start = (f32[25,4,128]{2,1,0:T(4,128)S(1)}, f32[25,4,128]{2,1,0:T(4,128)S(1)}, u32[]{:S(2)}, u32[]{:S(2)}) collective-permute-start(f32[25,4,128]{2,1,0:T(4,128)S(1)} %pack_walker.1.mine_ref.refs_0_), channel_id=1, source_target_pairs={{0,4},{4,0},{8,12},{12,8},{16,20},{20,16},{24,28},{28,24},{1,5},{5... | collective-permute-start | bytes 153608 | tf_op jit(solution)/shard_map/ppermute | solution.py:709
  8.6 9.5 %copy-start.6 = (f32[4,4,128]{2,1,0:T(4,128)S(1)}, f32[4,4,128]{2,1,0:T(4,128)}, u32[]{:S(2)}) copy-start(f32[4,4,128]{2,1,0:T(4,128)} %refs_5_.1) | copy-start | bytes 24580
  8.6 9.5 %copy-start.7 = (f32[4,4,128]{2,1,0:T(4,128)S(1)}, f32[4,4,128]{2,1,0:T(4,128)}, u32[]{:S(2)}) copy-start(f32[4,4,128]{2,1,0:T(4,128)} %refs_6_.1) | copy-start | bytes 24580
  8.6 9.5 %copy-start.8 = (s32[4,4,128]{2,1,0:T(4,128)S(1)}, s32[4,4,128]{2,1,0:T(4,128)}, u32[]{:S(2)}) copy-start(s32[4,4,128]{2,1,0:T(4,128)} %refs_7_.1) | copy-start | bytes 24580
  8.6 9.5 %copy-start.9 = (s32[4,4,128]{2,1,0:T(4,128)S(1)}, s32[4,4,128]{2,1,0:T(4,128)}, u32[]{:S(2)}) copy-start(s32[4,4,128]{2,1,0:T(4,128)} %refs_8_.2) | copy-start | bytes 24580
  9.3 6.7 %collective-permute-start.1 = (f32[25,4,128]{2,1,0:T(4,128)S(1)}, f32[25,4,128]{2,1,0:T(4,128)S(1)}, u32[]{:S(2)}, u32[]{:S(2)}) collective-permute-start(f32[25,4,128]{2,1,0:T(4,128)S(1)} %get-tuple-element.38), channel_id=1, source_target_pairs={{0,8},{4,12},{8,16},{12,20},{16,24},{20,28},{24,0},{28,4},{1,9},{5... | collective-permute-start | bytes 153608 | tf_op jit(solution)/shard_map/ppermute | solution.py:723
  11.4 5.1 %collective-permute-start.2 = (f32[25,4,128]{2,1,0:T(4,128)S(1)}, f32[25,4,128]{2,1,0:T(4,128)S(1)}, u32[]{:S(2)}, u32[]{:S(2)}) collective-permute-start(f32[25,4,128]{2,1,0:T(4,128)S(1)} %get-tuple-element.39), channel_id=1, source_target_pairs={{0,16},{4,20},{8,24},{12,28},{16,0},{20,4},{24,8},{28,12},{1,17},{... | collective-permute-start | bytes 153608 | tf_op jit(solution)/shard_map/ppermute | solution.py:723
  14.0 9.6 %copy-start = (f32[1,4,4,4,3,128]{5,3,4,2,1,0:T(4,128)S(1)}, f32[1,4,4,4,3,128]{5,3,4,2,1,0:T(4,128)}, u32[]{:S(2)}) copy-start(f32[1,4,4,4,3,128]{5,3,4,2,1,0:T(4,128)} %param.18) | copy-start | bytes 294916
  14.0 4.1 %collective-permute-start.3 = (f32[25,4,128]{2,1,0:T(4,128)S(1)}, f32[25,4,128]{2,1,0:T(4,128)S(1)}, u32[]{:S(2)}, u32[]{:S(2)}) collective-permute-start(f32[25,4,128]{2,1,0:T(4,128)S(1)} %get-tuple-element.40), channel_id=1, source_target_pairs={{0,24},{4,28},{8,0},{12,4},{16,8},{20,12},{24,16},{28,20},{1,25},{... | collective-permute-start | bytes 153608 | tf_op jit(solution)/shard_map/ppermute | solution.py:723
  18.1 5.4 %copy-start.2 = (s32[4,4,9]{2,1,0:T(4,128)S(1)}, s32[4,4,9]{2,1,0:T(4,128)}, u32[]{:S(2)}) copy-start(s32[4,4,9]{2,1,0:T(4,128)} %refs_0_.8) | copy-start | bytes 1732
  18.1 5.4 %copy-start.3 = (f32[4,4,128]{2,1,0:T(4,128)S(1)}, f32[4,4,128]{2,1,0:T(4,128)}, u32[]{:S(2)}) copy-start(f32[4,4,128]{2,1,0:T(4,128)} %refs_9_.5) | copy-start | bytes 24580
  18.8 4.8 %copy-start.1 = (f32[1,4,4,8]{3,2,1,0:T(4,128)S(1)}, f32[1,4,4,8]{3,2,1,0:T(4,128)}, u32[]{:S(2)}) copy-start(f32[1,4,4,8]{3,2,1,0:T(4,128)} %refs_0_.9) | copy-start | bytes 1540
  18.8 4.7 %collective-permute-start.5 = (f32[2,7,4,128]{3,2,1,0:T(4,128)S(1)}, f32[2,7,4,128]{3,2,1,0:T(4,128)S(1)}, u32[]{:S(2)}, u32[]{:S(2)}) collective-permute-start(f32[2,7,4,128]{3,2,1,0:T(4,128)S(1)} %get-tuple-element.43), channel_id=1, source_target_pairs={{2,0},{3,1},{0,2},{1,3},{6,4},{7,5},{4,6},{5,7},{10,8},{11,9},{8,1... | collective-permute-start | bytes 86024 | tf_op jit(solution)/shard_map/ppermute | solution.py:53
  20.4 3.2 %collective-permute-start.6 = (f32[4,7,2,128]{3,2,1,0:T(2,128)S(1)}, f32[4,7,2,128]{3,2,1,0:T(2,128)S(1)}, u32[]{:S(2)}, u32[]{:S(2)}) collective-permute-start(f32[4,7,2,128]{3,2,1,0:T(2,128)S(1)} %get-tuple-element.44), channel_id=1, source_target_pairs={{1,0},{0,1},{3,2},{2,3},{5,4},{4,5},{7,6},{6,7},{9,8},{8,9},{11,10... | collective-permute-start | bytes 86024 | tf_op jit(solution)/shard_map/ppermute | solution.py:53
  20.4 3.1 %collective-permute-start.4 = (f32[2,7,2,128]{3,2,1,0:T(2,128)S(1)}, f32[2,7,2,128]{3,2,1,0:T(2,128)S(1)}, u32[]{:S(2)}, u32[]{:S(2)}) collective-permute-start(f32[2,7,2,128]{3,2,1,0:T(2,128)S(1)} %get-tuple-element.42), channel_id=1, source_target_pairs={{3,0},{2,1},{1,2},{0,3},{7,4},{6,5},{5,6},{4,7},{11,8},{10,9},{9,1... | collective-permute-start | bytes 43016 | tf_op jit(solution)/shard_map/ppermute | solution.py:53
  34.1 4.0 %collective-permute-start.8 = (f32[2,4,4,128]{3,2,1,0:T(4,128)S(1)}, f32[2,4,4,128]{3,2,1,0:T(4,128)S(1)}, u32[]{:S(2)}, u32[]{:S(2)}) collective-permute-start(f32[2,4,4,128]{3,2,1,0:T(4,128)S(1)} %get-tuple-element.49), channel_id=1, source_target_pairs={{2,0},{3,1},{0,2},{1,3},{6,4},{7,5},{4,6},{5,7},{10,8},{11,9},{8,1... | collective-permute-start | bytes 49160 | tf_op jit(solution)/shard_map/ppermute | solution.py:53
  35.0 3.1 %collective-permute-start.9 = (f32[4,4,2,128]{3,2,1,0:T(2,128)S(1)}, f32[4,4,2,128]{3,2,1,0:T(2,128)S(1)}, u32[]{:S(2)}, u32[]{:S(2)}) collective-permute-start(f32[4,4,2,128]{3,2,1,0:T(2,128)S(1)} %get-tuple-element.50), channel_id=1, source_target_pairs={{1,0},{0,1},{3,2},{2,3},{5,4},{4,5},{7,6},{6,7},{9,8},{8,9},{11,10... | collective-permute-start | bytes 49160 | tf_op jit(solution)/shard_map/ppermute | solution.py:53
  35.0 3.1 %collective-permute-start.7 = (f32[2,5,2,128]{3,2,1,0:T(2,128)S(1)}, f32[2,5,2,128]{3,2,1,0:T(2,128)S(1)}, u32[]{:S(2)}, u32[]{:S(2)}) collective-permute-start(f32[2,5,2,128]{3,2,1,0:T(2,128)S(1)} %get-tuple-element.48), channel_id=1, source_target_pairs={{3,0},{2,1},{1,2},{0,3},{7,4},{6,5},{5,6},{4,7},{11,8},{10,9},{9,1... | collective-permute-start | bytes 30728 | tf_op jit(solution)/shard_map/ppermute | solution.py:53
  48.6 4.6 %collective-permute-start.11 = (f32[2,4,4,128]{3,2,1,0:T(4,128)S(1)}, f32[2,4,4,128]{3,2,1,0:T(4,128)S(1)}, u32[]{:S(2)}, u32[]{:S(2)}) collective-permute-start(f32[2,4,4,128]{3,2,1,0:T(4,128)S(1)} %get-tuple-element.56), channel_id=1, source_target_pairs={{2,0},{3,1},{0,2},{1,3},{6,4},{7,5},{4,6},{5,7},{10,8},{11,9},{8,1... | collective-permute-start | bytes 49160 | tf_op jit(solution)/shard_map/ppermute | solution.py:53
  50.1 3.1 %collective-permute-start.12 = (f32[4,4,2,128]{3,2,1,0:T(2,128)S(1)}, f32[4,4,2,128]{3,2,1,0:T(2,128)S(1)}, u32[]{:S(2)}, u32[]{:S(2)}) collective-permute-start(f32[4,4,2,128]{3,2,1,0:T(2,128)S(1)} %get-tuple-element.57), channel_id=1, source_target_pairs={{1,0},{0,1},{3,2},{2,3},{5,4},{4,5},{7,6},{6,7},{9,8},{8,9},{11,10... | collective-permute-start | bytes 49160 | tf_op jit(solution)/shard_map/ppermute | solution.py:53
  50.1 3.1 %collective-permute-start.10 = (f32[2,5,2,128]{3,2,1,0:T(2,128)S(1)}, f32[2,5,2,128]{3,2,1,0:T(2,128)S(1)}, u32[]{:S(2)}, u32[]{:S(2)}) collective-permute-start(f32[2,5,2,128]{3,2,1,0:T(2,128)S(1)} %get-tuple-element.55), channel_id=1, source_target_pairs={{3,0},{2,1},{1,2},{0,3},{7,4},{6,5},{5,6},{4,7},{11,8},{10,9},{9,1... | collective-permute-start | bytes 30728 | tf_op jit(solution)/shard_map/ppermute | solution.py:53
  63.7 4.0 %collective-permute-start.14 = (f32[2,4,4,128]{3,2,1,0:T(4,128)S(1)}, f32[2,4,4,128]{3,2,1,0:T(4,128)S(1)}, u32[]{:S(2)}, u32[]{:S(2)}) collective-permute-start(f32[2,4,4,128]{3,2,1,0:T(4,128)S(1)} %get-tuple-element.62), channel_id=1, source_target_pairs={{2,0},{3,1},{0,2},{1,3},{6,4},{7,5},{4,6},{5,7},{10,8},{11,9},{8,1... | collective-permute-start | bytes 49160 | tf_op jit(solution)/shard_map/ppermute | solution.py:53
  64.5 3.1 %collective-permute-start.15 = (f32[4,4,2,128]{3,2,1,0:T(2,128)S(1)}, f32[4,4,2,128]{3,2,1,0:T(2,128)S(1)}, u32[]{:S(2)}, u32[]{:S(2)}) collective-permute-start(f32[4,4,2,128]{3,2,1,0:T(2,128)S(1)} %get-tuple-element.63), channel_id=1, source_target_pairs={{1,0},{0,1},{3,2},{2,3},{5,4},{4,5},{7,6},{6,7},{9,8},{8,9},{11,10... | collective-permute-start | bytes 49160 | tf_op jit(solution)/shard_map/ppermute | solution.py:53
  64.5 3.1 %collective-permute-start.13 = (f32[2,5,2,128]{3,2,1,0:T(2,128)S(1)}, f32[2,5,2,128]{3,2,1,0:T(2,128)S(1)}, u32[]{:S(2)}, u32[]{:S(2)}) collective-permute-start(f32[2,5,2,128]{3,2,1,0:T(2,128)S(1)} %get-tuple-element.61), channel_id=1, source_target_pairs={{3,0},{2,1},{1,2},{0,3},{7,4},{6,5},{5,6},{4,7},{11,8},{10,9},{9,1... | collective-permute-start | bytes 30728 | tf_op jit(solution)/shard_map/ppermute | solution.py:53
  78.9 1.9 %collective-permute-start.18 = (f32[8,128]{1,0:T(8,128)S(1)}, f32[8,128]{1,0:T(8,128)S(1)}, u32[]{:S(2)}, u32[]{:S(2)}) collective-permute-start(f32[8,128]{1,0:T(8,128)S(1)} %get-tuple-element.69.refs_2_), channel_id=1, source_target_pairs={{1,0},{0,1},{3,2},{2,3},{5,4},{4,5},{7,6},{6,7},{9,8},{8,9},{11,10... | collective-permute-start | bytes 12296 | tf_op jit(solution)/shard_map/ppermute | solution.py:53
  79.4 3.6 %collective-permute-start.17 = (f32[8,128]{1,0:T(8,128)S(1)}, f32[8,128]{1,0:T(8,128)S(1)}, u32[]{:S(2)}, u32[]{:S(2)}) collective-permute-start(f32[8,128]{1,0:T(8,128)S(1)} %get-tuple-element.69.refs_2_), channel_id=1, source_target_pairs={{2,0},{3,1},{0,2},{1,3},{6,4},{7,5},{4,6},{5,7},{10,8},{11,9},{8,1... | collective-permute-start | bytes 12296 | tf_op jit(solution)/shard_map/ppermute | solution.py:53
  80.6 3.0 %collective-permute-start.16 = (f32[8,128]{1,0:T(8,128)S(1)}, f32[8,128]{1,0:T(8,128)S(1)}, u32[]{:S(2)}, u32[]{:S(2)}) collective-permute-start(f32[8,128]{1,0:T(8,128)S(1)} %get-tuple-element.69.refs_2_), channel_id=1, source_target_pairs={{3,0},{2,1},{1,2},{0,3},{7,4},{6,5},{5,6},{4,7},{11,8},{10,9},{9,1... | collective-permute-start | bytes 12296 | tf_op jit(solution)/shard_map/ppermute | solution.py:53

commit v5 on v4

--- a/solution.py
+++ b/solution.py
@@ -117,8 +117,10 @@
 
 
 def lane_column(row, first, sub_iota):
-    lane = lax.broadcasted_iota(jnp.int32, sub_iota.shape, 1)
-    hit = lane == lax.broadcasted_iota(jnp.int32, sub_iota.shape, 0) + first
+    shape = (sub_iota.shape[0], row.shape[1])
+    hit = lax.broadcasted_iota(jnp.int32, shape, 1) == (
+        lax.broadcasted_iota(jnp.int32, shape, 0) + first
+    )
     return jnp.broadcast_to(
         jnp.sum(jnp.where(hit, row, 0.0), axis=1, keepdims=True), sub_iota.shape
     )
@@ -130,13 +132,12 @@
 
 
 def noise_table(anoise_ref, moment, sub_iota):
-    tables = []
-    for site in range(NSITE):
-        table = jnp.zeros_like(sub_iota)
-        for sub in range(NSUB):
-            table = jnp.where(sub_iota == float(sub), anoise_ref[0, moment, site, sub], table)
-        tables.append(table)
-    return jnp.stack(tables)
+    return jnp.stack(
+        [
+            lane_column(anoise_ref[0, moment, site : site + 1, :], 0, sub_iota)
+            for site in range(NSITE)
+        ]
+    )
 
 
 def packed_rows(ref):
@@ -160,7 +161,7 @@
         taken, refs[:n] = refs[:n], []
         return taken
 
-    part_ref, anoise_ref = take(2)
+    part_hbm, anoise_ref = take(2)
     coord_refs = take(nb)
     (stat_ref,) = take(1) if moment > 0 else (None,)
     (tot_ref,) = take(1) if moment > 0 and not cfg["covered"] else (None,)
@@ -173,6 +174,9 @@
     (stato_ref,) = take(1) if moment == 0 else (None,)
     (sumo_ref,) = take(1) if last else (None,)
     pool_ref, col_ref, fcol_ref, sum_ref, feat_ref, wide_ref, rhs_ref, coef_ref, off_ref, io_ref = take(10)
+    part_ref, part_sem = take(2)
+    part_copy = pltpu.make_async_copy(part_hbm, part_ref, part_sem)
+    part_copy.start()
 
     sub_iota = lax.broadcasted_iota(jnp.int32, (NSUB, lanes), 0).astype(jnp.float32)
     if moment == 0:
@@ -252,6 +256,8 @@
     ins = io_ref
     outs = (io_ref, sum_ref)
     near = cfg["roomy"] & (stray < REACH)
+
+    part_copy.wait()
 
     @pl.when(near)
     def _():
@@ -551,11 +557,10 @@
     rows_x, rows_y = cfg["rows_x"], cfg["rows_y"]
     last = moment == STEPS - 1
     vmem = pl.BlockSpec(memory_space=pltpu.VMEM)
-    smem = pl.BlockSpec(memory_space=pltpu.SMEM)
     noise_spec = pl.BlockSpec(
         (1, 1, rows_x, 3, rows_y, lanes), lambda i: (0, moment, 0, 0, 0, 0)
     )
-    args = [(parts, smem), (anoise, smem)] + [(block, vmem) for block in blocks]
+    args = [(parts, pl.BlockSpec(memory_space=pltpu.HBM)), (anoise, vmem)] + [(block, vmem) for block in blocks]
     if moment > 0:
         args.append((stat, vmem))
     if totals is not None:
@@ -594,6 +599,8 @@
             pltpu.VMEM((pool + 1, 32, 2 * lanes), jnp.bfloat16),
             pltpu.SMEM((2, pool), jnp.float32),
             pltpu.VMEM((tiles, 8, lanes), jnp.float32),
+            pltpu.SMEM(parts.shape, jnp.int32),
+            pltpu.SemaphoreType.DMA(()),
         ],
         compiler_params=pltpu.CompilerParams(vmem_limit_bytes=4 * SMALL),
         name="langevin_step",
@@ -601,9 +608,15 @@
 
 
 def angle_kernel(cfg, *refs):
-    anoise_ref, ang_ref = refs[:2]
-    tot_refs, (theta_ref, speed_ref) = refs[2:-2], refs[-2:]
+    anoise_ref, ang_ref, disp_ref, vel_ref = refs[:4]
+    *tot_refs, theta_ref, speed_ref, dispo_ref, velo_ref, sems = refs[4:]
     lanes = cfg["lanes"]
+    copies = [
+        pltpu.make_async_copy(disp_ref, dispo_ref, sems.at[0]),
+        pltpu.make_async_copy(vel_ref, velo_ref, sems.at[1]),
+    ]
+    for copy in copies:
+        copy.start()
     sub_iota = lax.broadcasted_iota(jnp.int32, (NSUB, lanes), 0).astype(jnp.float32)
     packed = packed_totals([ref[...] for ref in tot_refs])
     results = angle_step(
@@ -617,25 +630,30 @@
         for site in range(NSITE):
             row = jnp.sum(jnp.where(hit, result[site], 0.0), axis=0, keepdims=True)
             ref[0, site : site + 1, :] = row[:, 0:NSUB]
-
-
-def angle_call(cfg, anoise, ang, totals):
+    for copy in copies:
+        copy.wait()
+
+
+def angle_call(cfg, anoise, ang, disp, vel, totals):
     vmem = pl.BlockSpec(memory_space=pltpu.VMEM)
+    hbm = pl.BlockSpec(memory_space=pltpu.HBM)
     shape = jax.ShapeDtypeStruct((1, NSITE, NSUB), jnp.float32)
+    vectors = jax.ShapeDtypeStruct(disp.shape, jnp.float32)
     return pl.pallas_call(
         functools.partial(angle_kernel, cfg),
-        out_shape=(shape, shape),
-        in_specs=[pl.BlockSpec(memory_space=pltpu.SMEM)] + [vmem] * (1 + len(totals)),
-        out_specs=(vmem, vmem),
+        out_shape=(shape, shape, vectors, vectors),
+        in_specs=[vmem] * (4 + len(totals)),
+        out_specs=(vmem, vmem, hbm, hbm),
+        scratch_shapes=[pltpu.SemaphoreType.DMA((2,))],
         name="last_angles",
         compiler_params=pltpu.CompilerParams(vmem_limit_bytes=SMALL),
-    )(anoise, ang, *totals)
+    )(anoise, ang, disp, vel, *totals)
 
 
 def send_kernel(width, sets, slot_ref, mine_ref, other_ref, *out_refs):
     me = lax.axis_index("walker")
     for k, ref in enumerate(out_refs, 1):
-        wanted = slot_ref[lax.rem(me + k * width, width * sets)]
+        wanted = slot_of(slot_ref, lax.rem(me + k * width, width * sets))
         own = lax.rem(wanted, width) == lax.rem(me, width)
 
         @pl.when(own)
@@ -653,7 +671,7 @@
     *pay_refs, vel_ref, ang_ref = refs[sets + 5 :]
     rows_x = vel_ref.shape[0]
     me = lax.axis_index("walker")
-    source = slot_ref[me]
+    source = slot_of(slot_ref, me)
     hop = lax.rem(me // width - source // width + sets, sets)
     away = (lax.rem(source, width) != lax.rem(me, width)).astype(jnp.int32)
     choice = jnp.where(hop > 0, hop + 1, away)
@@ -679,14 +697,32 @@
                 ref[ri, :, cj : cj + 1, :] = own_ref[i, :, j : j + 1, :]
 
 
-def pack_kernel(pos_ref, vel_ref, theta_ref, speed_ref, out_ref):
+def pack_kernel(pos_ref, vel_ref, theta_ref, speed_ref, out_ref, angle_ref, sems):
     rows_x = pos_ref.shape[0]
+    copies = [
+        pltpu.make_async_copy(theta_ref.at[0], angle_ref.at[0], sems.at[0]),
+        pltpu.make_async_copy(speed_ref.at[0], angle_ref.at[1], sems.at[1]),
+    ]
     for i in range(rows_x):
-        out_ref[6 * i : 6 * i + 3] = pos_ref[i]
-        out_ref[6 * i + 3 : 6 * i + 6] = vel_ref[i]
+        for kind, ref in enumerate((pos_ref, vel_ref)):
+            copies.append(
+                pltpu.make_async_copy(
+                    ref.at[i], out_ref.at[pl.ds(6 * i + 3 * kind, 3)], sems.at[2 + 2 * i + kind]
+                )
+            )
+    for copy in copies:
+        copy.start()
     out_ref[6 * rows_x] = jnp.zeros(out_ref.shape[1:], jnp.float32)
-    out_ref[6 * rows_x, :, 0:NSUB] = theta_ref[0]
-    out_ref[6 * rows_x, :, NSUB : 2 * NSUB] = speed_ref[0]
+    for copy in copies:
+        copy.wait()
+    for kind in range(2):
+        out_ref[6 * rows_x, :, kind * NSUB : (kind + 1) * NSUB] = angle_ref[kind]
+
+
+def slot_of(slot_ref, index):
+    slots = slot_ref[...].astype(jnp.float32)
+    lane = lax.broadcasted_iota(jnp.int32, slots.shape, 1)
+    return jnp.sum(jnp.where(lane == index, slots, 0.0)).astype(jnp.int32)
 
 
 def clone(cfg, positions, velocities, theta, speed, source_slot, charges, strengths, atom_site, atom_sub):
@@ -695,15 +731,19 @@
     sets = peers // width
     rows_x, rows_y, lanes = charges.shape
     vmem = pl.BlockSpec(memory_space=pltpu.VMEM)
-    smem = pl.BlockSpec(memory_space=pltpu.SMEM)
     message = pl.pallas_call(
         pack_kernel,
         out_shape=jax.ShapeDtypeStruct((6 * rows_x + 1, rows_y, lanes), jnp.float32),
-        in_specs=[vmem] * 4,
+        in_specs=[pl.BlockSpec(memory_space=pltpu.HBM)] * 4,
         out_specs=vmem,
+        scratch_shapes=[
+            pltpu.VMEM((2, NSITE, NSUB), jnp.float32),
+            pltpu.SemaphoreType.DMA((2 + 2 * rows_x,)),
+        ],
         name="pack_walker",
         compiler_params=pltpu.CompilerParams(vmem_limit_bytes=SMALL),
     )(positions, velocities, theta, speed)
+    source_slot = source_slot.reshape(1, peers)
     other = message
     if width == 2:
         other = lax.ppermute(message, "walker", [(w, w ^ 1) for w in range(peers)])
@@ -713,7 +753,7 @@
         sent = pl.pallas_call(
             functools.partial(send_kernel, width, sets),
             out_shape=(shape,) * (sets - 1),
-            in_specs=[smem, vmem, vmem],
+            in_specs=[vmem, vmem, vmem],
             out_specs=(vmem,) * (sets - 1),
             name="choose_sent",
         compiler_params=pltpu.CompilerParams(vmem_limit_bytes=SMALL),
@@ -729,7 +769,7 @@
     return pl.pallas_call(
         functools.partial(pick_kernel, width, sets, cfg["windows"]),
         out_shape=tuple(jax.ShapeDtypeStruct(shape, jnp.float32) for shape in shapes),
-        in_specs=[smem] + [vmem] * (len(blocks) + 4),
+        in_specs=[vmem] * (len(blocks) + 5),
         out_specs=(vmem,) * len(shapes),
         name="choose_received",
         compiler_params=pltpu.CompilerParams(vmem_limit_bytes=SMALL),
@@ -752,7 +792,7 @@
         windows=[window(offset, rows_x, rows_y) for offset in [(0, 0)] + offsets],
         sources=pool_sources(rows_x, rows_y, count_x, count_y, offsets),
         depth=128,
-        pool_group=next(g for g in (12, 6, 4, 3, 2, 1) if (rows_x + 2) * (rows_y + 2) % g == 0),
+        pool_group=next(g for g in (36, 6, 4, 3, 2, 1) if (rows_x + 2) * (rows_y + 2) % g == 0),
         roomy=min(rows_x * count_x, rows_y * count_y) >= 8,
         box_x=float(rows_x * count_x),
         box_y=float(rows_y * count_y),
@@ -810,9 +850,9 @@
         totals = gather_blocks([packed] * cfg["blocks"])
     else:
         totals = [lax.psum(packed, ("gx", "gy"))]
-    theta, theta_speed = angle_call(cfg, theta_noise, ang, totals)
+    theta, theta_speed, disp, vel = angle_call(cfg, theta_noise, ang, pays[0], vel, totals)
     back = lambda value: value.transpose(0, 2, 1, 3)[None]
-    return back(pays[0]), back(vel), theta, theta_speed
+    return back(disp), back(vel), theta, theta_speed
 
 
 def solution(mesh):

time: 85.3 us -> 81.1 us (0.951)
  Pallas kernels: 45.4 us -> 40.9 us
    pallas_call x4, Pallas kernels: 42.7 us -> 38.8 us  [step_call(): pl.pallas_call(functools.partial(step_kernel, cfg, moment), grid=(1,), ou...]
where the time goes in v5:
time: 81.1 us; the launch traced here: 80.8 us
  Pallas kernels  40.9 us (50%)
  starting transfers between devices  19.9 us (25%)
  waiting for transfers between devices  16.2 us (20%)
  local copies, waits for them, and re-layouts  2.88 us (4%)
  between operations  0.97 us (1%)
    pallas_call x4, Pallas kernels, step_call(): pl.pallas_call(functools.partial(step_kernel, cfg, moment), grid=(1,), ou...  38.8 us
    ppermute x15, waiting for transfers between devices, shifted(): return lax.ppermute(value, ('gx', 'gy'), pairs)  11.3 us
    ppermute x15, starting transfers between devices, shifted(): return lax.ppermute(value, ('gx', 'gy'), pairs)  10.8 us
    ppermute x3, starting transfers between devices, clone(): lax.ppermute(value, 'walker', [(w, (w + k * width) % peers) for w in rang...  6.1 us
    ppermute x1, starting transfers between devices, clone(): other = lax.ppermute(message, 'walker', [(w, w ^ 1) for w in range(peers)])  3.03 us
    unnamed x26, local copies, waits for them, and re-layouts  2.88 us
    ppermute x3, waiting for transfers between devices, clone(): lax.ppermute(value, 'walker', [(w, (w + k * width) % peers) for w in rang...  2.76 us
    ppermute x1, waiting for transfers between devices, clone(): other = lax.ppermute(message, 'walker', [(w, w ^ 1) for w in range(peers)])  2.09 us
  transfers between devices with their start and end apart: 19, of which 10 were waited for; matrix products, arithmetic and copies ran while one was open for 0% of the time, Pallas kernels for 0%

profile of v5, /device:TPU:0, one launch (start us, length us, event | category | flops | bytes accessed | tf_op | source)
XLA Modules:
  0.0 80.8 jit_solution(6408950114792620320)
XLA Ops:
  0.6 0.0 copy-start.11
  0.6 0.7 copy-done.11
  1.3 0.7 copy-done.4
  2.1 0.7 copy-done.5
  2.8 0.7 copy-done.12
  3.5 0.2 pack_walker.1.mine_ref.refs_0_
  3.7 0.0 copy-start.10
  3.7 3.0 %collective-permute-start = (f32[25,4,128]{2,1,0:T(4,128)S(1)}, f32[25,4,128]{2,1,0:T(4,128)S(1)}, u32[]{:S(2)}, u32[]{:S(2)}) collective-permute-start(f32[25,4,128]{2,1,0:T(4,128)S(1)} %pack_walker.1.mine_ref.refs_0_), channel_id=1, source_target_pairs={{0,4},{4,0},{8,12},{12,8},{16,20},{20,16},{24,28},{28,24},{1,5},{5... | collective-permute-start | bytes 153608 | tf_op jit(solution)/shard_map/ppermute | solution.py:749
  6.7 2.1 %collective-permute-done.other_ref.refs_1_ = f32[25,4,128]{2,1,0:T(4,128)S(1)} collective-permute-done((f32[25,4,128]{2,1,0:T(4,128)S(1)}, f32[25,4,128]{2,1,0:T(4,128)S(1)}, u32[]{:S(2)}, u32[]{:S(2)}) %collective-permute-start) | collective-permute-done | bytes 51232 | tf_op jit(solution)/shard_map/ppermute | solution.py:749
  8.8 0.0 copy-done.10
  8.8 0.0 copy-start.9
  8.9 0.4 choose_sent.1
  9.3 2.2 %collective-permute-start.1 = (f32[25,4,128]{2,1,0:T(4,128)S(1)}, f32[25,4,128]{2,1,0:T(4,128)S(1)}, u32[]{:S(2)}, u32[]{:S(2)}) collective-permute-start(f32[25,4,128]{2,1,0:T(4,128)S(1)} %get-tuple-element.40), channel_id=1, source_target_pairs={{0,8},{4,12},{8,16},{12,20},{16,24},{20,28},{24,0},{28,4},{1,9},{5... | collective-permute-start | bytes 153608 | tf_op jit(solution)/shard_map/ppermute | solution.py:763
  11.4 2.6 %collective-permute-start.2 = (f32[25,4,128]{2,1,0:T(4,128)S(1)}, f32[25,4,128]{2,1,0:T(4,128)S(1)}, u32[]{:S(2)}, u32[]{:S(2)}) collective-permute-start(f32[25,4,128]{2,1,0:T(4,128)S(1)} %get-tuple-element.41), channel_id=1, source_target_pairs={{0,16},{4,20},{8,24},{12,28},{16,0},{20,4},{24,8},{28,12},{1,17},{... | collective-permute-start | bytes 153608 | tf_op jit(solution)/shard_map/ppermute | solution.py:763
  14.0 1.3 %collective-permute-start.3 = (f32[25,4,128]{2,1,0:T(4,128)S(1)}, f32[25,4,128]{2,1,0:T(4,128)S(1)}, u32[]{:S(2)}, u32[]{:S(2)}) collective-permute-start(f32[25,4,128]{2,1,0:T(4,128)S(1)} %get-tuple-element.42), channel_id=1, source_target_pairs={{0,24},{4,28},{8,0},{12,4},{16,8},{20,12},{24,16},{28,20},{1,25},{... | collective-permute-start | bytes 153608 | tf_op jit(solution)/shard_map/ppermute | solution.py:763
  15.4 0.6 collective-permute-done.1.refs_2_
  16.0 0.5 collective-permute-done.2.refs_3_
  16.5 1.6 %collective-permute-done.3.refs_4_ = f32[25,4,128]{2,1,0:T(4,128)S(1)} collective-permute-done((f32[25,4,128]{2,1,0:T(4,128)S(1)}, f32[25,4,128]{2,1,0:T(4,128)S(1)}, u32[]{:S(2)}, u32[]{:S(2)}) %collective-permute-start.3) | collective-permute-done | bytes 51232 | tf_op jit(solution)/shard_map/ppermute | solution.py:763
  18.1 0.0 copy-done.6
  18.1 0.0 copy-done.7
  18.1 0.0 copy-done.8
  18.2 0.0 copy-done.9
  18.2 0.0 copy-start.2
  18.2 0.0 copy-start.3
  18.2 0.2 choose_received.1
  18.4 0.0 copy-start.1
  18.4 1.6 %collective-permute-start.5 = (f32[2,7,4,128]{3,2,1,0:T(4,128)S(1)}, f32[2,7,4,128]{3,2,1,0:T(4,128)S(1)}, u32[]{:S(2)}, u32[]{:S(2)}) collective-permute-start(f32[2,7,4,128]{3,2,1,0:T(4,128)S(1)} %get-tuple-element.45), channel_id=1, source_target_pairs={{2,0},{3,1},{0,2},{1,3},{6,4},{7,5},{4,6},{5,7},{10,8},{11,9},{8,1... | collective-permute-start | bytes 86024 | tf_op jit(solution)/shard_map/ppermute | solution.py:53
  20.0 0.0 collective-permute-start.6
  20.0 0.6 collective-permute-start.4
  20.6 2.5 %collective-permute-done.4.refs_3_ = f32[2,7,2,128]{3,2,1,0:T(2,128)S(1)} collective-permute-done((f32[2,7,2,128]{3,2,1,0:T(2,128)S(1)}, f32[2,7,2,128]{3,2,1,0:T(2,128)S(1)}, u32[]{:S(2)}, u32[]{:S(2)}) %collective-permute-start.4) | collective-permute-done | bytes 14368 | tf_op jit(solution)/shard_map/ppermute | solution.py:53
  23.1 0.0 collective-permute-done.5.refs_4_
  23.1 0.0 collective-permute-done.6.refs_5_
  23.1 0.0 copy-done
  23.2 0.0 copy-done.2
  23.2 0.0 copy-done.3
  23.2 9.7 %langevin_step.4 = (f32[4,4,4,128]{3,2,1,0:T(4,128)S(1)}, f32[2,5,2,128]{3,2,1,0:T(2,128)S(1)}, f32[2,4,4,128]{3,2,1,0:T(4,128)S(1)}, f32[4,4,2,128]{3,2,1,0:T(2...) custom-call(s32[4,4,9]{2,1,0:T(4,128)S(1)} %copy-done.2, ...), custom_call_target="tpu_custom_call" | custom-call | tf_op jit(solution)/shard_map/langevin_step/pallas_call | solution.py:585
  32.9 0.9 %collective-permute-start.8 = (f32[2,4,4,128]{3,2,1,0:T(4,128)S(1)}, f32[2,4,4,128]{3,2,1,0:T(4,128)S(1)}, u32[]{:S(2)}, u32[]{:S(2)}) collective-permute-start(f32[2,4,4,128]{3,2,1,0:T(4,128)S(1)} %get-tuple-element.51), channel_id=1, source_target_pairs={{2,0},{3,1},{0,2},{1,3},{6,4},{7,5},{4,6},{5,7},{10,8},{11,9},{8,1... | collective-permute-start | bytes 49160 | tf_op jit(solution)/shard_map/ppermute | solution.py:53
  33.7 0.0 collective-permute-start.9
  33.7 1.3 %collective-permute-start.7 = (f32[2,5,2,128]{3,2,1,0:T(2,128)S(1)}, f32[2,5,2,128]{3,2,1,0:T(2,128)S(1)}, u32[]{:S(2)}, u32[]{:S(2)}) collective-permute-start(f32[2,5,2,128]{3,2,1,0:T(2,128)S(1)} %get-tuple-element.50), channel_id=1, source_target_pairs={{3,0},{2,1},{1,2},{0,3},{7,4},{6,5},{5,6},{4,7},{11,8},{10,9},{9,1... | collective-permute-start | bytes 30728 | tf_op jit(solution)/shard_map/ppermute | solution.py:53
  35.1 1.8 %collective-permute-done.7.refs_3_ = f32[2,5,2,128]{3,2,1,0:T(2,128)S(1)} collective-permute-done((f32[2,5,2,128]{3,2,1,0:T(2,128)S(1)}, f32[2,5,2,128]{3,2,1,0:T(2,128)S(1)}, u32[]{:S(2)}, u32[]{:S(2)}) %collective-permute-start.7) | collective-permute-done | bytes 10272 | tf_op jit(solution)/shard_map/ppermute | solution.py:53
  36.8 0.0 collective-permute-done.8.refs_4_
  36.8 0.0 collective-permute-done.9.refs_5_
  36.8 9.7 %langevin_step.5 = (f32[4,4,4,128]{3,2,1,0:T(4,128)S(1)}, f32[2,5,2,128]{3,2,1,0:T(2,128)S(1)}, f32[2,4,4,128]{3,2,1,0:T(4,128)S(1)}, f32[4,4,2,128]{3,2,1,0:T(2...) custom-call(s32[4,4,9]{2,1,0:T(4,128)S(1)} %copy-done.2, f32[1,4,4,8]{3,2,1,0:T(4,128)S(1)} %copy-done.1, ...), custom_call_target="tpu_custom_call" | custom-call | tf_op jit(solution)/shard_map/langevin_step/pallas_call | solution.py:585
  46.5 1.5 %collective-permute-start.11 = (f32[2,4,4,128]{3,2,1,0:T(4,128)S(1)}, f32[2,4,4,128]{3,2,1,0:T(4,128)S(1)}, u32[]{:S(2)}, u32[]{:S(2)}) collective-permute-start(f32[2,4,4,128]{3,2,1,0:T(4,128)S(1)} %get-tuple-element.58), channel_id=1, source_target_pairs={{2,0},{3,1},{0,2},{1,3},{6,4},{7,5},{4,6},{5,7},{10,8},{11,9},{8,1... | collective-permute-start | bytes 49160 | tf_op jit(solution)/shard_map/ppermute | solution.py:53
  48.0 0.0 collective-permute-start.12
  48.0 0.7 collective-permute-start.10
  48.7 2.4 %collective-permute-done.10.refs_3_ = f32[2,5,2,128]{3,2,1,0:T(2,128)S(1)} collective-permute-done((f32[2,5,2,128]{3,2,1,0:T(2,128)S(1)}, f32[2,5,2,128]{3,2,1,0:T(2,128)S(1)}, u32[]{:S(2)}, u32[]{:S(2)}) %collective-permute-start.10) | collective-permute-done | bytes 10272 | tf_op jit(solution)/shard_map/ppermute | solution.py:53
  51.1 0.0 collective-permute-done.11.refs_4_
  51.1 0.0 collective-permute-done.12.refs_5_
  51.1 9.7 %langevin_step.6 = (f32[4,4,4,128]{3,2,1,0:T(4,128)S(1)}, f32[2,5,2,128]{3,2,1,0:T(2,128)S(1)}, f32[2,4,4,128]{3,2,1,0:T(4,128)S(1)}, f32[4,4,2,128]{3,2,1,0:T(2...) custom-call(s32[4,4,9]{2,1,0:T(4,128)S(1)} %copy-done.2, f32[1,4,4,8]{3,2,1,0:T(4,128)S(1)} %copy-done.1, ...), custom_call_target="tpu_custom_call" | custom-call | tf_op jit(solution)/shard_map/langevin_step/pallas_call | solution.py:585
  60.8 0.9 %collective-permute-start.14 = (f32[2,4,4,128]{3,2,1,0:T(4,128)S(1)}, f32[2,4,4,128]{3,2,1,0:T(4,128)S(1)}, u32[]{:S(2)}, u32[]{:S(2)}) collective-permute-start(f32[2,4,4,128]{3,2,1,0:T(4,128)S(1)} %get-tuple-element.64), channel_id=1, source_target_pairs={{2,0},{3,1},{0,2},{1,3},{6,4},{7,5},{4,6},{5,7},{10,8},{11,9},{8,1... | collective-permute-start | bytes 49160 | tf_op jit(solution)/shard_map/ppermute | solution.py:53
  61.7 0.0 collective-permute-start.15
  61.7 1.3 %collective-permute-start.13 = (f32[2,5,2,128]{3,2,1,0:T(2,128)S(1)}, f32[2,5,2,128]{3,2,1,0:T(2,128)S(1)}, u32[]{:S(2)}, u32[]{:S(2)}) collective-permute-start(f32[2,5,2,128]{3,2,1,0:T(2,128)S(1)} %get-tuple-element.63), channel_id=1, source_target_pairs={{3,0},{2,1},{1,2},{0,3},{7,4},{6,5},{5,6},{4,7},{11,8},{10,9},{9,1... | collective-permute-start | bytes 30728 | tf_op jit(solution)/shard_map/ppermute | solution.py:53
  63.0 1.8 %collective-permute-done.13.refs_3_ = f32[2,5,2,128]{3,2,1,0:T(2,128)S(1)} collective-permute-done((f32[2,5,2,128]{3,2,1,0:T(2,128)S(1)}, f32[2,5,2,128]{3,2,1,0:T(2,128)S(1)}, u32[]{:S(2)}, u32[]{:S(2)}) %collective-permute-start.13) | collective-permute-done | bytes 10272 | tf_op jit(solution)/shard_map/ppermute | solution.py:53
  64.8 0.0 collective-permute-done.14.refs_4_
  64.8 0.0 collective-permute-done.15.refs_5_
  64.8 9.8 %langevin_step.7 = (f32[4,3,4,128]{3,2,1,0:T(4,128)S(1)}, f32[4,3,4,128]{3,2,1,0:T(4,128)S(1)}, f32[2,4,8,128]{3,2,1,0:T(8,128)S(1)}, f32[8,128]{1,0:T(8,128)S(1)}) custom-call(s32[4,4,9]{2,1,0:T(4,128)S(1)} %copy-done.2, f32[1,4,4,8]{3,2,1,0:T(4,128)S(1)} %copy-done.1, f32[4,4,4,128]{3,2,1,0:T(4,128)S(1)} %get-tuple-element.62.refs_2_, ...), custom_call_target="tpu_custom_call" | custom-call | tf_op jit(solution)/shard_map/langevin_step/pallas_call | solution.py:585
  74.6 0.6 collective-permute-start.18
  75.2 1.2 %collective-permute-start.17 = (f32[8,128]{1,0:T(8,128)S(1)}, f32[8,128]{1,0:T(8,128)S(1)}, u32[]{:S(2)}, u32[]{:S(2)}) collective-permute-start(f32[8,128]{1,0:T(8,128)S(1)} %get-tuple-element.71.refs_4_), channel_id=1, source_target_pairs={{2,0},{3,1},{0,2},{1,3},{6,4},{7,5},{4,6},{5,7},{10,8},{11,9},{8,1... | collective-permute-start | bytes 12296 | tf_op jit(solution)/shard_map/ppermute | solution.py:53
  76.4 0.2 collective-permute-start.16
  76.6 0.0 collective-permute-done.18.refs_7_
  76.6 2.2 %collective-permute-done.17.refs_6_ = f32[8,128]{1,0:T(8,128)S(1)} collective-permute-done((f32[8,128]{1,0:T(8,128)S(1)}, f32[8,128]{1,0:T(8,128)S(1)}, u32[]{:S(2)}, u32[]{:S(2)}) %collective-permute-start.17) | collective-permute-done | bytes 4128 | tf_op jit(solution)/shard_map/ppermute | solution.py:53
  78.8 0.6 collective-permute-done.16.refs_5_
  79.5 1.2 %last_angles.1 = (f32[1,4,8]{2,1,0:T(4,128)}, f32[1,4,8]{2,1,0:T(4,128)}, f32[4,3,4,128]{3,2,1,0:T(4,128)}, f32[4,3,4,128]{3,2,1,0:T(4,128)}) custom-call(f32[1,4,4,8]{3,2,1,0:T(4,128)S(1)} %copy-done.1, f32[2,4,8,128]{3,2,1,0:T(8,128)S(1)} %get-tuple-element.68.refs_1_, f32[4,3,4,128]{3,2,1,0:T(4,128)S(1)} %get-tuple-element.69.refs_2_, ...), custom_call_target="tpu_custom_call" | custom-call | tf_op jit(solution)/shard_map/last_angles/pallas_call | solution.py:642
  (8 shorter events, 0.0 us)
Async XLA Ops:
  0.6 0.7 copy-start.11
  1.3 0.7 copy-start.4
  2.1 0.7 copy-start.5
  2.8 0.7 copy-start.12
  3.7 5.1 %copy-start.10 = (s32[8]{0:T(128)S(1)}, s32[8]{0:T(128)}, u32[]{:S(2)}) copy-start(s32[8]{0:T(128)} %param.17) | copy-start | bytes 100
  3.7 5.1 %collective-permute-start = (f32[25,4,128]{2,1,0:T(4,128)S(1)}, f32[25,4,128]{2,1,0:T(4,128)S(1)}, u32[]{:S(2)}, u32[]{:S(2)}) collective-permute-start(f32[25,4,128]{2,1,0:T(4,128)S(1)} %pack_walker.1.mine_ref.refs_0_), channel_id=1, source_target_pairs={{0,4},{4,0},{8,12},{12,8},{16,20},{20,16},{24,28},{28,24},{1,5},{5... | collective-permute-start | bytes 153608 | tf_op jit(solution)/shard_map/ppermute | solution.py:749
  8.8 9.3 %copy-start.6 = (f32[4,4,128]{2,1,0:T(4,128)S(1)}, f32[4,4,128]{2,1,0:T(4,128)}, u32[]{:S(2)}) copy-start(f32[4,4,128]{2,1,0:T(4,128)} %refs_5_.1) | copy-start | bytes 24580
  8.8 9.3 %copy-start.7 = (f32[4,4,128]{2,1,0:T(4,128)S(1)}, f32[4,4,128]{2,1,0:T(4,128)}, u32[]{:S(2)}) copy-start(f32[4,4,128]{2,1,0:T(4,128)} %refs_6_.1) | copy-start | bytes 24580
  8.8 9.3 %copy-start.8 = (s32[4,4,128]{2,1,0:T(4,128)S(1)}, s32[4,4,128]{2,1,0:T(4,128)}, u32[]{:S(2)}) copy-start(s32[4,4,128]{2,1,0:T(4,128)} %refs_7_.1) | copy-start | bytes 24580
  8.8 9.3 %copy-start.9 = (s32[4,4,128]{2,1,0:T(4,128)S(1)}, s32[4,4,128]{2,1,0:T(4,128)}, u32[]{:S(2)}) copy-start(s32[4,4,128]{2,1,0:T(4,128)} %refs_8_.2) | copy-start | bytes 24580
  9.3 6.7 %collective-permute-start.1 = (f32[25,4,128]{2,1,0:T(4,128)S(1)}, f32[25,4,128]{2,1,0:T(4,128)S(1)}, u32[]{:S(2)}, u32[]{:S(2)}) collective-permute-start(f32[25,4,128]{2,1,0:T(4,128)S(1)} %get-tuple-element.40), channel_id=1, source_target_pairs={{0,8},{4,12},{8,16},{12,20},{16,24},{20,28},{24,0},{28,4},{1,9},{5... | collective-permute-start | bytes 153608 | tf_op jit(solution)/shard_map/ppermute | solution.py:763
  11.4 5.1 %collective-permute-start.2 = (f32[25,4,128]{2,1,0:T(4,128)S(1)}, f32[25,4,128]{2,1,0:T(4,128)S(1)}, u32[]{:S(2)}, u32[]{:S(2)}) collective-permute-start(f32[25,4,128]{2,1,0:T(4,128)S(1)} %get-tuple-element.41), channel_id=1, source_target_pairs={{0,16},{4,20},{8,24},{12,28},{16,0},{20,4},{24,8},{28,12},{1,17},{... | collective-permute-start | bytes 153608 | tf_op jit(solution)/shard_map/ppermute | solution.py:763
  14.0 9.1 %copy-start = (f32[1,4,4,4,3,128]{5,3,4,2,1,0:T(4,128)S(1)}, f32[1,4,4,4,3,128]{5,3,4,2,1,0:T(4,128)}, u32[]{:S(2)}) copy-start(f32[1,4,4,4,3,128]{5,3,4,2,1,0:T(4,128)} %param.18) | copy-start | bytes 294916
  14.0 4.1 %collective-permute-start.3 = (f32[25,4,128]{2,1,0:T(4,128)S(1)}, f32[25,4,128]{2,1,0:T(4,128)S(1)}, u32[]{:S(2)}, u32[]{:S(2)}) collective-permute-start(f32[25,4,128]{2,1,0:T(4,128)S(1)} %get-tuple-element.42), channel_id=1, source_target_pairs={{0,24},{4,28},{8,0},{12,4},{16,8},{20,12},{24,16},{28,20},{1,25},{... | collective-permute-start | bytes 153608 | tf_op jit(solution)/shard_map/ppermute | solution.py:763
  18.2 5.0 %copy-start.2 = (s32[4,4,9]{2,1,0:T(4,128)S(1)}, s32[4,4,9]{2,1,0:T(4,128)}, u32[]{:S(2)}) copy-start(s32[4,4,9]{2,1,0:T(4,128)} %refs_0_.8) | copy-start | bytes 1732
  18.2 5.0 %copy-start.3 = (f32[4,4,128]{2,1,0:T(4,128)S(1)}, f32[4,4,128]{2,1,0:T(4,128)}, u32[]{:S(2)}) copy-start(f32[4,4,128]{2,1,0:T(4,128)} %refs_9_.5) | copy-start | bytes 24580
  18.4 4.8 %copy-start.1 = (f32[1,4,4,8]{3,2,1,0:T(4,128)S(1)}, f32[1,4,4,8]{3,2,1,0:T(4,128)}, u32[]{:S(2)}) copy-start(f32[1,4,4,8]{3,2,1,0:T(4,128)} %refs_0_.9) | copy-start | bytes 1540
  18.4 4.7 %collective-permute-start.5 = (f32[2,7,4,128]{3,2,1,0:T(4,128)S(1)}, f32[2,7,4,128]{3,2,1,0:T(4,128)S(1)}, u32[]{:S(2)}, u32[]{:S(2)}) collective-permute-start(f32[2,7,4,128]{3,2,1,0:T(4,128)S(1)} %get-tuple-element.45), channel_id=1, source_target_pairs={{2,0},{3,1},{0,2},{1,3},{6,4},{7,5},{4,6},{5,7},{10,8},{11,9},{8,1... | collective-permute-start | bytes 86024 | tf_op jit(solution)/shard_map/ppermute | solution.py:53
  20.0 3.2 %collective-permute-start.6 = (f32[4,7,2,128]{3,2,1,0:T(2,128)S(1)}, f32[4,7,2,128]{3,2,1,0:T(2,128)S(1)}, u32[]{:S(2)}, u32[]{:S(2)}) collective-permute-start(f32[4,7,2,128]{3,2,1,0:T(2,128)S(1)} %get-tuple-element.46), channel_id=1, source_target_pairs={{1,0},{0,1},{3,2},{2,3},{5,4},{4,5},{7,6},{6,7},{9,8},{8,9},{11,10... | collective-permute-start | bytes 86024 | tf_op jit(solution)/shard_map/ppermute | solution.py:53
  20.0 3.1 %collective-permute-start.4 = (f32[2,7,2,128]{3,2,1,0:T(2,128)S(1)}, f32[2,7,2,128]{3,2,1,0:T(2,128)S(1)}, u32[]{:S(2)}, u32[]{:S(2)}) collective-permute-start(f32[2,7,2,128]{3,2,1,0:T(2,128)S(1)} %get-tuple-element.44), channel_id=1, source_target_pairs={{3,0},{2,1},{1,2},{0,3},{7,4},{6,5},{5,6},{4,7},{11,8},{10,9},{9,1... | collective-permute-start | bytes 43016 | tf_op jit(solution)/shard_map/ppermute | solution.py:53
  32.9 4.0 %collective-permute-start.8 = (f32[2,4,4,128]{3,2,1,0:T(4,128)S(1)}, f32[2,4,4,128]{3,2,1,0:T(4,128)S(1)}, u32[]{:S(2)}, u32[]{:S(2)}) collective-permute-start(f32[2,4,4,128]{3,2,1,0:T(4,128)S(1)} %get-tuple-element.51), channel_id=1, source_target_pairs={{2,0},{3,1},{0,2},{1,3},{6,4},{7,5},{4,6},{5,7},{10,8},{11,9},{8,1... | collective-permute-start | bytes 49160 | tf_op jit(solution)/shard_map/ppermute | solution.py:53
  33.7 3.1 %collective-permute-start.9 = (f32[4,4,2,128]{3,2,1,0:T(2,128)S(1)}, f32[4,4,2,128]{3,2,1,0:T(2,128)S(1)}, u32[]{:S(2)}, u32[]{:S(2)}) collective-permute-start(f32[4,4,2,128]{3,2,1,0:T(2,128)S(1)} %get-tuple-element.52), channel_id=1, source_target_pairs={{1,0},{0,1},{3,2},{2,3},{5,4},{4,5},{7,6},{6,7},{9,8},{8,9},{11,10... | collective-permute-start | bytes 49160 | tf_op jit(solution)/shard_map/ppermute | solution.py:53
  33.7 3.1 %collective-permute-start.7 = (f32[2,5,2,128]{3,2,1,0:T(2,128)S(1)}, f32[2,5,2,128]{3,2,1,0:T(2,128)S(1)}, u32[]{:S(2)}, u32[]{:S(2)}) collective-permute-start(f32[2,5,2,128]{3,2,1,0:T(2,128)S(1)} %get-tuple-element.50), channel_id=1, source_target_pairs={{3,0},{2,1},{1,2},{0,3},{7,4},{6,5},{5,6},{4,7},{11,8},{10,9},{9,1... | collective-permute-start | bytes 30728 | tf_op jit(solution)/shard_map/ppermute | solution.py:53
  46.5 4.6 %collective-permute-start.11 = (f32[2,4,4,128]{3,2,1,0:T(4,128)S(1)}, f32[2,4,4,128]{3,2,1,0:T(4,128)S(1)}, u32[]{:S(2)}, u32[]{:S(2)}) collective-permute-start(f32[2,4,4,128]{3,2,1,0:T(4,128)S(1)} %get-tuple-element.58), channel_id=1, source_target_pairs={{2,0},{3,1},{0,2},{1,3},{6,4},{7,5},{4,6},{5,7},{10,8},{11,9},{8,1... | collective-permute-start | bytes 49160 | tf_op jit(solution)/shard_map/ppermute | solution.py:53
  48.0 3.1 %collective-permute-start.12 = (f32[4,4,2,128]{3,2,1,0:T(2,128)S(1)}, f32[4,4,2,128]{3,2,1,0:T(2,128)S(1)}, u32[]{:S(2)}, u32[]{:S(2)}) collective-permute-start(f32[4,4,2,128]{3,2,1,0:T(2,128)S(1)} %get-tuple-element.59), channel_id=1, source_target_pairs={{1,0},{0,1},{3,2},{2,3},{5,4},{4,5},{7,6},{6,7},{9,8},{8,9},{11,10... | collective-permute-start | bytes 49160 | tf_op jit(solution)/shard_map/ppermute | solution.py:53
  48.0 3.1 %collective-permute-start.10 = (f32[2,5,2,128]{3,2,1,0:T(2,128)S(1)}, f32[2,5,2,128]{3,2,1,0:T(2,128)S(1)}, u32[]{:S(2)}, u32[]{:S(2)}) collective-permute-start(f32[2,5,2,128]{3,2,1,0:T(2,128)S(1)} %get-tuple-element.57), channel_id=1, source_target_pairs={{3,0},{2,1},{1,2},{0,3},{7,4},{6,5},{5,6},{4,7},{11,8},{10,9},{9,1... | collective-permute-start | bytes 30728 | tf_op jit(solution)/shard_map/ppermute | solution.py:53
  60.8 4.0 %collective-permute-start.14 = (f32[2,4,4,128]{3,2,1,0:T(4,128)S(1)}, f32[2,4,4,128]{3,2,1,0:T(4,128)S(1)}, u32[]{:S(2)}, u32[]{:S(2)}) collective-permute-start(f32[2,4,4,128]{3,2,1,0:T(4,128)S(1)} %get-tuple-element.64), channel_id=1, source_target_pairs={{2,0},{3,1},{0,2},{1,3},{6,4},{7,5},{4,6},{5,7},{10,8},{11,9},{8,1... | collective-permute-start | bytes 49160 | tf_op jit(solution)/shard_map/ppermute | solution.py:53
  61.7 3.1 %collective-permute-start.15 = (f32[4,4,2,128]{3,2,1,0:T(2,128)S(1)}, f32[4,4,2,128]{3,2,1,0:T(2,128)S(1)}, u32[]{:S(2)}, u32[]{:S(2)}) collective-permute-start(f32[4,4,2,128]{3,2,1,0:T(2,128)S(1)} %get-tuple-element.65), channel_id=1, source_target_pairs={{1,0},{0,1},{3,2},{2,3},{5,4},{4,5},{7,6},{6,7},{9,8},{8,9},{11,10... | collective-permute-start | bytes 49160 | tf_op jit(solution)/shard_map/ppermute | solution.py:53
  61.7 3.1 %collective-permute-start.13 = (f32[2,5,2,128]{3,2,1,0:T(2,128)S(1)}, f32[2,5,2,128]{3,2,1,0:T(2,128)S(1)}, u32[]{:S(2)}, u32[]{:S(2)}) collective-permute-start(f32[2,5,2,128]{3,2,1,0:T(2,128)S(1)} %get-tuple-element.63), channel_id=1, source_target_pairs={{3,0},{2,1},{1,2},{0,3},{7,4},{6,5},{5,6},{4,7},{11,8},{10,9},{9,1... | collective-permute-start | bytes 30728 | tf_op jit(solution)/shard_map/ppermute | solution.py:53
  74.6 2.0 %collective-permute-start.18 = (f32[8,128]{1,0:T(8,128)S(1)}, f32[8,128]{1,0:T(8,128)S(1)}, u32[]{:S(2)}, u32[]{:S(2)}) collective-permute-start(f32[8,128]{1,0:T(8,128)S(1)} %get-tuple-element.71.refs_4_), channel_id=1, source_target_pairs={{1,0},{0,1},{3,2},{2,3},{5,4},{4,5},{7,6},{6,7},{9,8},{8,9},{11,10... | collective-permute-start | bytes 12296 | tf_op jit(solution)/shard_map/ppermute | solution.py:53
  75.2 3.6 %collective-permute-start.17 = (f32[8,128]{1,0:T(8,128)S(1)}, f32[8,128]{1,0:T(8,128)S(1)}, u32[]{:S(2)}, u32[]{:S(2)}) collective-permute-start(f32[8,128]{1,0:T(8,128)S(1)} %get-tuple-element.71.refs_4_), channel_id=1, source_target_pairs={{2,0},{3,1},{0,2},{1,3},{6,4},{7,5},{4,6},{5,7},{10,8},{11,9},{8,1... | collective-permute-start | bytes 12296 | tf_op jit(solution)/shard_map/ppermute | solution.py:53
  76.4 3.0 %collective-permute-start.16 = (f32[8,128]{1,0:T(8,128)S(1)}, f32[8,128]{1,0:T(8,128)S(1)}, u32[]{:S(2)}, u32[]{:S(2)}) collective-permute-start(f32[8,128]{1,0:T(8,128)S(1)} %get-tuple-element.71.refs_4_), channel_id=1, source_target_pairs={{3,0},{2,1},{1,2},{0,3},{7,4},{6,5},{5,6},{4,7},{11,8},{10,9},{9,1... | collective-permute-start | bytes 12296 | tf_op jit(solution)/shard_map/ppermute | solution.py:53

commit v6 on v5

--- a/solution.py
+++ b/solution.py
@@ -22,6 +22,8 @@
 MIDDLE_Z = 1.0
 REACH = 1.49
 FAR = 2.0**126
+GROUP = 2
+AHEAD = 2
 SMALL = 4 * 2**20
 ROWS = 16
 
@@ -173,7 +175,7 @@
     velo_ref, ango_ref = take(2)
     (stato_ref,) = take(1) if moment == 0 else (None,)
     (sumo_ref,) = take(1) if last else (None,)
-    pool_ref, col_ref, fcol_ref, sum_ref, feat_ref, wide_ref, rhs_ref, coef_ref, off_ref, io_ref = take(10)
+    pool_ref, col_ref, fcol_ref, sum_ref, feat_ref, wide_ref, rhs_ref, coef_ref, off_ref, io_ref, tall_ref, begin_ref, weight_ref = take(13)
     part_ref, part_sem = take(2)
     part_copy = pltpu.make_async_copy(part_hbm, part_ref, part_sem)
     part_copy.start()
@@ -263,7 +265,7 @@
     def _():
         near_forces(
             cfg, lambdas, part_ref, off_ref, pool_ref, feat_ref, wide_ref, rhs_ref,
-            coef_ref, ins, outs, sub_iota,
+            coef_ref, tall_ref, begin_ref, weight_ref, ins, outs, sub_iota,
         )
 
     @pl.when(jnp.logical_not(near))
@@ -311,7 +313,7 @@
 
 def near_forces(
     cfg, lambdas, part_ref, off_ref, pool_ref, feat_ref, wide_ref, rhs_ref,
-    coef_ref, ins, outs, sub_iota,
+    coef_ref, tall_ref, begin_ref, weight_ref, ins, outs, sub_iota,
 ):
     lanes = cfg["lanes"]
     depth = cfg["depth"]
@@ -356,24 +358,29 @@
         feat_ref[index] = features
         wide_ref[index] = jnp.dot(features, pick, preferred_element_type=jnp.float32)
         coef = jnp.concatenate([high, middle, low, nothing], axis=0).astype(jnp.bfloat16)
+        coef = jnp.concatenate([coef] + [m.astype(jnp.bfloat16) for m in member], axis=0)
         coef_ref[index] = jnp.concatenate([coef, coef], axis=1)
 
     lax.fori_loop(0, cfg["pool"] // cfg["pool_group"], some_pool, 0)
     none_columns = lax.broadcasted_iota(jnp.int32, (lanes, depth), 1)
     feat_ref[cfg["pool"]] = jnp.where(none_columns == 6, 1.0, 0.0).astype(jnp.bfloat16)
     wide_ref[cfg["pool"]] = jnp.zeros((lanes, lanes), jnp.float32)
-    coef_ref[cfg["pool"]] = jnp.zeros((32, 2 * lanes), jnp.bfloat16)
+    coef_ref[cfg["pool"]] = jnp.zeros((64, 2 * lanes), jnp.bfloat16)
 
     spread = [lam - lam * lam for lam in lambdas]
     half = [0.5 - lam for lam in lambdas]
-
-    def one_tile(tile, carry):
-        own = (tile // cfg["rows_y"] + 1) * (cfg["rows_y"] + 2) + tile % cfg["rows_y"] + 1
-        block, moved, norm = centred(own)
+    rows_x, rows_y = cfg["rows_x"], cfg["rows_y"]
+    _, sum_ref = outs
+    tall_ref[...] = jnp.zeros_like(tall_ref)
+    begin_ref[...] = jnp.zeros_like(begin_ref)
+
+    def own_tile(i, j):
+        return (i + 1) * (rows_y + 2) + j + 1
+
+    def own_table(i, j):
+        block, moved, norm = centred(own_tile(i, j))
         group, site_row = block[GRP : GRP + 1, :], block[SIT : SIT + 1, :]
         lam, charge, strength = (block[r : r + 1, :] for r in (LAM, CHG, STR))
-        ratio = charge / strength
-
         gap = jnp.where(rows < 3, -2.0 * moved, 0.0)
         gap = jnp.where(rows == 3, -0.5 * lam, gap)
         gap = jnp.where(rows == 5, 1.0, gap)
@@ -388,67 +395,154 @@
         columns = (
             (gap, [f - 0.5 * p for f, p in zip(far, pair)]),
             (jnp.where(rows == 3, lam, 0.0), pair),
-            (jnp.where(rows == 3, 1.0, 0.0), by_group(half, group, sub_iota)),
-            (jnp.where(rows == 4, ratio, 0.0), [nothing] * NSITE),
+            (jnp.where(rows == 4, charge / strength, 0.0), [nothing] * NSITE),
         )
         for column, (table, member) in enumerate(columns):
             high, middle, low = split3(table)
             tops = [m.astype(jnp.bfloat16).astype(jnp.float32) for m in member]
             rests = [m - t for m, t in zip(member, tops)]
-            rhs_ref[column] = jnp.concatenate(
+            rhs_ref[i * rows_y + j, column] = jnp.concatenate(
                 [high, middle, high, middle, low, high] + tops + rests + pad, axis=0
             ).astype(jnp.bfloat16)
-
-        def some_partners(k, sums):
-            indices = [part_of(part_ref, cfg, tile, k + u) for u in range(cfg["slots"])]
-            indices = [jnp.where(index < 0, cfg["pool"], index) for index in indices]
-            outs = []
-            for first in range(0, len(indices), 3):
-                some = indices[first : first + 3]
-                out = table_dot(jnp.concatenate([feat_ref[index] for index in some], axis=0), rhs_ref)
-                outs += [out[n * lanes : (n + 1) * lanes] for n in range(len(some))]
-            moments, fd = sums
-            for index, out in zip(indices, outs):
-                tops, rests = [], []
-                for i in range(lanes // ROWS):
-                    here = slice(ROWS * i, ROWS * i + ROWS)
-                    gap2, s, w, q = (out[here, c * lanes : (c + 1) * lanes] for c in range(4))
-                    eb = wide_ref[index, here, :]
-                    rs = lax.rsqrt(gap2)
-                    t = rs * rs * rs
-                    a = eb * t
-                    b = (s * t) * (a + 0.25 * q)
-                    sens = (rs * (a + q) + b) * w
-                    for j in range(ROWS // 8):
-                        fd = fd + sens[8 * j : 8 * j + 8, :]
-                    top = b.astype(jnp.bfloat16)
-                    tops.append(top)
-                    rests.append((b - top.astype(jnp.float32)).astype(jnp.bfloat16))
-                moments = moments + jnp.dot(
-                    coef_ref[index],
-                    jnp.concatenate(tops + rests, axis=0),
+        weight = jnp.where(rows < 3, moved * strength, jnp.where(rows == 6, strength, 0.0))
+        weight = jnp.concatenate([*split3(weight), nothing], axis=0).astype(jnp.bfloat16)
+        weight_ref[i * rows_y + j] = jnp.concatenate([weight, weight], axis=1)
+
+    for i in range(rows_x):
+        for j in range(rows_y):
+            own_table(i, j)
+
+    def three(value):
+        return value[0:8] + value[8:16] + value[16:24]
+
+    def tables(i, j, steps):
+        own = own_tile(i, j)
+        indices = []
+        for di, dj in steps:
+            index = own + di * (rows_y + 2) + dj
+            listed = part_ref[i, j, (di + 1) * 3 + dj + 1] > 0
+            indices.append(jnp.where(listed, index, cfg["pool"]))
+        out = table_dot(
+            jnp.concatenate([feat_ref[index] for index in indices], axis=0),
+            rhs_ref.at[i * rows_y + j],
+        )
+        return indices, [out[n * lanes : (n + 1) * lanes] for n in range(len(steps))]
+
+    def all_pairs(i, work):
+        ready = [tables(i, *work[n]) for n in range(AHEAD)]
+        for n, (j, steps) in enumerate(work):
+            if n + AHEAD < len(work):
+                ready.append(tables(i, *work[n + AHEAD]))
+            indices, outs = ready[n]
+            for step, values in zip(steps, some_pairs(i, j, steps, indices, outs)):
+                yield j, step, values
+
+    def groups(work):
+        return [
+            (j, steps[first : first + GROUP])
+            for j, steps in work
+            for first in range(0, len(steps), GROUP)
+        ]
+
+    def some_pairs(i, j, steps, indices, outs):
+        results = []
+        for out, index, step in zip(outs, indices, steps):
+            pieces = [[], [], [], []]
+            for r in range(lanes // ROWS):
+                here = slice(ROWS * r, ROWS * r + ROWS)
+                gap2, s, q = (out[here, c * lanes : (c + 1) * lanes] for c in range(3))
+                eb = wide_ref[index, ROWS * r : ROWS * r + ROWS, :]
+                rs = lax.rsqrt(gap2)
+                t = rs * rs * rs
+                a = eb * t
+                b = (s * t) * (a + 0.25 * q)
+                sens = rs * (a + q) + b
+                for kind, value in enumerate((b, sens)):
+                    top = value.astype(jnp.bfloat16)
+                    pieces[2 * kind].append(top)
+                    pieces[2 * kind + 1].append(
+                        (value - top.astype(jnp.float32)).astype(jnp.bfloat16)
+                    )
+            b_top, b_rest, s_top, s_rest = (jnp.concatenate(p, axis=0) for p in pieces)
+            moments = jnp.dot(
+                coef_ref[index, 0:32], jnp.concatenate([b_top, b_rest], axis=0),
+                preferred_element_type=jnp.float32,
+            )
+            drives = jnp.dot(
+                coef_ref[index], jnp.concatenate([s_top, s_rest], axis=0),
+                preferred_element_type=jnp.float32,
+            )
+            if step > (0, 0):
+                back = lax.dot_general(
+                    weight_ref[i * rows_y + j], jnp.concatenate([b_top, b_rest], axis=1), (((1,), (1,)), ((), ())),
                     preferred_element_type=jnp.float32,
                 )
-            return moments, fd
-
-        moments, fd = some_partners(0, (jnp.zeros((32, lanes), jnp.float32), nothing))
-        moments = moments[0:8] + moments[8:16] + moments[16:24]
-        fd = jnp.sum(fd, axis=0, keepdims=True)
-        forces = moved[0:3, :] * moments[6:7, :] - moments[0:3, :]
-        rs = lax.rsqrt(1.5 - 0.5 * lam)
-        t = rs * rs * rs
-        a, q = strength * t, ratio * charge
-        itself = rs * (a + q) + lam * t * (a + 0.25 * q)
-        drive = strength * (fd - 0.5 * itself)
-        finish_tile(cfg, tile, (4.0 * strength) * forces, drive, block, ins, outs, sub_iota)
+                tall_ref[index] += three(back)
+            results.append((three(moments), three(drives[0:32]), drives[32:64]))
+        return results
+
+    def add(total, values):
+        return [x + y for x, y in zip(total, values)]
+
+    work = []
+    for j in range(rows_y):
+        steps = [
+            (-1, d) for d in (-1, 0, 1) if not (j == 0 and d == -1 or j == rows_y - 1 and d == 1)
+        ]
+        work.append((j, steps))
+    empty = [nothing, nothing, jnp.zeros((NSITE * NSUB, lanes), jnp.float32)]
+    border = [empty] * rows_y
+    for j, _, values in all_pairs(0, groups(work)):
+        border[j] = add(border[j], values)
+    for j, total in enumerate(border):
+        begin_ref[j] = jnp.concatenate(total, axis=0)
+
+    def one_row(i, carry):
+        inner = jnp.where(i < rows_x - 1, 1.0, 0.0)
+        work = []
+        for j in range(rows_y):
+            steps = [(0, 0), (0, 1), (1, -1), (1, 0), (1, 1)]
+            steps += [(0, -1), (-1, -1)] if j == 0 else []
+            steps += [(-1, 1)] if j == rows_y - 1 else []
+            work.append((j, steps))
+        zero = jnp.zeros((NSITE * NSUB, lanes), jnp.float32)
+        sums = [
+            [begin_ref[j, 0:8], begin_ref[j, 8:16], begin_ref[j, 16:], zero, zero]
+            for j in range(rows_y)
+        ]
+        for j, (di, dj), (m, d, g) in all_pairs(i, groups(work)):
+            if (di, dj) <= (0, 0) or not 0 <= j + dj < rows_y:
+                kind = 2
+            else:
+                kind = 3 if di == 0 else 4
+            sums[j][0] = sums[j][0] + m
+            sums[j][1] = sums[j][1] + d
+            sums[j][kind] = sums[j][kind] + g
+        kept = []
+        for j, (moments, drive, once, twice, below) in enumerate(sums):
+            block, moved, _ = centred(own_tile(i, j))
+            kept.append((block, moved, moments, drive, once + twice + below, twice + inner * below))
+        for j, (block, moved, moments, drive, once, twice) in enumerate(kept):
+            group = block[GRP : GRP + 1, :]
+            lam, charge, strength = (block[r : r + 1, :] for r in (LAM, CHG, STR))
+            others = tall_ref[own_tile(i, j)]
+            forces = strength * (moved[0:3] * moments[6:7] - moments[0:3])
+            forces = forces + (moved[0:3] * others[6:7] - others[0:3])
+            rs = lax.rsqrt(1.5 - 0.5 * lam)
+            t = rs * rs * rs
+            a, q = strength * t, charge * charge / strength
+            itself = rs * (a + q) + lam * t * (a + 0.25 * q)
+            mine = by_group([ones] * NSITE, group, sub_iota)
+            for site in range(NSITE):
+                here = slice(site * NSUB, site * NSUB + NSUB)
+                both = once[here] + twice[here]
+                value = mine[site] * (drive[3:4] - 0.5 * itself + half[site] * both)
+                sum_ref[site] += strength * (value + lam * twice[here])
+            finish_tile(cfg, i * rows_y + j, 4.0 * forces, None, block, ins, outs, sub_iota)
+        begin_ref[...] = jnp.zeros_like(begin_ref)
         return carry
 
-    def some_tiles(k, carry):
-        for u in range(4):
-            one_tile(k * 4 + u, carry)
-        return carry
-
-    lax.fori_loop(0, cfg["tiles"] // 4, some_tiles, 0)
+    lax.fori_loop(0, rows_x, one_row, 0)
 
 
 def any_forces(cfg, part_ref, pool_ref, col_ref, fcol_ref, ins, outs, sub_iota):
@@ -459,9 +553,6 @@
         own = (tile // cfg["rows_y"] + 1) * (cfg["rows_y"] + 2) + tile % cfg["rows_y"] + 1
         block = pool_ref[own]
         col_ref[...] = block.T
-        count = jnp.int32(0)
-        for k in range(cfg["slots"]):
-            count += (part_of(part_ref, cfg, tile, k) >= 0).astype(jnp.int32)
 
         def one_chunk(c, carry):
             start = pl.multiple_of(c * chunk, chunk)
@@ -471,7 +562,8 @@
 
             def one_partner(k, sums):
                 fx, fy, fz, fd = sums
-                index = part_of(part_ref, cfg, tile, k)
+                index = own + (k // 3 - 1) * (cfg["rows_y"] + 2) + k % 3 - 1
+                listed = part_of(part_ref, cfg, tile, k) > 0
                 other = pool_ref[index]
 
                 def own_col(row):
@@ -486,7 +578,7 @@
                 r2 = dx * dx + dy * dy + dz * dz
                 same = (own_col(GRP) == other_row(GRP)) & (own_col(GRP) >= 0.0)
                 site = (own_col(SIT) == other_row(SIT)) & (own_col(SIT) >= 0.0)
-                drop = (site & jnp.logical_not(same)) | (diagonal & (index == own))
+                drop = (site & jnp.logical_not(same)) | (diagonal & (index == own)) | jnp.logical_not(listed)
                 lam_a, lam_b = own_col(LAM), other_row(LAM)
                 s = jnp.where(same, lam_a, lam_a * lam_b)
                 w = jnp.where(same, 0.5, lam_b)
@@ -502,7 +594,7 @@
                 return fx + b * dx, fy + b * dy, fz + b * dz, fd + sens
 
             zero = jnp.zeros((chunk, lanes), jnp.float32)
-            sums = lax.fori_loop(0, count, one_partner, (zero, zero, zero, zero))
+            sums = lax.fori_loop(0, 9, one_partner, (zero, zero, zero, zero))
             for row, value in enumerate(sums):
                 fcol_ref[pl.ds(start, chunk), row : row + 1] = jnp.sum(
                     value, axis=1, keepdims=True
@@ -532,6 +624,8 @@
     )
     ins[tile, 0:3, :] = block[0:3, :] + step_size * speeds
     ins[tile, 4:7, :] = speeds
+    if drive is None:
+        return
     group = block[GRP : GRP + 1, :]
     for site in range(NSITE):
         sum_ref[site] += jnp.where(group == sub_iota + float(site * NSUB), drive, 0.0)
@@ -595,10 +689,13 @@
             pltpu.VMEM((NSITE, NSUB, lanes), jnp.float32),
             pltpu.VMEM((pool + 1, lanes, depth), jnp.bfloat16),
             pltpu.VMEM((pool + 1, lanes, lanes), jnp.float32),
-            pltpu.VMEM((4, depth, lanes), jnp.bfloat16),
-            pltpu.VMEM((pool + 1, 32, 2 * lanes), jnp.bfloat16),
+            pltpu.VMEM((tiles, 3, depth, lanes), jnp.bfloat16),
+            pltpu.VMEM((pool + 1, 64, 2 * lanes), jnp.bfloat16),
             pltpu.SMEM((2, pool), jnp.float32),
             pltpu.VMEM((tiles, 8, lanes), jnp.float32),
+            pltpu.VMEM((pool + 1, 8, lanes), jnp.float32),
+            pltpu.VMEM((rows_y, 16 + NSITE * NSUB, lanes), jnp.float32),
+            pltpu.VMEM((tiles, 32, 2 * lanes), jnp.bfloat16),
             pltpu.SMEM(parts.shape, jnp.int32),
             pltpu.SemaphoreType.DMA(()),
         ],
@@ -741,7 +838,6 @@
             pltpu.SemaphoreType.DMA((2 + 2 * rows_x,)),
         ],
         name="pack_walker",
-        compiler_params=pltpu.CompilerParams(vmem_limit_bytes=SMALL),
     )(positions, velocities, theta, speed)
     source_slot = source_slot.reshape(1, peers)
     other = message
@@ -831,6 +927,10 @@
         lambda_theta, theta_velocity, source_slot, charges, strengths, atom_site, atom_sub,
     )
     noise = atom_noise.transpose(0, 1, 2, 4, 3, 5)
+    at_x = jnp.arange(rows_x)[:, None, None] + 1 + jnp.arange(9) // 3 - 1
+    at_y = jnp.arange(rows_y)[:, None] + 1 + jnp.arange(9) % 3 - 1
+    entries = at_x * (rows_y + 2) + at_y
+    listed = jnp.any(partners[..., None, :] == entries[..., None], axis=-1).astype(jnp.int32)
     first = pays[0]
     pool_stat = None
     for moment in range(STEPS):
@@ -838,7 +938,7 @@
         if moment > 0 and not cfg["covered"]:
             totals = lax.psum(pays[0][:, 3].reshape(tiles, lanes)[:NSUB], ("gx", "gy"))
         outs = step_call(
-            cfg, moment, partners, theta_noise, gather_blocks(pays), pool_stat, totals, vel,
+            cfg, moment, listed, theta_noise, gather_blocks(pays), pool_stat, totals, vel,
             noise, inverse_mass, ang, first,
         )
         own = cfg["blocks"] if moment < STEPS - 1 else 1

time: 81.1 us -> 76.3 us (0.941)
  Pallas kernels: 40.9 us -> 37.8 us
  local copies, waits for them, and re-layouts: 2.88 us -> 1.07 us
  waiting for transfers between devices: 16.2 us -> 15.2 us
  other arithmetic: 0 us -> 0.94 us
    pallas_call x4, Pallas kernels: 38.8 us -> 34.4 us  [step_call(): pl.pallas_call(functools.partial(step_kernel, cfg, moment), grid=(1,), ou...]
    unnamed x26 -> x22, local copies, waits for them, and re-layouts: 2.88 us -> 0.85 us
    pallas_call x1, Pallas kernels: 0.21 us -> 1.6 us  [clone(): pl.pallas_call(pack_kernel, out_shape=jax.ShapeDtypeStruct((6 * rows_x +...]
    ppermute x15, waiting for transfers between devices: 11.3 us -> 10.4 us  [shifted(): return lax.ppermute(value, ('gx', 'gy'), pairs)]
  transfers between devices with their start and end apart: 19 -> 19, of which waited for: 10 -> 10; matrix products, arithmetic and copies ran while one was open for 0% -> 2% of each run, Pallas kernels for 0% -> 0%
where the time goes in v6:
time: 76.3 us; the launch traced here: 76.1 us
  Pallas kernels  37.8 us (50%)
  starting transfers between devices  20.2 us (26%)
  waiting for transfers between devices  15.2 us (20%)
  local copies, waits for them, and re-layouts  1.07 us (1%)
  between operations  0.95 us (1%)
  other arithmetic  0.94 us (1%)
    pallas_call x4, Pallas kernels, step_call(): pl.pallas_call(functools.partial(step_kernel, cfg, moment), grid=(1,), ou...  34.4 us
    ppermute x15, starting transfers between devices, shifted(): return lax.ppermute(value, ('gx', 'gy'), pairs)  11 us
    ppermute x15, waiting for transfers between devices, shifted(): return lax.ppermute(value, ('gx', 'gy'), pairs)  10.4 us
    ppermute x3, starting transfers between devices, clone(): lax.ppermute(value, 'walker', [(w, (w + k * width) % peers) for w in rang...  6.1 us
    ppermute x1, starting transfers between devices, clone(): other = lax.ppermute(message, 'walker', [(w, w ^ 1) for w in range(peers)])  3.03 us
    ppermute x3, waiting for transfers between devices, clone(): lax.ppermute(value, 'walker', [(w, (w + k * width) % peers) for w in rang...  2.68 us
    ppermute x1, waiting for transfers between devices, clone(): other = lax.ppermute(message, 'walker', [(w, w ^ 1) for w in range(peers)])  2.11 us
    pallas_call x1, Pallas kernels, clone(): pl.pallas_call(pack_kernel, out_shape=jax.ShapeDtypeStruct((6 * rows_x +...  1.6 us
  transfers between devices with their start and end apart: 19, of which 10 were waited for; matrix products, arithmetic and copies ran while one was open for 2% of the time, Pallas kernels for 0%

profile of v6, /device:TPU:0, one launch (start us, length us, event | category | flops | bytes accessed | tf_op | source)
XLA Modules:
  0.0 76.1 jit_solution(14175260933313434691)
XLA Ops:
  0.6 1.6 %pack_walker.1.mine_ref.refs_0_ = f32[25,4,128]{2,1,0:T(4,128)} custom-call(f32[4,3,4,128]{3,2,1,0:T(4,128)} %bitcast.20, f32[4,3,4,128]{3,2,1,0:T(4,128)} %bitcast.21, f32[1,4,8]{2,1,0:T(4,128)} %theta_ref.1, f32[1,4,8]{2,1,0:T(4,128)} %speed_ref.1), custom_call_target="tpu_custom_call" | custom-call | tf_op jit(solution)/shard_map/pack_walker/pallas_call | solution.py:831
  2.2 3.0 %collective-permute-start = (f32[25,4,128]{2,1,0:T(4,128)}, f32[25,4,128]{2,1,0:T(4,128)S(1)}, u32[]{:S(2)}, u32[]{:S(2)}) collective-permute-start(f32[25,4,128]{2,1,0:T(4,128)} %pack_walker.1.mine_ref.refs_0_), channel_id=1, source_target_pairs={{0,4},{4,0},{8,12},{12,8},{16,20},{20,16},{24,28},{28,24},{1,5},{5... | collective-permute-start | bytes 153608 | tf_op jit(solution)/shard_map/ppermute | solution.py:845
  5.3 0.1 add_multiply_fusion
  5.4 0.1 copy.19
  5.5 2.1 %collective-permute-done.other_ref.refs_1_ = f32[25,4,128]{2,1,0:T(4,128)S(1)} collective-permute-done((f32[25,4,128]{2,1,0:T(4,128)}, f32[25,4,128]{2,1,0:T(4,128)S(1)}, u32[]{:S(2)}, u32[]{:S(2)}) %collective-permute-start) | collective-permute-done | bytes 51232 | tf_op jit(solution)/shard_map/ppermute | solution.py:845
  7.6 0.0 copy-done.9
  7.6 0.8 %copy-done.1 = f32[25,4,128]{2,1,0:T(4,128)S(1)} copy-done((f32[25,4,128]{2,1,0:T(4,128)S(1)}, f32[25,4,128]{2,1,0:T(4,128)}, u32[]{:S(2)}) %copy-start.1) | copy-done | bytes 51224
  8.4 0.4 choose_sent.1
  8.8 2.2 %collective-permute-start.1 = (f32[25,4,128]{2,1,0:T(4,128)S(1)}, f32[25,4,128]{2,1,0:T(4,128)S(1)}, u32[]{:S(2)}, u32[]{:S(2)}) collective-permute-start(f32[25,4,128]{2,1,0:T(4,128)S(1)} %get-tuple-element.40), channel_id=1, source_target_pairs={{0,8},{4,12},{8,16},{12,20},{16,24},{20,28},{24,0},{28,4},{1,9},{5... | collective-permute-start | bytes 153608 | tf_op jit(solution)/shard_map/ppermute | solution.py:859
  11.0 2.6 %collective-permute-start.2 = (f32[25,4,128]{2,1,0:T(4,128)S(1)}, f32[25,4,128]{2,1,0:T(4,128)S(1)}, u32[]{:S(2)}, u32[]{:S(2)}) collective-permute-start(f32[25,4,128]{2,1,0:T(4,128)S(1)} %get-tuple-element.41), channel_id=1, source_target_pairs={{0,16},{4,20},{8,24},{12,28},{16,0},{20,4},{24,8},{28,12},{1,17},{... | collective-permute-start | bytes 153608 | tf_op jit(solution)/shard_map/ppermute | solution.py:859
  13.5 1.3 %collective-permute-start.3 = (f32[25,4,128]{2,1,0:T(4,128)S(1)}, f32[25,4,128]{2,1,0:T(4,128)S(1)}, u32[]{:S(2)}, u32[]{:S(2)}) collective-permute-start(f32[25,4,128]{2,1,0:T(4,128)S(1)} %get-tuple-element.42), channel_id=1, source_target_pairs={{0,24},{4,28},{8,0},{12,4},{16,8},{20,12},{24,16},{28,20},{1,25},{... | collective-permute-start | bytes 153608 | tf_op jit(solution)/shard_map/ppermute | solution.py:859
  14.9 0.1 broadcast_add_fusion
  15.0 0.5 collective-permute-done.1.refs_2_
  15.5 0.5 collective-permute-done.2.refs_3_
  16.1 1.6 %collective-permute-done.3.refs_4_ = f32[25,4,128]{2,1,0:T(4,128)S(1)} collective-permute-done((f32[25,4,128]{2,1,0:T(4,128)S(1)}, f32[25,4,128]{2,1,0:T(4,128)S(1)}, u32[]{:S(2)}, u32[]{:S(2)}) %collective-permute-start.3) | collective-permute-done | bytes 51232 | tf_op jit(solution)/shard_map/ppermute | solution.py:859
  17.7 0.0 copy-done.2
  17.7 0.0 copy-done.5
  17.7 0.0 copy-done.6
  17.7 0.0 copy-done.7
  17.7 0.0 copy-done.8
  17.7 0.0 copy-start.10
  17.7 0.0 copy-start
  17.7 0.2 choose_received.1
  17.9 1.6 %collective-permute-start.5 = (f32[2,7,4,128]{3,2,1,0:T(4,128)S(1)}, f32[2,7,4,128]{3,2,1,0:T(4,128)S(1)}, u32[]{:S(2)}, u32[]{:S(2)}) collective-permute-start(f32[2,7,4,128]{3,2,1,0:T(4,128)S(1)} %get-tuple-element.45), channel_id=1, source_target_pairs={{2,0},{3,1},{0,2},{1,3},{6,4},{7,5},{4,6},{5,7},{10,8},{11,9},{8,1... | collective-permute-start | bytes 86024 | tf_op jit(solution)/shard_map/ppermute | solution.py:55
  19.5 0.0 collective-permute-start.6
  19.5 0.6 collective-permute-start.4
  20.1 0.0 copy-done.10
  20.1 0.8 %compare_reduce_fusion = pred[4,4,9]{1,2,0:T(8,128)(4,1)S(1)} fusion(s32[4,4,9]{1,2,0:T(8,128)S(1)} %broadcast_add_fusion, s32[4,4,9]{2,1,0:T(4,128)S(1)} %copy-done.10), kind=kLoop, calls=%fused_computation | loop fusion | flops 2448 | bytes 1296 | tf_op jit(solution)/shard_map/reduce_or | solution.py:933
  20.9 0.1 copy.20
  21.0 1.6 %collective-permute-done.4.refs_3_ = f32[2,7,2,128]{3,2,1,0:T(2,128)S(1)} collective-permute-done((f32[2,7,2,128]{3,2,1,0:T(2,128)S(1)}, f32[2,7,2,128]{3,2,1,0:T(2,128)S(1)}, u32[]{:S(2)}, u32[]{:S(2)}) %collective-permute-start.4) | collective-permute-done | bytes 14368 | tf_op jit(solution)/shard_map/ppermute | solution.py:55
  22.7 0.0 collective-permute-done.5.refs_4_
  22.7 0.0 collective-permute-done.6.refs_5_
  22.7 0.0 copy-done
  22.7 0.0 copy-done.3
  22.7 0.0 copy-done.4
  22.7 8.6 %langevin_step.4 = (f32[4,4,4,128]{3,2,1,0:T(4,128)S(1)}, f32[2,5,2,128]{3,2,1,0:T(2,128)S(1)}, f32[2,4,4,128]{3,2,1,0:T(4,128)S(1)}, f32[4,4,2,128]{3,2,1,0:T(2...) custom-call(s32[4,4,9]{2,1,0:T(4,128)S(1)} %convert_element_type.3.refs_0_, ...), custom_call_target="tpu_custom_call" | custom-call | tf_op jit(solution)/shard_map/langevin_step/pallas_call | solution.py:679
  31.3 0.9 %collective-permute-start.8 = (f32[2,4,4,128]{3,2,1,0:T(4,128)S(1)}, f32[2,4,4,128]{3,2,1,0:T(4,128)S(1)}, u32[]{:S(2)}, u32[]{:S(2)}) collective-permute-start(f32[2,4,4,128]{3,2,1,0:T(4,128)S(1)} %get-tuple-element.51), channel_id=1, source_target_pairs={{2,0},{3,1},{0,2},{1,3},{6,4},{7,5},{4,6},{5,7},{10,8},{11,9},{8,1... | collective-permute-start | bytes 49160 | tf_op jit(solution)/shard_map/ppermute | solution.py:55
  32.1 0.0 collective-permute-start.9
  32.1 1.3 %collective-permute-start.7 = (f32[2,5,2,128]{3,2,1,0:T(2,128)S(1)}, f32[2,5,2,128]{3,2,1,0:T(2,128)S(1)}, u32[]{:S(2)}, u32[]{:S(2)}) collective-permute-start(f32[2,5,2,128]{3,2,1,0:T(2,128)S(1)} %get-tuple-element.50), channel_id=1, source_target_pairs={{3,0},{2,1},{1,2},{0,3},{7,4},{6,5},{5,6},{4,7},{11,8},{10,9},{9,1... | collective-permute-start | bytes 30728 | tf_op jit(solution)/shard_map/ppermute | solution.py:55
  33.5 1.8 %collective-permute-done.7.refs_3_ = f32[2,5,2,128]{3,2,1,0:T(2,128)S(1)} collective-permute-done((f32[2,5,2,128]{3,2,1,0:T(2,128)S(1)}, f32[2,5,2,128]{3,2,1,0:T(2,128)S(1)}, u32[]{:S(2)}, u32[]{:S(2)}) %collective-permute-start.7) | collective-permute-done | bytes 10272 | tf_op jit(solution)/shard_map/ppermute | solution.py:55
  35.2 0.0 collective-permute-done.8.refs_4_
  35.2 0.0 collective-permute-done.9.refs_5_
  35.2 8.6 %langevin_step.5 = (f32[4,4,4,128]{3,2,1,0:T(4,128)S(1)}, f32[2,5,2,128]{3,2,1,0:T(2,128)S(1)}, f32[2,4,4,128]{3,2,1,0:T(4,128)S(1)}, f32[4,4,2,128]{3,2,1,0:T(2...) custom-call(s32[4,4,9]{2,1,0:T(4,128)S(1)} %convert_element_type.3.refs_0_, ...), custom_call_target="tpu_custom_call" | custom-call | tf_op jit(solution)/shard_map/langevin_step/pallas_call | solution.py:679
  43.8 1.5 %collective-permute-start.11 = (f32[2,4,4,128]{3,2,1,0:T(4,128)S(1)}, f32[2,4,4,128]{3,2,1,0:T(4,128)S(1)}, u32[]{:S(2)}, u32[]{:S(2)}) collective-permute-start(f32[2,4,4,128]{3,2,1,0:T(4,128)S(1)} %get-tuple-element.58), channel_id=1, source_target_pairs={{2,0},{3,1},{0,2},{1,3},{6,4},{7,5},{4,6},{5,7},{10,8},{11,9},{8,1... | collective-permute-start | bytes 49160 | tf_op jit(solution)/shard_map/ppermute | solution.py:55
  45.3 0.0 collective-permute-start.12
  45.3 0.7 collective-permute-start.10
  46.0 2.4 %collective-permute-done.10.refs_3_ = f32[2,5,2,128]{3,2,1,0:T(2,128)S(1)} collective-permute-done((f32[2,5,2,128]{3,2,1,0:T(2,128)S(1)}, f32[2,5,2,128]{3,2,1,0:T(2,128)S(1)}, u32[]{:S(2)}, u32[]{:S(2)}) %collective-permute-start.10) | collective-permute-done | bytes 10272 | tf_op jit(solution)/shard_map/ppermute | solution.py:55
  48.4 0.0 collective-permute-done.11.refs_4_
  48.4 0.0 collective-permute-done.12.refs_5_
  48.4 8.7 %langevin_step.6 = (f32[4,4,4,128]{3,2,1,0:T(4,128)S(1)}, f32[2,5,2,128]{3,2,1,0:T(2,128)S(1)}, f32[2,4,4,128]{3,2,1,0:T(4,128)S(1)}, f32[4,4,2,128]{3,2,1,0:T(2...) custom-call(s32[4,4,9]{2,1,0:T(4,128)S(1)} %convert_element_type.3.refs_0_, ...), custom_call_target="tpu_custom_call" | custom-call | tf_op jit(solution)/shard_map/langevin_step/pallas_call | solution.py:679
  57.2 0.9 %collective-permute-start.14 = (f32[2,4,4,128]{3,2,1,0:T(4,128)S(1)}, f32[2,4,4,128]{3,2,1,0:T(4,128)S(1)}, u32[]{:S(2)}, u32[]{:S(2)}) collective-permute-start(f32[2,4,4,128]{3,2,1,0:T(4,128)S(1)} %get-tuple-element.64), channel_id=1, source_target_pairs={{2,0},{3,1},{0,2},{1,3},{6,4},{7,5},{4,6},{5,7},{10,8},{11,9},{8,1... | collective-permute-start | bytes 49160 | tf_op jit(solution)/shard_map/ppermute | solution.py:55
  58.0 0.0 collective-permute-start.15
  58.0 1.3 %collective-permute-start.13 = (f32[2,5,2,128]{3,2,1,0:T(2,128)S(1)}, f32[2,5,2,128]{3,2,1,0:T(2,128)S(1)}, u32[]{:S(2)}, u32[]{:S(2)}) collective-permute-start(f32[2,5,2,128]{3,2,1,0:T(2,128)S(1)} %get-tuple-element.63), channel_id=1, source_target_pairs={{3,0},{2,1},{1,2},{0,3},{7,4},{6,5},{5,6},{4,7},{11,8},{10,9},{9,1... | collective-permute-start | bytes 30728 | tf_op jit(solution)/shard_map/ppermute | solution.py:55
  59.4 1.8 %collective-permute-done.13.refs_3_ = f32[2,5,2,128]{3,2,1,0:T(2,128)S(1)} collective-permute-done((f32[2,5,2,128]{3,2,1,0:T(2,128)S(1)}, f32[2,5,2,128]{3,2,1,0:T(2,128)S(1)}, u32[]{:S(2)}, u32[]{:S(2)}) %collective-permute-start.13) | collective-permute-done | bytes 10272 | tf_op jit(solution)/shard_map/ppermute | solution.py:55
  61.1 0.0 collective-permute-done.14.refs_4_
  61.1 0.0 collective-permute-done.15.refs_5_
  61.2 8.6 %langevin_step.7 = (f32[4,3,4,128]{3,2,1,0:T(4,128)S(1)}, f32[4,3,4,128]{3,2,1,0:T(4,128)S(1)}, f32[2,4,8,128]{3,2,1,0:T(8,128)S(1)}, f32[8,128]{1,0:T(8,128)S(1)}) custom-call(s32[4,4,9]{2,1,0:T(4,128)S(1)} %convert_element_type.3.refs_0_, f32[1,4,4,8]{3,2,1,0:T(4,128)S(1)} %copy-done.3, f32[4,4,4,128]{3,2,1,0:T(4,128)S(1)} %get-tuple-element.62.refs_2_, ...), custom_call_target="tpu_custom_call" | custom-call | tf_op jit(solution)/shard_map/langevin_step/pallas_call | solution.py:679
  69.7 1.4 %collective-permute-start.16 = (f32[8,128]{1,0:T(8,128)S(1)}, f32[8,128]{1,0:T(8,128)S(1)}, u32[]{:S(2)}, u32[]{:S(2)}) collective-permute-start(f32[8,128]{1,0:T(8,128)S(1)} %get-tuple-element.71.refs_4_), channel_id=1, source_target_pairs={{3,0},{2,1},{1,2},{0,3},{7,4},{6,5},{5,6},{4,7},{11,8},{10,9},{9,1... | collective-permute-start | bytes 12296 | tf_op jit(solution)/shard_map/ppermute | solution.py:55
  71.1 0.8 %collective-permute-start.17 = (f32[8,128]{1,0:T(8,128)S(1)}, f32[8,128]{1,0:T(8,128)S(1)}, u32[]{:S(2)}, u32[]{:S(2)}) collective-permute-start(f32[8,128]{1,0:T(8,128)S(1)} %get-tuple-element.71.refs_4_), channel_id=1, source_target_pairs={{2,0},{3,1},{0,2},{1,3},{6,4},{7,5},{4,6},{5,7},{10,8},{11,9},{8,1... | collective-permute-start | bytes 12296 | tf_op jit(solution)/shard_map/ppermute | solution.py:55
  71.9 0.0 collective-permute-start.18
  71.9 0.9 %collective-permute-done.16.refs_5_ = f32[8,128]{1,0:T(8,128)S(1)} collective-permute-done((f32[8,128]{1,0:T(8,128)S(1)}, f32[8,128]{1,0:T(8,128)S(1)}, u32[]{:S(2)}, u32[]{:S(2)}) %collective-permute-start.16) | collective-permute-done | bytes 4128 | tf_op jit(solution)/shard_map/ppermute | solution.py:55
  72.8 1.9 %collective-permute-done.17.refs_6_ = f32[8,128]{1,0:T(8,128)S(1)} collective-permute-done((f32[8,128]{1,0:T(8,128)S(1)}, f32[8,128]{1,0:T(8,128)S(1)}, u32[]{:S(2)}, u32[]{:S(2)}) %collective-permute-start.17) | collective-permute-done | bytes 4128 | tf_op jit(solution)/shard_map/ppermute | solution.py:55
  74.7 0.0 collective-permute-done.18.refs_7_
  74.7 1.2 %last_angles.1 = (f32[1,4,8]{2,1,0:T(4,128)}, f32[1,4,8]{2,1,0:T(4,128)}, f32[4,3,4,128]{3,2,1,0:T(4,128)}, f32[4,3,4,128]{3,2,1,0:T(4,128)}) custom-call(f32[1,4,4,8]{3,2,1,0:T(4,128)S(1)} %copy-done.3, f32[2,4,8,128]{3,2,1,0:T(8,128)S(1)} %get-tuple-element.68.refs_1_, f32[4,3,4,128]{3,2,1,0:T(4,128)S(1)} %get-tuple-element.69.refs_2_, ...), custom_call_target="tpu_custom_call" | custom-call | tf_op jit(solution)/shard_map/last_angles/pallas_call | solution.py:739
  (12 shorter events, 0.0 us)
Async XLA Ops:
  2.2 5.3 %collective-permute-start = (f32[25,4,128]{2,1,0:T(4,128)}, f32[25,4,128]{2,1,0:T(4,128)S(1)}, u32[]{:S(2)}, u32[]{:S(2)}) collective-permute-start(f32[25,4,128]{2,1,0:T(4,128)} %pack_walker.1.mine_ref.refs_0_), channel_id=1, source_target_pairs={{0,4},{4,0},{8,12},{12,8},{16,20},{20,16},{24,28},{28,24},{1,5},{5... | collective-permute-start | bytes 153608 | tf_op jit(solution)/shard_map/ppermute | solution.py:845
  5.5 2.1 %copy-start.9 = (s32[8]{0:T(128)S(1)}, s32[8]{0:T(128)}, u32[]{:S(2)}) copy-start(s32[8]{0:T(128)} %param.17) | copy-start | bytes 100
  7.6 0.8 %copy-start.1 = (f32[25,4,128]{2,1,0:T(4,128)S(1)}, f32[25,4,128]{2,1,0:T(4,128)}, u32[]{:S(2)}) copy-start(f32[25,4,128]{2,1,0:T(4,128)} %pack_walker.1.mine_ref.refs_0_) | copy-start | bytes 153604
  8.4 9.3 %copy-start.2 = (f32[25,4,128]{2,1,0:T(4,128)S(1)}, f32[25,4,128]{2,1,0:T(4,128)}, u32[]{:S(2)}) copy-start(f32[25,4,128]{2,1,0:T(4,128)} %pack_walker.1.mine_ref.refs_0_) | copy-start | bytes 153604
  8.8 6.7 %collective-permute-start.1 = (f32[25,4,128]{2,1,0:T(4,128)S(1)}, f32[25,4,128]{2,1,0:T(4,128)S(1)}, u32[]{:S(2)}, u32[]{:S(2)}) collective-permute-start(f32[25,4,128]{2,1,0:T(4,128)S(1)} %get-tuple-element.40), channel_id=1, source_target_pairs={{0,8},{4,12},{8,16},{12,20},{16,24},{20,28},{24,0},{28,4},{1,9},{5... | collective-permute-start | bytes 153608 | tf_op jit(solution)/shard_map/ppermute | solution.py:859
  11.0 5.1 %collective-permute-start.2 = (f32[25,4,128]{2,1,0:T(4,128)S(1)}, f32[25,4,128]{2,1,0:T(4,128)S(1)}, u32[]{:S(2)}, u32[]{:S(2)}) collective-permute-start(f32[25,4,128]{2,1,0:T(4,128)S(1)} %get-tuple-element.41), channel_id=1, source_target_pairs={{0,16},{4,20},{8,24},{12,28},{16,0},{20,4},{24,8},{28,12},{1,17},{... | collective-permute-start | bytes 153608 | tf_op jit(solution)/shard_map/ppermute | solution.py:859
  13.5 4.1 %collective-permute-start.3 = (f32[25,4,128]{2,1,0:T(4,128)S(1)}, f32[25,4,128]{2,1,0:T(4,128)S(1)}, u32[]{:S(2)}, u32[]{:S(2)}) collective-permute-start(f32[25,4,128]{2,1,0:T(4,128)S(1)} %get-tuple-element.42), channel_id=1, source_target_pairs={{0,24},{4,28},{8,0},{12,4},{16,8},{20,12},{24,16},{28,20},{1,25},{... | collective-permute-start | bytes 153608 | tf_op jit(solution)/shard_map/ppermute | solution.py:859
  14.9 2.8 %copy-start.5 = (f32[4,4,128]{2,1,0:T(4,128)S(1)}, f32[4,4,128]{2,1,0:T(4,128)}, u32[]{:S(2)}) copy-start(f32[4,4,128]{2,1,0:T(4,128)} %refs_5_.1) | copy-start | bytes 24580
  14.9 2.8 %copy-start.6 = (f32[4,4,128]{2,1,0:T(4,128)S(1)}, f32[4,4,128]{2,1,0:T(4,128)}, u32[]{:S(2)}) copy-start(f32[4,4,128]{2,1,0:T(4,128)} %refs_6_.1) | copy-start | bytes 24580
  14.9 2.8 %copy-start.7 = (s32[4,4,128]{2,1,0:T(4,128)S(1)}, s32[4,4,128]{2,1,0:T(4,128)}, u32[]{:S(2)}) copy-start(s32[4,4,128]{2,1,0:T(4,128)} %refs_7_.1) | copy-start | bytes 24580
  14.9 2.8 %copy-start.8 = (s32[4,4,128]{2,1,0:T(4,128)S(1)}, s32[4,4,128]{2,1,0:T(4,128)}, u32[]{:S(2)}) copy-start(s32[4,4,128]{2,1,0:T(4,128)} %refs_8_.2) | copy-start | bytes 24580
  17.7 2.4 %copy-start.10 = (s32[4,4,9]{2,1,0:T(4,128)S(1)}, s32[4,4,9]{2,1,0:T(4,128)}, u32[]{:S(2)}) copy-start(s32[4,4,9]{2,1,0:T(4,128)} %param.25) | copy-start | bytes 1732
  17.7 5.0 %copy-start = (f32[1,4,4,4,3,128]{5,3,4,2,1,0:T(4,128)S(1)}, f32[1,4,4,4,3,128]{5,3,4,2,1,0:T(4,128)}, u32[]{:S(2)}) copy-start(f32[1,4,4,4,3,128]{5,3,4,2,1,0:T(4,128)} %param.18) | copy-start | bytes 294916
  17.9 4.7 %collective-permute-start.5 = (f32[2,7,4,128]{3,2,1,0:T(4,128)S(1)}, f32[2,7,4,128]{3,2,1,0:T(4,128)S(1)}, u32[]{:S(2)}, u32[]{:S(2)}) collective-permute-start(f32[2,7,4,128]{3,2,1,0:T(4,128)S(1)} %get-tuple-element.45), channel_id=1, source_target_pairs={{2,0},{3,1},{0,2},{1,3},{6,4},{7,5},{4,6},{5,7},{10,8},{11,9},{8,1... | collective-permute-start | bytes 86024 | tf_op jit(solution)/shard_map/ppermute | solution.py:55
  19.5 3.2 %collective-permute-start.6 = (f32[4,7,2,128]{3,2,1,0:T(2,128)S(1)}, f32[4,7,2,128]{3,2,1,0:T(2,128)S(1)}, u32[]{:S(2)}, u32[]{:S(2)}) collective-permute-start(f32[4,7,2,128]{3,2,1,0:T(2,128)S(1)} %get-tuple-element.46), channel_id=1, source_target_pairs={{1,0},{0,1},{3,2},{2,3},{5,4},{4,5},{7,6},{6,7},{9,8},{8,9},{11,10... | collective-permute-start | bytes 86024 | tf_op jit(solution)/shard_map/ppermute | solution.py:55
  19.5 3.1 %collective-permute-start.4 = (f32[2,7,2,128]{3,2,1,0:T(2,128)S(1)}, f32[2,7,2,128]{3,2,1,0:T(2,128)S(1)}, u32[]{:S(2)}, u32[]{:S(2)}) collective-permute-start(f32[2,7,2,128]{3,2,1,0:T(2,128)S(1)} %get-tuple-element.44), channel_id=1, source_target_pairs={{3,0},{2,1},{1,2},{0,3},{7,4},{6,5},{5,6},{4,7},{11,8},{10,9},{9,1... | collective-permute-start | bytes 43016 | tf_op jit(solution)/shard_map/ppermute | solution.py:55
  21.0 1.6 %copy-start.3 = (f32[1,4,4,8]{3,2,1,0:T(4,128)S(1)}, f32[1,4,4,8]{3,2,1,0:T(4,128)}, u32[]{:S(2)}) copy-start(f32[1,4,4,8]{3,2,1,0:T(4,128)} %refs_0_.1) | copy-start | bytes 1540
  21.0 1.6 %copy-start.4 = (f32[4,4,128]{2,1,0:T(4,128)S(1)}, f32[4,4,128]{2,1,0:T(4,128)}, u32[]{:S(2)}) copy-start(f32[4,4,128]{2,1,0:T(4,128)} %refs_9_.5) | copy-start | bytes 24580
  31.3 4.0 %collective-permute-start.8 = (f32[2,4,4,128]{3,2,1,0:T(4,128)S(1)}, f32[2,4,4,128]{3,2,1,0:T(4,128)S(1)}, u32[]{:S(2)}, u32[]{:S(2)}) collective-permute-start(f32[2,4,4,128]{3,2,1,0:T(4,128)S(1)} %get-tuple-element.51), channel_id=1, source_target_pairs={{2,0},{3,1},{0,2},{1,3},{6,4},{7,5},{4,6},{5,7},{10,8},{11,9},{8,1... | collective-permute-start | bytes 49160 | tf_op jit(solution)/shard_map/ppermute | solution.py:55
  32.1 3.1 %collective-permute-start.9 = (f32[4,4,2,128]{3,2,1,0:T(2,128)S(1)}, f32[4,4,2,128]{3,2,1,0:T(2,128)S(1)}, u32[]{:S(2)}, u32[]{:S(2)}) collective-permute-start(f32[4,4,2,128]{3,2,1,0:T(2,128)S(1)} %get-tuple-element.52), channel_id=1, source_target_pairs={{1,0},{0,1},{3,2},{2,3},{5,4},{4,5},{7,6},{6,7},{9,8},{8,9},{11,10... | collective-permute-start | bytes 49160 | tf_op jit(solution)/shard_map/ppermute | solution.py:55
  32.1 3.1 %collective-permute-start.7 = (f32[2,5,2,128]{3,2,1,0:T(2,128)S(1)}, f32[2,5,2,128]{3,2,1,0:T(2,128)S(1)}, u32[]{:S(2)}, u32[]{:S(2)}) collective-permute-start(f32[2,5,2,128]{3,2,1,0:T(2,128)S(1)} %get-tuple-element.50), channel_id=1, source_target_pairs={{3,0},{2,1},{1,2},{0,3},{7,4},{6,5},{5,6},{4,7},{11,8},{10,9},{9,1... | collective-permute-start | bytes 30728 | tf_op jit(solution)/shard_map/ppermute | solution.py:55
  43.8 4.6 %collective-permute-start.11 = (f32[2,4,4,128]{3,2,1,0:T(4,128)S(1)}, f32[2,4,4,128]{3,2,1,0:T(4,128)S(1)}, u32[]{:S(2)}, u32[]{:S(2)}) collective-permute-start(f32[2,4,4,128]{3,2,1,0:T(4,128)S(1)} %get-tuple-element.58), channel_id=1, source_target_pairs={{2,0},{3,1},{0,2},{1,3},{6,4},{7,5},{4,6},{5,7},{10,8},{11,9},{8,1... | collective-permute-start | bytes 49160 | tf_op jit(solution)/shard_map/ppermute | solution.py:55
  45.3 3.1 %collective-permute-start.12 = (f32[4,4,2,128]{3,2,1,0:T(2,128)S(1)}, f32[4,4,2,128]{3,2,1,0:T(2,128)S(1)}, u32[]{:S(2)}, u32[]{:S(2)}) collective-permute-start(f32[4,4,2,128]{3,2,1,0:T(2,128)S(1)} %get-tuple-element.59), channel_id=1, source_target_pairs={{1,0},{0,1},{3,2},{2,3},{5,4},{4,5},{7,6},{6,7},{9,8},{8,9},{11,10... | collective-permute-start | bytes 49160 | tf_op jit(solution)/shard_map/ppermute | solution.py:55
  45.3 3.1 %collective-permute-start.10 = (f32[2,5,2,128]{3,2,1,0:T(2,128)S(1)}, f32[2,5,2,128]{3,2,1,0:T(2,128)S(1)}, u32[]{:S(2)}, u32[]{:S(2)}) collective-permute-start(f32[2,5,2,128]{3,2,1,0:T(2,128)S(1)} %get-tuple-element.57), channel_id=1, source_target_pairs={{3,0},{2,1},{1,2},{0,3},{7,4},{6,5},{5,6},{4,7},{11,8},{10,9},{9,1... | collective-permute-start | bytes 30728 | tf_op jit(solution)/shard_map/ppermute | solution.py:55
  57.2 4.0 %collective-permute-start.14 = (f32[2,4,4,128]{3,2,1,0:T(4,128)S(1)}, f32[2,4,4,128]{3,2,1,0:T(4,128)S(1)}, u32[]{:S(2)}, u32[]{:S(2)}) collective-permute-start(f32[2,4,4,128]{3,2,1,0:T(4,128)S(1)} %get-tuple-element.64), channel_id=1, source_target_pairs={{2,0},{3,1},{0,2},{1,3},{6,4},{7,5},{4,6},{5,7},{10,8},{11,9},{8,1... | collective-permute-start | bytes 49160 | tf_op jit(solution)/shard_map/ppermute | solution.py:55
  58.0 3.1 %collective-permute-start.15 = (f32[4,4,2,128]{3,2,1,0:T(2,128)S(1)}, f32[4,4,2,128]{3,2,1,0:T(2,128)S(1)}, u32[]{:S(2)}, u32[]{:S(2)}) collective-permute-start(f32[4,4,2,128]{3,2,1,0:T(2,128)S(1)} %get-tuple-element.65), channel_id=1, source_target_pairs={{1,0},{0,1},{3,2},{2,3},{5,4},{4,5},{7,6},{6,7},{9,8},{8,9},{11,10... | collective-permute-start | bytes 49160 | tf_op jit(solution)/shard_map/ppermute | solution.py:55
  58.0 3.1 %collective-permute-start.13 = (f32[2,5,2,128]{3,2,1,0:T(2,128)S(1)}, f32[2,5,2,128]{3,2,1,0:T(2,128)S(1)}, u32[]{:S(2)}, u32[]{:S(2)}) collective-permute-start(f32[2,5,2,128]{3,2,1,0:T(2,128)S(1)} %get-tuple-element.63), channel_id=1, source_target_pairs={{3,0},{2,1},{1,2},{0,3},{7,4},{6,5},{5,6},{4,7},{11,8},{10,9},{9,1... | collective-permute-start | bytes 30728 | tf_op jit(solution)/shard_map/ppermute | solution.py:55
  69.7 3.1 %collective-permute-start.16 = (f32[8,128]{1,0:T(8,128)S(1)}, f32[8,128]{1,0:T(8,128)S(1)}, u32[]{:S(2)}, u32[]{:S(2)}) collective-permute-start(f32[8,128]{1,0:T(8,128)S(1)} %get-tuple-element.71.refs_4_), channel_id=1, source_target_pairs={{3,0},{2,1},{1,2},{0,3},{7,4},{6,5},{5,6},{4,7},{11,8},{10,9},{9,1... | collective-permute-start | bytes 12296 | tf_op jit(solution)/shard_map/ppermute | solution.py:55
  71.1 3.6 %collective-permute-start.17 = (f32[8,128]{1,0:T(8,128)S(1)}, f32[8,128]{1,0:T(8,128)S(1)}, u32[]{:S(2)}, u32[]{:S(2)}) collective-permute-start(f32[8,128]{1,0:T(8,128)S(1)} %get-tuple-element.71.refs_4_), channel_id=1, source_target_pairs={{2,0},{3,1},{0,2},{1,3},{6,4},{7,5},{4,6},{5,7},{10,8},{11,9},{8,1... | collective-permute-start | bytes 12296 | tf_op jit(solution)/shard_map/ppermute | solution.py:55
  71.9 2.8 %collective-permute-start.18 = (f32[8,128]{1,0:T(8,128)S(1)}, f32[8,128]{1,0:T(8,128)S(1)}, u32[]{:S(2)}, u32[]{:S(2)}) collective-permute-start(f32[8,128]{1,0:T(8,128)S(1)} %get-tuple-element.71.refs_4_), channel_id=1, source_target_pairs={{1,0},{0,1},{3,2},{2,3},{5,4},{4,5},{7,6},{6,7},{9,8},{8,9},{11,10... | collective-permute-start | bytes 12296 | tf_op jit(solution)/shard_map/ppermute | solution.py:55
